TPU v7x, 32 devices: a whole 2x2x4 slice. The times are simulated.
32 devices in a mesh: head: 2 (over y), blk: 16 (over z, x, core).
Axes of the slice: x: 2, y: 2, z: 4, core: 2. Of those that a mesh axis runs over, the one named last changes fastest.
Arguments:
- tokens: bfloat16 [2, 2048, 768], P(None, ('blk', 'head')), may hold values from -6 to 6
- doc_ids: int32 [2, 2048], P(None, ('blk', 'head')), may hold values from 0 to 3, never falling along the last dimension, each value on 1 to 1536 neighbouring positions
- cotangent: bfloat16 [2, 2048, 768], P(None, ('blk', 'head')), may hold values from -6 to 6
- attn_weight: float32 [4, 768, 768], P(None, ('blk', 'head'))
- ffn_weight: float32 [3, 768, 2048], P(None, ('blk', 'head'))
- attn_moment: float32 [4, 768, 768], P(None, ('blk', 'head'))
- ffn_moment: float32 [3, 768, 2048], P(None, ('blk', 'head'))
Outputs:
- output: bfloat16 [2, 2048, 768], P(None, ('blk', 'head'))
- input_grad: float32 [2, 2048, 768], P(None, ('blk', 'head'))
- attn_grad: float32 [4, 768, 768], P(None, ('blk', 'head'))
- ffn_grad: float32 [3, 768, 2048], P(None, ('blk', 'head'))
- attn_master: float32 [4, 768, 768], P(None, ('blk', 'head'))
- ffn_master: float32 [3, 768, 2048], P(None, ('blk', 'head'))
- attn_moment_new: float32 [4, 768, 768], P(None, ('blk', 'head'))
- ffn_moment_new: float32 [3, 768, 2048], P(None, ('blk', 'head'))
- attn_copy: bfloat16 [4, 768, 768], P(None, ('blk', 'head'))
- ffn_copy: bfloat16 [3, 768, 2048], P(None, ('blk', 'head'))
Inputs may be any that keep to these rules, and one draw needn't show every extreme that they name: `doc_ids`: in each micro-batch the document numbers never fall along the sequence; every document has 1 to 1536 positions and one has exactly 1536.
All inputs are finite; a program needn't handle non-finite values.
Results may differ from a plain program's by a relative error of at most 0.04.
Values may be sent and summed in bfloat16 or wider, within the bound.
A program may use at most 320 MiB of HBM per device.

v0:
```python
import functools
import math

import jax
import jax.numpy as jnp
from jax import lax
from jax.experimental import pallas as pl
from jax.experimental.pallas import tpu as pltpu
from jax.sharding import PartitionSpec as P

D = 768
HEADS = 12
HEAD_DIM = 64
HALF = 32
FF = 2048
DOCS = 4
NS_STEPS = 5
GROUP = 8
SPARE = 2
BLOCK = 256

EPSILON = 1e-05
NEGATIVE = -1e30
RATES = (0.5, 0.5, 0.5, 7.0, 1.0, 1.0, 0.5)
COEFF_A = 3.4445
COEFF_B = -4.775
COEFF_C = 2.0315
OWNERS = (8, 9, 12, 21, 16, 17, 20)
MESH = pl.DeviceIdType.MESH
ANY = pl.BlockSpec(memory_space=pl.ANY)
VMEM = pl.BlockSpec(memory_space=pltpu.VMEM)
SMEM = pl.BlockSpec(memory_space=pltpu.SMEM)
SCALE = HEAD_DIM ** (-0.5)


def nt(a, b):
    return lax.dot_general(a, b, (((1,), (1,)), ((), ())), preferred_element_type=jnp.float32)


def nn(a, b):
    return jnp.dot(a, b, preferred_element_type=jnp.float32)


def attends(device):
    plane = device // GROUP
    return jnp.logical_and(plane < 4, plane != SPARE)


def combo_of(device):
    plane = device // GROUP
    place = device % GROUP
    return (place // 4) * HEADS + 4 * (plane - plane // 3) + place % 4


def device_of(combo):
    group = (combo % HEADS) // 4
    return GROUP * (group + group // 2) + 4 * (combo // HEADS) + combo % 4


class Net:
    def __init__(self, mesh):
        self.inner = mesh.shape["head"]
        self.count = mesh.shape["head"] * mesh.shape["blk"]
        self.planes = self.count // GROUP

    def permute(self, values, pairs):
        outer = self.count // self.inner

        def place(device):
            return (device % self.inner) * outer + device // self.inner

        return lax.ppermute(values, ("head", "blk"), [(place(i), place(j)) for i, j in pairs])

    def me(self):
        return lax.axis_index("blk") * self.inner + lax.axis_index("head")

    def at(self, device):
        return {"blk": device // self.inner, "head": device % self.inner}

    def meet(self, me, size):
        barrier = pltpu.get_barrier_semaphore()

        def greet(k, carry):
            pl.semaphore_signal(barrier, inc=1, device_id=self.at(peer(me, k, size)), device_id_type=MESH)
            return carry

        lax.fori_loop(1, size, greet, 0)
        pl.semaphore_wait(barrier, size - 1)

    def meet_attending(self, me):
        barrier = pltpu.get_barrier_semaphore()

        @pl.when(attends(me))
        def _():
            def greet(k, carry):
                other = peer(me, k, self.count)

                @pl.when(attends(other))
                def _():
                    pl.semaphore_signal(barrier, inc=1, device_id=self.at(other), device_id_type=MESH)

                return carry

            lax.fori_loop(1, self.count, greet, 0)
            pl.semaphore_wait(barrier, 2 * HEADS - 1)

    def shift(self, values, steps):
        far = GROUP * steps
        return self.permute(values, [(i, (i + far) % self.count) for i in range(self.count)])

    def flip(self, values, distance):
        return self.permute(values, [(i, i ^ distance) for i in range(self.count)])


def peer(me, k, size):
    return (me // size) * size + (me % size + k) % size


def flip_x(device):
    return device + 4 - 8 * ((device % GROUP) // 4)


def flip_y(device):
    return device + 1 - 2 * (device % 2)


def flip_core(device):
    return device + 2 - 4 * ((device % 4) // 2)


def spot_of(device):
    return 2 * (device % 4) + (device % GROUP) // 4


class Flow:
    def __init__(self, source, target, take, put, goes=None, size=None):
        self.source, self.target, self.take, self.put = source, target, take, put
        self.goes = goes or (lambda i, j: i >= 0)
        self.size = size

    def scratch(self):
        return []

    def semaphores(self):
        return self.size

    def bind(self, net, inputs, outputs, scratch, send, receive, local):
        self.net = net
        self.input, self.output = inputs[self.source], outputs[self.target]
        self.held = scratch
        self.send, self.receive, self.local = send, receive, local

    def copy(self, source, target, index, device):
        return pltpu.make_async_remote_copy(
            source,
            target,
            self.send.at[index],
            self.receive.at[index],
            device_id=self.net.at(device),
            device_id_type=MESH,
        )

    def remote(self, i, j, k):
        return self.copy(self.input.at[self.take(i, j)], self.output.at[self.put(i, j)], k, j)

    def near(self, i):
        return pltpu.make_async_copy(self.input.at[self.take(i, i)], self.output.at[self.put(i, i)], self.local)

    def start(self, me):
        def one(k, carry):
            other = peer(me, k, self.size)

            @pl.when(self.goes(me, other))
            def _():
                self.remote(me, other, k).start()

            return carry

        lax.fori_loop(1, self.size, one, 0)

        @pl.when(self.goes(me, me))
        def _():
            self.near(me).start()

    def middle(self, me):
        pass

    def finish(self, me):
        def one(k, carry):
            other = peer(me, k, self.size)

            @pl.when(self.goes(me, other))
            def _():
                self.remote(me, other, k).wait_send()

            before = peer(me, self.size - k, self.size)

            @pl.when(self.goes(before, me))
            def _():
                self.remote(before, me, k).wait_recv()

            return carry

        lax.fori_loop(1, self.size, one, 0)

        @pl.when(self.goes(me, me))
        def _():
            self.near(me).wait()


class Across(Flow):
    def semaphores(self):
        return self.net_planes

    def __init__(self, net, source, target, take, put):
        super().__init__(source, target, take, put, None, net.count)
        self.net_planes = net.planes

    def other(self, me, k):
        return (me + k * GROUP) % self.size

    def start(self, me):
        for k in range(1, self.net_planes):
            self.remote(me, self.other(me, k), k).start()
        self.near(me).start()

    def finish(self, me):
        for k in range(1, self.net_planes):
            self.remote(me, self.other(me, k), k).wait_send()
            self.remote(self.other(me, self.net_planes - k), me, k).wait_recv()
        self.near(me).wait()


class FanIn(Flow):
    def __init__(self, source, target, owner, take, put, goes=None, size=None):
        super().__init__(source, target, take, put, goes, size)
        self.owner = owner

    def sends(self, me):
        here = jnp.logical_and(me // self.size == self.owner // self.size, me != self.owner)
        return jnp.logical_and(here, self.goes(me, self.owner))

    def step(self, me):
        return (self.owner - me + self.net.count) % self.size

    def start(self, me):
        @pl.when(self.sends(me))
        def _():
            self.remote(me, self.owner, self.step(me)).start()

        @pl.when(jnp.logical_and(me == self.owner, self.goes(me, me)))
        def _():
            self.near(me).start()

    def finish(self, me):
        @pl.when(self.sends(me))
        def _():
            self.remote(me, self.owner, self.step(me)).wait_send()

        @pl.when(me == self.owner)
        def _():
            def one(k, carry):
                before = peer(me, self.size - k, self.size)

                @pl.when(self.goes(before, me))
                def _():
                    self.remote(before, me, k).wait_recv()

                return carry

            lax.fori_loop(1, self.size, one, 0)

        @pl.when(jnp.logical_and(me == self.owner, self.goes(me, me)))
        def _():
            self.near(me).wait()


class FanOut(Flow):
    def __init__(self, source, target, owner, take, put):
        super().__init__(source, target, take, put)
        self.owner = owner

    def start(self, me):
        @pl.when(me == self.owner)
        def _():
            def one(k, carry):
                self.remote(me, peer(me, k, self.size), k).start()
                return carry

            lax.fori_loop(1, self.size, one, 0)
            self.near(me).start()

    def finish(self, me):
        @pl.when(me == self.owner)
        def _():
            def one(k, carry):
                self.remote(me, peer(me, k, self.size), k).wait_send()
                return carry

            lax.fori_loop(1, self.size, one, 0)
            self.near(me).wait()

        @pl.when(me != self.owner)
        def _():
            self.remote(self.owner, me, (me - self.owner + self.net.count) % self.size).wait_recv()


class PlaneGather(Flow):
    def __init__(self, source, target):
        super().__init__(source, target, None, None)

    def semaphores(self):
        return GROUP

    def partners(self, me):
        return [flip_x(me), flip_y(me), flip_x(flip_y(me))]

    def own(self, me, index, device):
        return self.copy(self.input, self.output.at[spot_of(me)], index, device)

    def passed(self, me, index, partner):
        block = self.output.at[spot_of(partner)]
        return self.copy(block, block, 4 + index, flip_core(me))

    def start(self, me):
        for index, partner in enumerate(self.partners(me)):
            self.own(me, 1 + index, partner).start()
        self.own(me, 0, flip_core(me)).start()
        pltpu.make_async_copy(self.input, self.output.at[spot_of(me)], self.local).start()

    def middle(self, me):
        for index, partner in enumerate(self.partners(me)):
            self.own(me, 1 + index, partner).wait_recv()
            self.passed(me, index, partner).start()

    def finish(self, me):
        for index, partner in enumerate(self.partners(me)):
            self.own(me, 1 + index, partner).wait_send()
            self.passed(me, index, partner).wait()
        self.own(me, 0, flip_core(me)).wait()
        pltpu.make_async_copy(self.input, self.output.at[spot_of(me)], self.local).wait()


class PlaneScatter(Flow):
    def __init__(self, source, target, block, planes=0):
        super().__init__(source, target, None, None)
        self.block, self.planes = block, planes

    def scratch(self):
        shapes = [pltpu.VMEM((4,) + self.block, jnp.bfloat16)] * 2 + [pltpu.VMEM((3,) + self.block, jnp.bfloat16)]
        if self.planes:
            shapes += [
                pltpu.VMEM(self.block, jnp.bfloat16),
                pltpu.VMEM((self.planes,) + self.block[1:], jnp.bfloat16),
            ]
        return shapes

    def semaphores(self):
        return 4 + self.planes

    def partners(self, me):
        return [flip_x(me), flip_y(me), flip_x(flip_y(me))]

    def half(self, core):
        return self.input.at[pl.ds(4 * core, 4)]

    def first(self, me):
        return self.copy(self.half(1 - (me % 4) // 2), self.held[1], 0, flip_core(me))

    def mine(self, me):
        return pltpu.make_async_copy(self.half((me % 4) // 2), self.held[0], self.local)

    def second(self, me, index, partner):
        return self.copy(self.held[0].at[spot_of(partner) % 4], self.held[2].at[index], 1 + index, partner)

    def third(self, me, k):
        plane = me // GROUP
        target = (plane + k) % self.planes
        return self.copy(self.held[3].at[target], self.held[4].at[plane], 4 + k, (me + k * GROUP) % self.net.count)

    def start(self, me):
        self.first(me).start()
        self.mine(me).start()

    def middle(self, me):
        self.mine(me).wait()
        self.first(me).wait_recv()
        low = jnp.bfloat16
        for index, partner in enumerate(self.partners(me)):
            slot = spot_of(partner) % 4
            self.held[0][slot] = (
                self.held[0][slot].astype(jnp.float32) + self.held[1][slot].astype(jnp.float32)
            ).astype(low)
            self.second(me, index, partner).start()

    def finish(self, me):
        slot = spot_of(me) % 4
        total = self.held[0][slot].astype(jnp.float32) + self.held[1][slot].astype(jnp.float32)
        for index, partner in enumerate(self.partners(me)):
            self.second(me, index, partner).wait_recv()
            total = total + self.held[2][index].astype(jnp.float32)
        if self.planes:
            self.held[3][...] = total.astype(jnp.bfloat16)
            for k in range(1, self.planes):
                self.third(me, k).start()
            plane = me // GROUP
            total = self.held[3][plane].astype(jnp.float32)
            for k in range(1, self.planes):
                self.third(me, k).wait_recv()
                total = total + self.held[4][(plane + self.planes - k) % self.planes].astype(jnp.float32)
        self.output[...] = total
        self.first(me).wait_send()
        for index, partner in enumerate(self.partners(me)):
            self.second(me, index, partner).wait_send()
        for k in range(1, self.planes):
            self.third(me, k).wait_send()


def bind_all(net, flows, inputs, outputs, scratch, send, receive, local):
    used = 0
    for number, flow in enumerate(flows):
        need = len(flow.scratch())
        flow.bind(
            net, inputs, outputs, scratch[used : used + need], send.at[number], receive.at[number], local.at[number]
        )
        used += need


def exchange_kernel(net, meet, flows, sources, targets, *refs):
    inputs = refs[:sources]
    outputs = refs[sources : sources + targets]
    me = net.me()
    meet(me)
    bind_all(net, flows, inputs, outputs, refs[sources + targets : -3], *refs[-3:])
    for flow in flows:
        flow.start(me)
    for flow in flows:
        flow.middle(me)
    for flow in flows:
        flow.finish(me)


def flow_scratch(flows):
    most = max(flow.semaphores() for flow in flows)
    return [shape for flow in flows for shape in flow.scratch()] + [
        pltpu.SemaphoreType.DMA((len(flows), most)),
        pltpu.SemaphoreType.DMA((len(flows), most)),
        pltpu.SemaphoreType.DMA((len(flows),)),
    ]


def exchange(net, name, number, flows, sources, shapes, size=None, meet=None):
    size = size or net.count
    for flow in flows:
        flow.size = flow.size or size
    summed = {flow.target for flow in flows if isinstance(flow, PlaneScatter)}
    moved = sum(math.prod(s.shape) * s.dtype.itemsize for s in shapes)
    return pl.pallas_call(
        functools.partial(
            exchange_kernel, net, meet or (lambda me: net.meet(me, size)), flows, len(sources), len(shapes)
        ),
        out_shape=shapes,
        in_specs=[ANY] * len(sources),
        out_specs=[VMEM if k in summed else ANY for k in range(len(shapes))],
        scratch_shapes=flow_scratch(flows),
        compiler_params=pltpu.CompilerParams(collective_id=number, has_side_effects=True),
        cost_estimate=pl.CostEstimate(flops=0, bytes_accessed=8 * moved, transcendentals=0),
        name=name,
    )(*sources)


def gather_kernel(net, flows, x_ref, w_ref, cut_ref, out_ref, all_ref, wall_ref, cut_all, out_all, send, receive, wsend, wreceive, local, *refs):
    count = net.count
    planes = net.planes
    me = net.me()
    plane = me // GROUP
    place = me % GROUP
    half = place // 4
    spot = place % 4
    across = flip_x(me)
    beside = flip_y(me)
    sibling = flip_core(me)
    net.meet(me, count)
    bind_all(net, flows, (cut_ref, out_ref), (cut_all, out_all), (), *refs)

    def remote(source, target, index, device):
        return pltpu.make_async_remote_copy(
            source, target, send.at[index], receive.at[index], device_id=net.at(device), device_id_type=MESH
        )

    swap = remote(x_ref.at[1 - half], all_ref.at[plane, half, spot], 0, across)
    swap.start()

    def second(step, which):
        target = (me + step * GROUP) % count
        block = all_ref.at[plane, which, spot]
        return remote(block, block, 1 + (step - 1) * 2 + (which + half) % 2, target)

    def direct(step):
        target = (me + step * GROUP) % count
        return remote(x_ref.at[half], all_ref.at[plane, half, spot], 1 + (step - 1) * 2, target)

    third_base = 1 + 2 * (planes - 1)

    def third(step, which):
        source_plane = (plane + planes - step) % planes
        block = all_ref.at[source_plane, which, spot]
        return remote(block, block, third_base + step * 2 + which, beside)

    fourth_base = third_base + 2 * planes

    def fourth(step, which):
        source_plane = (plane + planes - step) % planes
        block = all_ref.at[source_plane, which, pl.ds((spot // 2) * 2, 2)]
        return remote(block, block, fourth_base + step * 2 + which, sibling)

    for step in range(1, planes):
        direct(step).start()
    mine = pltpu.make_async_copy(x_ref.at[half], all_ref.at[plane, half, spot], local.at[0])
    mine.start()

    def weights(combo):
        target = device_of(combo)
        return pltpu.make_async_remote_copy(
            w_ref.at[combo % HEADS],
            wall_ref.at[me],
            wsend.at[combo],
            wreceive.at[me],
            device_id=net.at(target),
            device_id_type=MESH,
        )

    def send_weights(combo, carry):
        @pl.when(device_of(combo) != me)
        def _():
            weights(combo).start()

        return carry

    mine.wait()
    swap.wait_recv()
    for step in range(1, planes):
        second(step, 1 - half).start()
    for which in range(2):
        third(0, which).start()
    lax.fori_loop(0, 2 * HEADS, send_weights, 0)
    for flow in flows:
        flow.start(me)
    for step in range(planes):
        if step > 0:
            second(step, half).wait_recv()
            second(step, 1 - half).wait_recv()
            for which in range(2):
                third(step, which).start()
            for which in range(2):
                third(step - 1, which).wait_recv()
            for which in range(2):
                fourth(step - 1, which).start()
    for which in range(2):
        third(planes - 1, which).wait_recv()
    for which in range(2):
        fourth(planes - 1, which).start()
    for step in range(planes):
        for which in range(2):
            fourth(step, which).wait_recv()

    @pl.when(attends(me))
    def _():
        own = pltpu.make_async_copy(w_ref.at[combo_of(me) % HEADS], wall_ref.at[me], local.at[1])
        own.start()
        own.wait()

        def took(k, carry):
            before = (me + k) % count
            pltpu.make_async_remote_copy(
                w_ref.at[0],
                wall_ref.at[before],
                wsend.at[0],
                wreceive.at[before],
                device_id=net.at(before),
                device_id_type=MESH,
            ).wait_recv()
            return carry

        lax.fori_loop(1, count, took, 0)

    def sent(combo, carry):
        @pl.when(device_of(combo) != me)
        def _():
            weights(combo).wait_send()

        return carry

    lax.fori_loop(0, 2 * HEADS, sent, 0)
    swap.wait_send()
    for step in range(1, planes):
        direct(step).wait_send()
        second(step, 1 - half).wait_send()
    for step in range(planes):
        for which in range(2):
            third(step, which).wait_send()
            fourth(step, which).wait_send()
    for flow in flows:
        flow.finish(me)


def gather_tokens(net, number, normed, columns, cut, out):
    planes = net.planes
    copies = 1 + 2 * (planes - 1) + 4 * planes
    flows = [
        Flow(0, 0, lambda i, j: j % GROUP, lambda i, j: i % GROUP, size=GROUP),
        Across(net, 1, 1, lambda i, j: 0, lambda i, j: i // GROUP),
    ]
    shapes = [
        jax.ShapeDtypeStruct((planes, 2, 4) + normed.shape[1:], normed.dtype),
        jax.ShapeDtypeStruct((net.count,) + columns.shape[1:], columns.dtype),
        jax.ShapeDtypeStruct(cut.shape, cut.dtype),
        jax.ShapeDtypeStruct((planes,) + out.shape[1:], out.dtype),
    ]
    return pl.pallas_call(
        functools.partial(gather_kernel, net, flows),
        out_shape=shapes,
        in_specs=[ANY] * 4,
        out_specs=[ANY] * 4,
        scratch_shapes=[
            pltpu.SemaphoreType.DMA((copies,)),
            pltpu.SemaphoreType.DMA((copies,)),
            pltpu.SemaphoreType.DMA((2 * HEADS,)),
            pltpu.SemaphoreType.DMA((net.count,)),
            pltpu.SemaphoreType.DMA((2,)),
        ]
        + flow_scratch(flows),
        compiler_params=pltpu.CompilerParams(collective_id=number, has_side_effects=True),
        cost_estimate=pl.CostEstimate(flops=0, bytes_accessed=100 * 2**20, transcendentals=0),
        name="gather_tokens",
    )(normed, columns, cut, out)


def rope_rows(values, cosine, sine):
    first, second = values[:HALF], values[HALF:]
    return jnp.concatenate([first * cosine - second * sine, second * cosine + first * sine], axis=0)


def rope_rows_back(values, cosine, sine):
    first, second = values[:HALF], values[HALF:]
    return jnp.concatenate([first * cosine + second * sine, second * cosine - first * sine], axis=0)


def columns_of(index):
    return pl.ds(pl.multiple_of(index * BLOCK, BLOCK), BLOCK)


def positions(query_block, key_block):
    shape = (BLOCK, BLOCK)
    key = key_block * BLOCK + lax.broadcasted_iota(jnp.int32, shape, 0)
    query = query_block * BLOCK + lax.broadcasted_iota(jnp.int32, shape, 1)
    return key, query


def fold(rows):
    return jnp.concatenate([rows[:HALF], rows[HALF:]], axis=1)


def unfold(rows):
    return jnp.concatenate([rows[:, :HEAD_DIM], rows[:, HEAD_DIM:]], axis=0)


def attend_kernel(net, *refs):
    @pl.when(attends(net.me()))
    def _():
        attend_body(*refs)


def attend_body(first_ref, x_ref, w_ref, cos_ref, sin_ref, start_ref, qkv_ref, mixed_ref, total_ref, packed_ref, key_rows):
    blocks = qkv_ref.shape[1] // BLOCK
    weights = w_ref[...]

    def project(chunk, carry):
        tokens = x_ref[chunk // 2, chunk % 2].reshape(BLOCK, D)
        here = columns_of(chunk)
        made = nt(weights, tokens)
        cosine, sine = cos_ref[:, here], sin_ref[:, here]
        query = rope_rows(made[:HEAD_DIM], cosine, sine)
        key = rope_rows(made[HEAD_DIM : 2 * HEAD_DIM], cosine, sine)
        qkv_ref[:HEAD_DIM, here] = query.astype(jnp.bfloat16)
        qkv_ref[HEAD_DIM : 2 * HEAD_DIM, here] = key.astype(jnp.bfloat16)
        qkv_ref[2 * HEAD_DIM :, here] = made[2 * HEAD_DIM :].astype(jnp.bfloat16)
        key_rows[here, :] = key.T.astype(jnp.bfloat16)
        return carry

    lax.fori_loop(0, blocks, project, 0)

    def query_step(query_block, carry):
        here = columns_of(query_block)
        query = qkv_ref[:HEAD_DIM, here]
        start = start_ref[:, here]

        def key_step(key_block, held):
            top, total, mixed = held
            there = columns_of(key_block)
            scores = nn(key_rows[there, :], query) * SCALE
            key_at, query_at = positions(query_block, key_block)
            allowed = (key_at <= query_at) & (key_at >= start)
            scores = jnp.where(allowed, scores, NEGATIVE)
            new_top = jnp.maximum(top, jnp.max(scores, axis=0, keepdims=True))
            weights = jnp.where(allowed, jnp.exp(scores - new_top), 0.0)
            factor = jnp.exp(top - new_top)
            total = total * factor + jnp.sum(weights, axis=0, keepdims=True)
            mixed = mixed * factor + nn(qkv_ref[2 * HEAD_DIM :, there], weights.astype(jnp.bfloat16))
            return new_top, total, mixed

        top, total, mixed = lax.fori_loop(
            first_ref[query_block],
            query_block + 1,
            key_step,
            (
                jnp.full((1, BLOCK), NEGATIVE, jnp.float32),
                jnp.zeros((1, BLOCK), jnp.float32),
                jnp.zeros((HEAD_DIM, BLOCK), jnp.float32),
            ),
        )
        mixed = mixed / total
        mixed_ref[:, here] = mixed
        total_ref[:, here] = top + jnp.log(total)
        rows = mixed.T
        for part in range(BLOCK // 64):
            packed_ref[query_block * (BLOCK // 64) + part] = fold(rows[part * 64 : part * 64 + 64]).astype(
                jnp.bfloat16
            )
        return carry

    lax.fori_loop(0, blocks, query_step, 0)


def attend(net, first, tokens, weights, cosine, sine, start):
    length = start.shape[1]
    return pl.pallas_call(
        functools.partial(attend_kernel, net),
        out_shape=[
            jax.ShapeDtypeStruct((3 * HEAD_DIM, length), jnp.bfloat16),
            jax.ShapeDtypeStruct((HEAD_DIM, length), jnp.float32),
            jax.ShapeDtypeStruct((1, length), jnp.float32),
            jax.ShapeDtypeStruct((net.count, HALF, 128), jnp.bfloat16),
        ],
        in_specs=[SMEM] + [VMEM] * 5,
        out_specs=[VMEM] * 4,
        scratch_shapes=[pltpu.VMEM((length, HEAD_DIM), jnp.bfloat16)],
        cost_estimate=pl.CostEstimate(flops=2 * 10**9, bytes_accessed=8 * 2**20, transcendentals=2 * 10**6),
        name="attend",
    )(first, tokens, weights, cosine, sine, start)


def attend_back_kernel(net, *refs):
    @pl.when(attends(net.me()))
    def _():
        attend_back_body(*refs)


def attend_back_body(
    first_ref,
    x_ref,
    qkv_ref,
    mixed_ref,
    total_ref,
    cos_ref,
    sin_ref,
    start_ref,
    grad_ref,
    packed_ref,
    weight_ref,
    query_rows,
    key_rows,
    value_rows,
    grad_rows,
    grad_columns,
    correction,
    key_grad,
    value_grad,
    all_grad,
):
    blocks = qkv_ref.shape[1] // BLOCK
    parts = BLOCK // 64

    def prepare(chunk, carry):
        here = columns_of(chunk)
        turned = qkv_ref[:, here].astype(jnp.float32)
        query_rows[here, :] = turned[:HEAD_DIM].T.astype(jnp.bfloat16)
        key_rows[here, :] = turned[HEAD_DIM : 2 * HEAD_DIM].T.astype(jnp.bfloat16)
        value_rows[here, :] = turned[2 * HEAD_DIM :].T.astype(jnp.bfloat16)
        pieces = [unfold(grad_ref[chunk * parts + part].astype(jnp.float32)) for part in range(parts)]
        rows = jnp.concatenate(pieces, axis=0)
        grad_rows[here, :] = rows.astype(jnp.bfloat16)
        across = rows.T
        grad_columns[:, here] = across.astype(jnp.bfloat16)
        correction[:, here] = jnp.sum(across * mixed_ref[:, here], axis=0, keepdims=True)
        key_grad[here, :] = jnp.zeros((BLOCK, HEAD_DIM), jnp.float32)
        value_grad[here, :] = jnp.zeros((BLOCK, HEAD_DIM), jnp.float32)
        return carry

    lax.fori_loop(0, blocks, prepare, 0)

    def query_step(query_block, carry):
        here = columns_of(query_block)
        query = qkv_ref[:HEAD_DIM, here]
        start = start_ref[:, here]
        total = total_ref[:, here]
        fix = correction[:, here]
        grad = grad_columns[:, here]
        query_in_rows = query_rows[here, :]
        grad_in_rows = grad_rows[here, :]

        def key_step(key_block, query_grad):
            there = columns_of(key_block)
            scores = nn(key_rows[there, :], query) * SCALE
            key_at, query_at = positions(query_block, key_block)
            allowed = (key_at <= query_at) & (key_at >= start)
            weights = jnp.where(allowed, jnp.exp(scores - total), 0.0)
            value_grad[there, :] += nn(weights.astype(jnp.bfloat16), grad_in_rows)
            slope = nn(value_rows[there, :], grad)
            change = (weights * (slope - fix) * SCALE).astype(jnp.bfloat16)
            key_grad[there, :] += nn(change, query_in_rows)
            return query_grad + nn(qkv_ref[HEAD_DIM : 2 * HEAD_DIM, there], change)

        query_grad = lax.fori_loop(
            first_ref[query_block], query_block + 1, key_step, jnp.zeros((HEAD_DIM, BLOCK), jnp.float32)
        )
        query_grad = rope_rows_back(query_grad, cos_ref[:, here], sin_ref[:, here])
        all_grad[:HEAD_DIM, here] = query_grad.astype(jnp.bfloat16)
        rows = query_grad.T.astype(jnp.bfloat16)
        for part in range(parts):
            packed_ref[query_block * parts + part, :64, :HEAD_DIM] = rows[part * 64 : part * 64 + 64]
        return carry

    lax.fori_loop(0, blocks, query_step, 0)
    weight_ref[...] = jnp.zeros(weight_ref.shape, jnp.float32)

    def close(chunk, carry):
        here = columns_of(chunk)
        key = rope_rows_back(key_grad[here, :].T, cos_ref[:, here], sin_ref[:, here])
        value = value_grad[here, :]
        all_grad[HEAD_DIM : 2 * HEAD_DIM, here] = key.astype(jnp.bfloat16)
        all_grad[2 * HEAD_DIM :, here] = value.T.astype(jnp.bfloat16)
        rows = key.T.astype(jnp.bfloat16)
        for part in range(parts):
            token = chunk * parts + part
            packed_ref[token, :64, HEAD_DIM:] = rows[part * 64 : part * 64 + 64]
            packed_ref[token, 64:, :] = fold(value[part * 64 : part * 64 + 64]).astype(jnp.bfloat16)
        tokens = x_ref[chunk // 2, chunk % 2].reshape(BLOCK, D)
        weight_ref[...] += nn(all_grad[:, here], tokens)
        return carry

    lax.fori_loop(0, blocks, close, 0)


def attend_back(net, first, tokens, qkv, mixed, total, cosine, sine, start, grad):
    length = start.shape[1]
    rows = pltpu.VMEM((length, HEAD_DIM), jnp.bfloat16)
    sums = pltpu.VMEM((length, HEAD_DIM), jnp.float32)
    return pl.pallas_call(
        functools.partial(attend_back_kernel, net),
        out_shape=[
            jax.ShapeDtypeStruct((net.count, 96, 128), jnp.bfloat16),
            jax.ShapeDtypeStruct((3 * HEAD_DIM, D), jnp.float32),
        ],
        in_specs=[SMEM] + [VMEM] * 8,
        out_specs=[VMEM] * 2,
        scratch_shapes=[
            rows,
            rows,
            rows,
            rows,
            pltpu.VMEM((HEAD_DIM, length), jnp.bfloat16),
            pltpu.VMEM((1, length), jnp.float32),
            sums,
            sums,
            pltpu.VMEM((3 * HEAD_DIM, length), jnp.bfloat16),
        ],
        cost_estimate=pl.CostEstimate(flops=4 * 10**9, bytes_accessed=12 * 2**20, transcendentals=2 * 10**6),
        name="attend_back",
    )(first, tokens, qkv, mixed, total, cosine, sine, start, grad)


def layer_norm(values):
    center = values - jnp.mean(values, axis=-1, keepdims=True)
    spread = jnp.mean(center * center, axis=-1, keepdims=True)
    return center * lax.rsqrt(spread + EPSILON)


def norm_back(values, gradient):
    center = values - jnp.mean(values, axis=-1, keepdims=True)
    inverse = lax.rsqrt(jnp.mean(center * center, axis=-1, keepdims=True) + EPSILON)
    normed = center * inverse
    return inverse * (
        gradient
        - jnp.mean(gradient, axis=-1, keepdims=True)
        - normed * jnp.mean(gradient * normed, axis=-1, keepdims=True)
    )


def newton_kernel(net, head_ref, moment_ref, out_ref, ffn_ref, attn_out, ffn_out, wide, parts, moment, gram, polynomial, semaphore):
    me = net.me()

    def blocks_of(index):
        return pl.ds(pl.multiple_of(index * BLOCK, BLOCK), BLOCK)

    def move(source, target):
        copy = pltpu.make_async_copy(source, target, semaphore)
        copy.start()
        copy.wait()

    def mirror(target, i, j, block):
        target[i * BLOCK : (i + 1) * BLOCK, j * BLOCK : (j + 1) * BLOCK] = block.astype(jnp.bfloat16)
        if i != j:
            target[j * BLOCK : (j + 1) * BLOCK, i * BLOCK : (i + 1) * BLOCK] = block.T.astype(jnp.bfloat16)

    def solve(span, target):
        chunks = span // BLOCK

        def measure(index, total):
            values = wide[:, blocks_of(index)].astype(jnp.float32)
            return total + jnp.sum(values * values, axis=0, keepdims=True)

        total = lax.fori_loop(0, chunks, measure, jnp.zeros((1, BLOCK), jnp.float32))
        frobenius = jnp.sqrt(jnp.sum(total, axis=1, keepdims=True)) + 1e-07

        def scale(index, carry):
            here = blocks_of(index)
            wide[:, here] = (wide[:, here].astype(jnp.float32) / frobenius).astype(jnp.bfloat16)
            return carry

        lax.fori_loop(0, chunks, scale, 0)

        def step(_, carry):
            for i in range(D // BLOCK):
                for j in range(i + 1):
                    mirror(
                        gram,
                        i,
                        j,
                        nt(
                            wide[i * BLOCK : (i + 1) * BLOCK, :span],
                            wide[j * BLOCK : (j + 1) * BLOCK, :span],
                        ),
                    )
            for i in range(D // BLOCK):
                for j in range(i + 1):
                    square = nn(gram[i * BLOCK : (i + 1) * BLOCK, :], gram[:, j * BLOCK : (j + 1) * BLOCK])
                    linear = gram[i * BLOCK : (i + 1) * BLOCK, j * BLOCK : (j + 1) * BLOCK].astype(jnp.float32)
                    mirror(polynomial, i, j, COEFF_B * linear + COEFF_C * square)

            def advance(index, inner):
                here = blocks_of(index)
                old = wide[:, here]
                wide[:, here] = (COEFF_A * old.astype(jnp.float32) + nn(polynomial[...], old)).astype(jnp.bfloat16)
                return inner

            lax.fori_loop(0, chunks, advance, 0)
            return carry

        lax.fori_loop(0, NS_STEPS, step, 0)
        move(wide.at[:, pl.ds(0, span)], target)

    kind = jnp.int32(3)
    for matrix in range(7):
        kind = jnp.where(me == OWNERS[matrix], jnp.int32(0 if matrix < 3 else 1 if matrix == 3 else 2), kind)

    @pl.when(kind == 0)
    def _():
        move(head_ref, parts)
        move(moment_ref, moment)

        def join(pair, carry):
            first = parts[2 * pair].astype(jnp.float32) + parts[HEADS + 2 * pair].astype(jnp.float32)
            second = parts[2 * pair + 1].astype(jnp.float32) + parts[HEADS + 2 * pair + 1].astype(jnp.float32)
            here = pl.ds(pl.multiple_of(pair * 128, 128), 128)
            gradient = jnp.concatenate([first, second], axis=0).T
            wide[:, here] = (0.75 * gradient + 0.25 * moment[:, here].astype(jnp.float32)).astype(jnp.bfloat16)
            return carry

        lax.fori_loop(0, HEADS // 2, join, 0)
        solve(D, attn_out)

    @pl.when(kind == 1)
    def _():
        move(out_ref, wide.at[:, pl.ds(0, D)])
        solve(D, attn_out)

    @pl.when(kind == 2)
    def _():
        move(ffn_ref, wide)
        solve(FF, ffn_out)


def newton(net, heads, moment, out, ffn):
    return pl.pallas_call(
        functools.partial(newton_kernel, net),
        out_shape=[jax.ShapeDtypeStruct(out.shape, out.dtype), jax.ShapeDtypeStruct(ffn.shape, ffn.dtype)],
        in_specs=[ANY] * 4,
        out_specs=[ANY] * 2,
        scratch_shapes=[
            pltpu.VMEM((D, FF), jnp.bfloat16),
            pltpu.VMEM(heads.shape, jnp.bfloat16),
            pltpu.VMEM((D, D), jnp.bfloat16),
            pltpu.VMEM((D, D), jnp.bfloat16),
            pltpu.VMEM((D, D), jnp.bfloat16),
            pltpu.SemaphoreType.DMA,
        ],
        cost_estimate=pl.CostEstimate(flops=25 * 10**9, bytes_accessed=8 * 2**20, transcendentals=0),
        name="newton",
    )(heads, moment, out, ffn)


def pick(values, index):
    return lax.dynamic_index_in_dim(values, index, 0, keepdims=False)


def tn(a, b):
    return lax.dot_general(a, b, (((0,), (0,)), ((), ())), preferred_element_type=jnp.float32)


def on_device(net, tokens, doc_ids, cotangent, attn_weight, ffn_weight, attn_moment, ffn_moment):
    micro_count, token_count, width = tokens.shape
    rows = attn_weight.shape[1]
    count, planes = net.count, net.planes
    length = count * token_count
    me = net.me()
    plane, place = me // GROUP, me % GROUP
    x_bit = place // 4
    both = micro_count * token_count
    part = FF // GROUP
    low = jnp.bfloat16

    attn_low = attn_weight.astype(low)
    ffn_low = ffn_weight.astype(low)
    cut = ffn_low.reshape(3, rows, GROUP, part).transpose(2, 1, 0, 3).reshape(GROUP, rows, 3 * part)
    out_grad = cotangent.reshape(both, width)
    hidden = tokens.astype(jnp.float32).reshape(both, width)
    normed = layer_norm(hidden).astype(low)
    counts = jnp.sum((doc_ids[:, :, None] == jnp.arange(DOCS)[None, None, :]).astype(jnp.float32), axis=1)
    tail = jnp.pad(counts.reshape(-1).astype(low), (0, HEAD_DIM - micro_count * DOCS))
    columns = attn_low[:3].reshape(3, rows, HEADS, HEAD_DIM).transpose(2, 1, 0, 3).reshape(HEADS, rows, 3 * HEAD_DIM)
    columns = jnp.concatenate([columns, jnp.broadcast_to(tail, (HEADS, rows, HEAD_DIM))], axis=2)
    all_tokens, all_columns, plane_cut, plane_out = gather_tokens(
        net, 0, normed.reshape(micro_count, token_count, width), columns, cut, attn_low[3:]
    )
    late_own = plane_cut.reshape(GROUP * rows, 3 * part)
    late_full = jnp.zeros((planes, GROUP * rows, 3 * part), low)
    late_full = lax.dynamic_update_index_in_dim(late_full, late_own, plane, 0)
    for step in range(1, planes):
        late_full = lax.dynamic_update_index_in_dim(
            late_full, net.shift(late_own, step), (plane + planes - step) % planes, 0
        )
    late_full = late_full.reshape(D, 3 * part)
    gate_full, up_full, down_full = (late_full[:, part * k : part * (k + 1)] for k in range(3))

    head_weights = all_columns[:, :, : 3 * HEAD_DIM].reshape(D, 3 * HEAD_DIM).T
    every_count = jnp.sum(all_columns[:, 0, 3 * HEAD_DIM :].astype(jnp.float32), axis=0)
    own_count = lax.dynamic_slice_in_dim(every_count, x_bit * DOCS, DOCS, 0)
    starts = jnp.cumsum(own_count) - own_count
    index = jnp.arange(length).astype(jnp.float32)
    start = jnp.max(jnp.where(starts[:, None] <= index[None, :], starts[:, None], 0.0), axis=0)
    inverse = 10000.0 ** (-(jnp.arange(HALF, dtype=jnp.float32) * 2.0) / HEAD_DIM)
    angles = inverse[:, None] * (index - start)[None, :]
    cosine, sine = jnp.cos(angles), jnp.sin(angles)
    start = start.astype(jnp.int32)
    block_index = jnp.arange(length // BLOCK, dtype=jnp.int32)
    first = jnp.clip(start[::BLOCK] // BLOCK, 0, block_index)
    start = start[None, :]

    qkv, mixed, total, packed = attend(net, first, all_tokens, head_weights, cosine, sine, start)
    mixed_parts, moment_whole, plane_out_grad, out_full = exchange(
        net,
        "mixed_exchange",
        1,
        [PlaneGather(2, 2), PlaneGather(3, 3)]
        + [Flow(0, 0, lambda i, j: j, lambda i, j: combo_of(i), lambda i, j: attends(i))]
        + [FanIn(1, 1, OWNERS[k], lambda i, j, k=k: k, lambda i, j: i) for k in range(3)],
        [packed, attn_moment.astype(low), out_grad, plane_out],
        [
            jax.ShapeDtypeStruct((2 * HEADS, HALF, 128), low),
            jax.ShapeDtypeStruct((count, rows, D), low),
            jax.ShapeDtypeStruct((GROUP, both, width), low),
            jax.ShapeDtypeStruct((GROUP, planes, rows, D), low),
        ],
    )
    plane_out_grad = plane_out_grad.reshape(GROUP * both, width)
    out_full = out_full.reshape(2, 2, 2, planes, rows, D).transpose(3, 2, 0, 1, 4, 5).reshape(D, D)
    mixed_tokens = (
        mixed_parts.reshape(micro_count, HEADS, HALF, 2, HEAD_DIM).transpose(0, 3, 2, 1, 4).reshape(both, width)
    )

    middle = hidden + nn(mixed_tokens, out_full)
    second = layer_norm(middle).astype(low)
    (plane_second,) = exchange(
        net,
        "second_exchange",
        7,
        [PlaneGather(0, 0)],
        [second],
        [jax.ShapeDtypeStruct((GROUP, both, width), low)],
        GROUP,
    )
    plane_second = plane_second.reshape(GROUP * both, width)
    gate, up = nn(plane_second, gate_full), nn(plane_second, up_full)
    gate_sigmoid = jax.nn.sigmoid(gate)
    gate_silu = gate * gate_sigmoid
    product = (gate_silu * up).astype(low)
    product_grad = nn(plane_out_grad, down_full)
    gate_grad = (product_grad * up * gate_sigmoid * (1.0 + gate * (1.0 - gate_sigmoid))).astype(low)
    up_grad = (product_grad * gate_silu).astype(low)
    second_terms = (nt(gate_grad, gate_full) + nt(up_grad, up_full)).astype(low)
    result_terms = nt(product, down_full).astype(low)
    ffn_terms = jnp.concatenate(
        [
            tn(plane_second, gate_grad).astype(low),
            tn(plane_second, up_grad).astype(low),
            tn(plane_out_grad, product).astype(low),
        ],
        axis=1,
    ).reshape(planes, GROUP * rows, 3 * part)
    (second_grad,) = exchange(
        net,
        "second_grad_exchange",
        8,
        [PlaneScatter(0, 0, (both, width))],
        [second_terms.reshape(GROUP, both, width)],
        [jax.ShapeDtypeStruct((both, width), jnp.float32)],
        GROUP,
    )
    ffn_block = pick(ffn_terms, plane).astype(jnp.float32)
    for step in range(1, planes):
        ffn_block = ffn_block + net.shift(pick(ffn_terms, (plane + step) % planes), step).astype(jnp.float32)
    ffn_block = ffn_block.astype(low)

    middle_grad = out_grad.astype(jnp.float32) + norm_back(middle, second_grad)
    middle_low = middle_grad.astype(low)
    mixed_grad = nt(middle_low, out_full).astype(low)
    folded = (
        mixed_grad.reshape(micro_count, 2, HALF, HEADS, HEAD_DIM).transpose(0, 3, 2, 1, 4).reshape(2 * HEADS, HALF, 128)
    )
    out_terms = tn(mixed_tokens, middle_low).astype(low).reshape(planes, 2, 2, 2, rows, D)
    out_terms = out_terms.transpose(2, 3, 1, 0, 4, 5).reshape(GROUP, planes, rows, D)
    grad_parts, out_row_grad, ffn_parts = exchange(
        net,
        "mixed_grad_exchange",
        2,
        [
            PlaneScatter(1, 1, (planes, rows, D), planes),
            Flow(0, 0, lambda i, j: combo_of(j), lambda i, j: i, lambda i, j: attends(j)),
            Flow(2, 2, lambda i, j: j % GROUP, lambda i, j: i % GROUP, size=GROUP),
        ],
        [folded, out_terms, ffn_block.reshape(GROUP, rows, 3 * part)],
        [
            jax.ShapeDtypeStruct((count, HALF, 128), low),
            jax.ShapeDtypeStruct((rows, D), jnp.float32),
            jax.ShapeDtypeStruct((GROUP, rows, 3 * part), low),
        ],
    )
    ffn_grad = ffn_parts.reshape(GROUP, rows, 3, part).transpose(2, 1, 0, 3).reshape(3, rows, FF).astype(jnp.float32)
    ffn_moment_new = 0.5 * ffn_moment + 0.5 * ffn_grad
    out_moment_new = 0.5 * attn_moment[3] + 0.5 * out_row_grad
    ffn_update = (0.5 * ffn_grad + 0.5 * ffn_moment_new).astype(low)
    out_update = (0.5 * out_row_grad + 0.5 * out_moment_new).astype(low)
    update = jnp.concatenate([ffn_update.transpose(1, 0, 2).reshape(rows, 3 * FF), out_update], axis=1)
    updates = []
    for source in range(planes):
        if source == SPARE:
            updates.append(update)
        else:
            hop = [(GROUP * source + k, GROUP * SPARE + k) for k in range(GROUP)]
            updates.append(net.permute(update, hop))
    updates = jnp.stack(updates)
    ffn_updates = updates[:, :, : 3 * FF].reshape(planes, rows, 3, FF).transpose(2, 0, 1, 3)
    out_updates = updates[None, :, :, 3 * FF :]

    early_low, grad_parts = lax.optimization_barrier((attn_low[:3], grad_parts))
    attn_full = lax.all_gather(early_low, ("blk", "head"), axis=1, tiled=True)
    grad_packed, head_grad = attend_back(
        net, first, all_tokens, qkv, mixed, total, cosine, sine, start, grad_parts
    )
    head_low = head_grad.astype(low)
    grad_packed, head_low, ffn_updates, out_updates = lax.optimization_barrier(
        (grad_packed, head_low, ffn_updates, out_updates)
    )
    everything = (slice(None),)
    ffn_whole, out_whole = exchange(
        net,
        "update_exchange",
        4,
        [
            FanIn(
                0,
                0,
                OWNERS[4 + k],
                lambda i, j, k=k: k,
                lambda i, j: everything + (i % GROUP,),
                size=GROUP,
            )
            for k in range(3)
        ]
        + [FanIn(1, 1, OWNERS[3], lambda i, j: 0, lambda i, j: everything + (i % GROUP,), size=GROUP)],
        [ffn_updates, out_updates],
        [
            jax.ShapeDtypeStruct((planes, GROUP, rows, FF), low),
            jax.ShapeDtypeStruct((planes, GROUP, rows, D), low),
        ],
        GROUP,
    )
    (head_whole,) = exchange(
        net,
        "head_exchange",
        9,
        [
            FanIn(0, 0, OWNERS[k], lambda i, j, k=k: k, lambda i, j: combo_of(i), lambda i, j: attends(i))
            for k in range(3)
        ],
        [head_low.reshape(3, HEAD_DIM, D)],
        [jax.ShapeDtypeStruct((2 * HEADS, HEAD_DIM, D), low)],
        meet=net.meet_attending,
    )

    grad_packed, head_low, head_whole, ffn_whole = lax.optimization_barrier(
        (grad_packed, head_low, head_whole, ffn_whole)
    )
    head_rows = head_low.T.reshape(count, rows, 3 * HEAD_DIM)
    head_rows = jnp.pad(head_rows, ((0, 0), (0, 0), (0, 64))).reshape(planes, GROUP, rows * 2, 128)
    outgoing = jnp.concatenate([grad_packed.reshape(planes, GROUP, 96, 128), head_rows], axis=2)
    arrived = [pick(outgoing, plane)]
    for step in range(1, planes):
        hop = [
            (GROUP * p + k, (GROUP * (p + step) + k) % count) for p in range(4) if p != SPARE for k in range(GROUP)
        ]
        arrived.append(net.permute(pick(outgoing, (plane + step) % planes), hop))

    attn_done, ffn_done = newton(
        net, head_whole, moment_whole.reshape(D, D), out_whole.reshape(D, D), ffn_whole.reshape(D, FF)
    )
    attn_done, ffn_done, *arrived = lax.optimization_barrier((attn_done, ffn_done, *arrived))
    arrived = jnp.stack(arrived)
    arrived = jnp.stack([pick(arrived, (plane + planes - source) % planes) for source in range(4) if source != SPARE])

    attn_step, ffn_step, grads, result = exchange(
        net,
        "step_exchange",
        5,
        [PlaneScatter(3, 3, (both, width))]
        + [FanOut(0, 0, OWNERS[k], lambda i, j: j, lambda i, j, k=k: k) for k in range(4)]
        + [FanOut(1, 1, OWNERS[4 + k], lambda i, j: j, lambda i, j, k=k: k) for k in range(3)]
        + [
            Flow(
                2, 2, lambda i, j: everything + (j % GROUP,), lambda i, j: everything + (i % GROUP,), size=GROUP
            )
        ],
        [
            attn_done.reshape(count, rows, D),
            ffn_done.reshape(count, rows, FF),
            arrived,
            result_terms.reshape(GROUP, both, width),
        ],
        [
            jax.ShapeDtypeStruct((4, rows, D), low),
            jax.ShapeDtypeStruct((3, rows, FF), low),
            jax.ShapeDtypeStruct(arrived.shape, low),
            jax.ShapeDtypeStruct((both, width), jnp.float32),
        ],
    )

    grads = grads.reshape(3, micro_count, 4, 96 + 2 * rows, 128).transpose(1, 0, 2, 3, 4)
    grads = grads.reshape(micro_count, HEADS, 96 + 2 * rows, 128)
    summed = jnp.sum(grads[:, :, 96:].astype(jnp.float32), axis=0).reshape(HEADS, rows, 256)
    early_grad = summed[:, :, : 3 * HEAD_DIM].reshape(HEADS, rows, 3, HEAD_DIM).transpose(2, 1, 0, 3).reshape(3, rows, D)
    attn_grad = jnp.concatenate([early_grad, out_row_grad[None]], axis=0)
    attn_moment_new = 0.5 * attn_moment + 0.5 * attn_grad

    pair = grads[:, :, :64].reshape(micro_count, HEADS, token_count, 2, HEAD_DIM)
    query_key = pair.transpose(3, 0, 2, 1, 4).reshape(2, both, width)
    value = (
        grads[:, :, 64:96].reshape(micro_count, HEADS, HALF, 2, HEAD_DIM).transpose(0, 3, 2, 1, 4).reshape(both, width)
    )
    normed_grad = nt(query_key[0], attn_full[0]) + nt(query_key[1], attn_full[1]) + nt(value, attn_full[2])
    input_grad = middle_grad + norm_back(hidden, normed_grad)

    output = (middle + result).astype(low)

    rates = jnp.asarray(RATES, jnp.float32)[:, None, None]
    attn_master = attn_weight - rates[:4] * attn_step.astype(jnp.float32)
    ffn_master = ffn_weight - rates[4:] * ffn_step.astype(jnp.float32)
    shape = (micro_count, token_count, width)
    return (
        output.reshape(shape),
        input_grad.reshape(shape),
        attn_grad,
        ffn_grad,
        attn_master,
        ffn_master,
        attn_moment_new,
        ffn_moment_new,
        attn_master.astype(low),
        ffn_master.astype(low),
    )


def solution(mesh):
    wide = P(None, ("blk", "head"), None)
    return jax.shard_map(
        functools.partial(on_device, Net(mesh)),
        mesh=mesh,
        in_specs=(wide, P(None, ("blk", "head")), wide, wide, wide, wide, wide),
        out_specs=(wide,) * 10,
        check_vma=False,
    )
```

profile of v0, /device:TPU:18, one launch (start us, length us, event | category | flops | bytes accessed | tf_op | source)
XLA Modules:
  0.0 369.0 jit_solution(11370232993067208842)
XLA Ops:
  14.9 37.6 %gather_tokens.1 = (bf16[4,2,4,64,768]{4,3,2,1,0:T(8,128)(2,1)}, bf16[32,24,256]{2,1,0:T(8,128)(2,1)}, bf16[8,24,768]{2,1,0:T(8,128)(2,1)}, bf16[4,24,768]{2,1,0:T(8,128)(2,1)}) custom-call(bf16[2,64,768]{2,1,0:T(8,128)(2,1)} %multiply_convert_fusion.3.x_ref, bf16[12,24,256]{2,1,0:T(8,128)(2,1)} %pad_maximum_fusion.6.w_ref, ...), custom_call_target="tpu_custom_call" | custom-call | bytes 104857600 | tf_op jit(solution)/shard_map/gather_tokens/pallas_call | solution.py:620
  52.5 5.2 %collective-permute-start = (bf16[192,768]{1,0:T(8,128)(2,1)}, bf16[192,768]{1,0:T(8,128)(2,1)}, u32[]{:S(2)}, u32[]{:S(2)}) collective-permute-start(bf16[192,768]{1,0:T(8,128)(2,1)} %bitcast.227), channel_id=1, source_target_pairs={{0,4},{16,20},{1,5},{17,21},{2,6},{18,22},{3,7},{19,23},{4,8},{20,... | collective-permute-start | bytes 884744 | tf_op jit(solution)/shard_map/ppermute | solution.py:72
  58.7 2.8 collective-permute-start.2
  63.7 1.9 copy.64
  68.0 3.2 attend.1
  71.2 44.7 %mixed_exchange.1 = (bf16[24,32,128]{2,1,0:T(8,128)(2,1)}, bf16[32,24,768]{2,1,0:T(8,128)(2,1)}, bf16[8,128,768]{2,1,0:T(8,128)(2,1)}, bf16[8,4,24,768]{3,2,1,0:T(8,128)(2,1)}) custom-call(bf16[32,32,128]{2,1,0:T(8,128)(2,1)} %get-tuple-element.53.refs_0_, bf16[4,24,768]{2,1,0:T(8,128)(2,1)} %convert_element_type.165.refs_1_, bf16[128,768]{1,0:T(8,128)(2,1)} %bitcast.220, ...), custom_call_target="tpu_custom_call" | custom-call | bytes 33030144 | tf_op jit(solution)/shard_map/mixed_exchange/pallas_call | solution.py:458
  120.0 14.3 %second_exchange.1 = bf16[8,128,768]{2,1,0:T(8,128)(2,1)} custom-call(bf16[128,768]{1,0:T(8,128)(2,1)} %fusion.16.refs_0_), custom_call_target="tpu_custom_call" | custom-call | bytes 12582912 | tf_op jit(solution)/shard_map/second_exchange/pallas_call | solution.py:458
  146.2 2.4 copy.69
  148.6 2.1 dynamic-slice_bitcast_fusion.2
  152.4 6.3 %collective-permute-start.4 = (bf16[192,768]{1,0:T(8,128)(2,1)}, bf16[192,768]{1,0:T(8,128)(2,1)}, u32[]{:S(2)}, u32[]{:S(2)}) collective-permute-start(bf16[192,768]{1,0:T(8,128)(2,1)} %get-tuple-element.116), channel_id=1, source_target_pairs={{0,8},{16,24},{1,9},{17,25},{2,10},{18,26},{3,11},{19,27},{4,12},{... | collective-permute-start | bytes 884744 | tf_op jit(solution)/shard_map/ppermute | solution.py:72
  158.8 2.8 add_convert_fusion
  161.6 15.6 %second_grad_exchange.1 = f32[128,768]{1,0:T(8,128)} custom-call(bf16[8,128,768]{2,1,0:T(8,128)(2,1)} %bitcast.179), custom_call_target="tpu_custom_call" | custom-call | bytes 3145728 | tf_op jit(solution)/shard_map/second_grad_exchange/pallas_call | solution.py:458
  184.3 2.8 convolution_convert_fusion
  187.0 2.1 fusion.4
  189.1 26.2 %mixed_grad_exchange.1 = (bf16[32,32,128]{2,1,0:T(8,128)(2,1)}, f32[24,768]{1,0:T(8,128)}, bf16[8,24,768]{2,1,0:T(8,128)(2,1)}) custom-call(bf16[24,32,128]{2,1,0:T(8,128)(2,1)} %reshape.317.refs_0_, bf16[8,4,24,768]{3,2,1,0:T(8,128)(2,1)} %bitcast.183, bf16[8,24,768]{2,1,0:T(8,128)(2,1)} %bitcast.214), custom_call_target="tpu_custom_call" | custom-call | bytes 5046272 | tf_op jit(solution)/shard_map/mixed_grad_exchange/pallas_call | solution.py:458
  222.7 3.6 attend_back.1
  226.2 1.8 convert_element_type.184
  228.1 3.3 collective-permute-done.6
  231.4 8.6 %collective-permute-done.7 = bf16[24,6912]{1,0:T(8,128)(2,1)S(1)} collective-permute-done((bf16[24,6912]{1,0:T(8,128)(2,1)S(1)}, bf16[24,6912]{1,0:T(8,128)(2,1)S(1)}, u32[]{:S(2)}, u32[]{:S(2)}) %collective-permute-start.7) | collective-permute-done | bytes 331808 | tf_op jit(solution)/shard_map/ppermute | solution.py:72
  243.9 23.0 %update_exchange.1 = (bf16[4,8,24,2048]{3,2,1,0:T(8,128)(2,1)}, bf16[4,8,24,768]{3,2,1,0:T(8,128)(2,1)}) custom-call(bf16[3,4,24,2048]{3,2,1,0:T(8,128)(2,1)} %bitcast.184, bf16[1,4,24,768]{3,2,1,0:T(8,128)(2,1)} %maximum_bitcast_fusion.refs_1_), custom_call_target="tpu_custom_call" | custom-call | bytes 34603008 | tf_op jit(solution)/shard_map/update_exchange/pallas_call | solution.py:458
  272.7 37.7 %newton.1 = (bf16[768,768]{1,0:T(8,128)(2,1)}, bf16[768,2048]{1,0:T(8,128)(2,1)}) custom-call(bf16[24,64,768]{2,1,0:T(8,128)(2,1)} %head_exchange.1.head_ref, bf16[768,768]{1,0:T(8,128)(2,1)} %bitcast.236, bf16[768,768]{1,0:T(8,128)(2,1)} %bitcast.237, bf16[768,2048]{1,0:T(8,128)(2,1)} %bitcast.235), custom_call_target="tpu_custom_call" | custom-call | flops 24999999488 | bytes 8388608 | tf_op jit(solution)/shard_map/newton/pallas_call | solution.py:995
  311.7 35.2 %step_exchange.1 = (bf16[4,24,768]{2,1,0:T(8,128)(2,1)}, bf16[3,24,2048]{2,1,0:T(8,128)(2,1)}, bf16[3,8,144,128]{3,2,1,0:T(8,128)(2,1)}, f32[128,768]{1,0:T(8,128)}) custom-call(bf16[32,24,768]{2,1,0:T(8,128)(2,1)} %bitcast.209, bf16[32,24,2048]{2,1,0:T(8,128)(2,1)} %bitcast.190, bf16[3,8,144,128]{3,2,1,0:T(8,128)(2,1)} %pad_maximum_fusion.3.refs_2_, ...), custom_call_target="tpu_custom_call" | custom-call | bytes 13762560 | tf_op jit(solution)/shard_map/step_exchange/pallas_call | solution.py:458
  357.4 1.8 convolution_add_fusion.1
  359.3 1.9 fusion.33
  (199 shorter events, 66.8 us)
Async XLA Ops:
  7.2 3.9 %copy-start.4 = (bf16[2,64,768]{2,1,0:T(8,128)(2,1)S(1)}, bf16[2,64,768]{2,1,0:T(8,128)(2,1)}, u32[]{:S(2)}) copy-start(bf16[2,64,768]{2,1,0:T(8,128)(2,1)} %param.8) | copy-start | bytes 589828
  7.2 348.4 %all-gather.2.cloned.1.call-start = ((), (), s32[]{:S(2)}) async-start(), calls=%async_computation | async-start | bytes 3649536 | tf_op jit(solution)/shard_map/all_gather | solution.py:1177
  8.3 3.9 %copy-start.17 = (bf16[3,24,768]{2,1,0:T(8,128)(2,1)}, bf16[3,24,768]{2,1,0:T(8,128)(2,1)S(1)}, u32[]{:S(2)}) copy-start(bf16[3,24,768]{2,1,0:T(8,128)(2,1)S(1)} %slice.93) | copy-start | bytes 331780
  8.3 4.3 %copy-start.34 = (s32[2,64]{1,0:T(2,128)S(1)}, s32[2,64]{1,0:T(2,128)}, u32[]{:S(2)}) copy-start(s32[2,64]{1,0:T(2,128)} %param.9) | copy-start | bytes 1540
  8.3 4.5 %copy-start.7 = (f32[3,24,2048]{2,1,0:T(8,128)S(1)}, f32[3,24,2048]{2,1,0:T(8,128)}, u32[]{:S(2)}) copy-start(f32[3,24,2048]{2,1,0:T(8,128)} %param.12) | copy-start | bytes 1769476
  13.2 52.3 %copy-start.14 = (f32[4,24,768]{2,1,0:T(8,128)S(1)}, f32[4,24,768]{2,1,0:T(8,128)}, u32[]{:S(2)}) copy-start(f32[4,24,768]{2,1,0:T(8,128)} %param.13) | copy-start | bytes 884740
  52.5 81.8 %collective-permute-start = (bf16[192,768]{1,0:T(8,128)(2,1)}, bf16[192,768]{1,0:T(8,128)(2,1)}, u32[]{:S(2)}, u32[]{:S(2)}) collective-permute-start(bf16[192,768]{1,0:T(8,128)(2,1)} %bitcast.227), channel_id=1, source_target_pairs={{0,4},{16,20},{1,5},{17,21},{2,6},{18,22},{3,7},{19,23},{4,8},{20,... | collective-permute-start | bytes 884744 | tf_op jit(solution)/shard_map/ppermute | solution.py:72
  57.8 77.7 %collective-permute-start.1 = (bf16[192,768]{1,0:T(8,128)(2,1)}, bf16[192,768]{1,0:T(8,128)(2,1)}, u32[]{:S(2)}, u32[]{:S(2)}) collective-permute-start(bf16[192,768]{1,0:T(8,128)(2,1)} %bitcast.228), channel_id=1, source_target_pairs={{0,8},{16,24},{1,9},{17,25},{2,10},{18,26},{3,11},{19,27},{4,12},{... | collective-permute-start | bytes 884744 | tf_op jit(solution)/shard_map/ppermute | solution.py:72
  58.7 77.8 %collective-permute-start.2 = (bf16[192,768]{1,0:T(8,128)(2,1)}, bf16[192,768]{1,0:T(8,128)(2,1)}, u32[]{:S(2)}, u32[]{:S(2)}) collective-permute-start(bf16[192,768]{1,0:T(8,128)(2,1)} %bitcast.229), channel_id=1, source_target_pairs={{0,12},{16,28},{1,13},{17,29},{2,14},{18,30},{3,15},{19,31},{4,0},... | collective-permute-start | bytes 884744 | tf_op jit(solution)/shard_map/ppermute | solution.py:72
  63.0 5.0 %copy-start.31 = (s32[2048]{0:T(1024)}, s32[2048]{0:T(1024)S(1)}, u32[]{:S(2)}) copy-start(s32[2048]{0:T(1024)S(1)} %get-tuple-element.124) | copy-start | bytes 24580
  134.3 3.2 copy-start.12
  140.8 2.9 copy-start.21
  148.6 10.2 %copy-start.24 = (bf16[1024,256]{1,0:T(8,128)(2,1)S(1)}, bf16[1024,256]{1,0:T(8,128)(2,1)}, u32[]{:S(2)}) copy-start(bf16[1024,256]{1,0:T(8,128)(2,1)} %copy-done.23) | copy-start | bytes 1572868
  150.7 36.3 %collective-permute-start.3 = (bf16[192,768]{1,0:T(8,128)(2,1)}, bf16[192,768]{1,0:T(8,128)(2,1)}, u32[]{:S(2)}, u32[]{:S(2)}) collective-permute-start(bf16[192,768]{1,0:T(8,128)(2,1)} %get-tuple-element.114), channel_id=1, source_target_pairs={{0,4},{16,20},{1,5},{17,21},{2,6},{18,22},{3,7},{19,23},{4,8},{20,... | collective-permute-start | bytes 884744 | tf_op jit(solution)/shard_map/ppermute | solution.py:72
  152.4 34.6 %collective-permute-start.4 = (bf16[192,768]{1,0:T(8,128)(2,1)}, bf16[192,768]{1,0:T(8,128)(2,1)}, u32[]{:S(2)}, u32[]{:S(2)}) collective-permute-start(bf16[192,768]{1,0:T(8,128)(2,1)} %get-tuple-element.116), channel_id=1, source_target_pairs={{0,8},{16,24},{1,9},{17,25},{2,10},{18,26},{3,11},{19,27},{4,12},{... | collective-permute-start | bytes 884744 | tf_op jit(solution)/shard_map/ppermute | solution.py:72
  158.8 28.3 %collective-permute-start.5 = (bf16[192,768]{1,0:T(8,128)(2,1)}, bf16[192,768]{1,0:T(8,128)(2,1)}, u32[]{:S(2)}, u32[]{:S(2)}) collective-permute-start(bf16[192,768]{1,0:T(8,128)(2,1)} %get-tuple-element.115), channel_id=1, source_target_pairs={{0,12},{16,28},{1,13},{17,29},{2,14},{18,30},{3,15},{19,31},{4,0},... | collective-permute-start | bytes 884744 | tf_op jit(solution)/shard_map/ppermute | solution.py:72
  161.6 16.9 %copy-start.19 = (bf16[2,64,768]{2,1,0:T(8,128)(2,1)S(1)}, bf16[2,64,768]{2,1,0:T(8,128)(2,1)}, u32[]{:S(2)}) copy-start(bf16[2,64,768]{2,1,0:T(8,128)(2,1)} %param.10) | copy-start | bytes 589828
  218.8 12.6 %collective-permute-start.6 = (bf16[24,6912]{1,0:T(8,128)(2,1)S(1)}, bf16[24,6912]{1,0:T(8,128)(2,1)S(1)}, u32[]{:S(2)}, u32[]{:S(2)}) collective-permute-start(bf16[24,6912]{1,0:T(8,128)(2,1)S(1)} %get-tuple-element.120), channel_id=1, source_target_pairs={{0,8},{16,24},{1,9},{17,25},{2,10},{18,26},{3,11},{19,27}} | collective-permute-start | bytes 995336 | tf_op jit(solution)/shard_map/ppermute | solution.py:72
  220.1 19.9 %collective-permute-start.7 = (bf16[24,6912]{1,0:T(8,128)(2,1)S(1)}, bf16[24,6912]{1,0:T(8,128)(2,1)S(1)}, u32[]{:S(2)}, u32[]{:S(2)}) collective-permute-start(bf16[24,6912]{1,0:T(8,128)(2,1)S(1)} %get-tuple-element.120), channel_id=1, source_target_pairs={{4,8},{20,24},{5,9},{21,25},{6,10},{22,26},{7,11},{23,27}} | collective-permute-start | bytes 995336 | tf_op jit(solution)/shard_map/ppermute | solution.py:72
  221.4 18.6 %collective-permute-start.8 = (bf16[24,6912]{1,0:T(8,128)(2,1)S(1)}, bf16[24,6912]{1,0:T(8,128)(2,1)S(1)}, u32[]{:S(2)}, u32[]{:S(2)}) collective-permute-start(bf16[24,6912]{1,0:T(8,128)(2,1)S(1)} %get-tuple-element.120), channel_id=1, source_target_pairs={{12,8},{28,24},{13,9},{29,25},{14,10},{30,26},{15,11},{31,27}} | collective-permute-start | bytes 995336 | tf_op jit(solution)/shard_map/ppermute | solution.py:72
  243.9 23.0 %copy-start.6 = (bf16[192,768]{1,0:T(8,128)(2,1)S(1)}, bf16[192,768]{1,0:T(8,128)(2,1)}, u32[]{:S(2)}) copy-start(bf16[192,768]{1,0:T(8,128)(2,1)} %convert_element_type.184) | copy-start | bytes 884740
  268.8 41.6 %collective-permute-start.10 = (bf16[8,144,128]{2,1,0:T(8,128)(2,1)}, bf16[8,144,128]{2,1,0:T(8,128)(2,1)S(1)}, u32[]{:S(2)}, u32[]{:S(2)}) collective-permute-start(bf16[8,144,128]{2,1,0:T(8,128)(2,1)} %get-tuple-element.113), channel_id=1, source_target_pairs={{0,8},{16,24},{1,9},{17,25},{2,10},{18,26},{3,11},{19,27},{4,12},{... | collective-permute-start | bytes 884744 | tf_op jit(solution)/shard_map/ppermute | solution.py:72
  270.1 40.3 %collective-permute-start.11 = (bf16[8,144,128]{2,1,0:T(8,128)(2,1)S(1)}, bf16[8,144,128]{2,1,0:T(8,128)(2,1)S(1)}, u32[]{:S(2)}, u32[]{:S(2)}) collective-permute-start(bf16[8,144,128]{2,1,0:T(8,128)(2,1)S(1)} %get-tuple-element.110), channel_id=1, source_target_pairs={{0,12},{16,28},{1,13},{17,29},{2,14},{18,30},{3,15},{19,31},{4,0},... | collective-permute-start | bytes 884744 | tf_op jit(solution)/shard_map/ppermute | solution.py:72
  271.4 39.0 %collective-permute-start.9 = (bf16[8,144,128]{2,1,0:T(8,128)(2,1)S(1)}, bf16[8,144,128]{2,1,0:T(8,128)(2,1)S(1)}, u32[]{:S(2)}, u32[]{:S(2)}) collective-permute-start(bf16[8,144,128]{2,1,0:T(8,128)(2,1)S(1)} %get-tuple-element.112), channel_id=1, source_target_pairs={{0,4},{16,20},{1,5},{17,21},{2,6},{18,22},{3,7},{19,23},{4,8},{20,... | collective-permute-start | bytes 884744 | tf_op jit(solution)/shard_map/ppermute | solution.py:72
  (24 other events, 35.6 us)
Sparse Core Ops, SparseCore 0:
  217.2 65.3 all-gather.1
where the time goes:
time: 372 us; the launch traced here: 369 us
  Pallas kernels  243 us (65%)
  local copies, waits for them, and re-layouts  30.1 us (8%)
  other arithmetic  26 us (7%)
  starting transfers between devices  24.8 us (7%)
  matrix products  18.1 us (5%)
  between operations  15.2 us (4%)
  waiting for transfers between devices  12 us (3%)
    pallas_call x7, Pallas kernels, exchange(): pl.pallas_call(functools.partial(exchange_kernel, net, meet or (lambda me...  161 us
    pallas_call x1, Pallas kernels, newton(): pl.pallas_call(functools.partial(newton_kernel, net), out_shape=[jax.Shap...  37.7 us
    pallas_call x1, Pallas kernels, gather_tokens(): pl.pallas_call(functools.partial(gather_kernel, net, flows), out_shape=sh...  37.6 us
    ppermute x12, starting transfers between devices, permute(): lax.ppermute(values, ('head', 'blk'), [(place(i), place(j)) for i, j in p...  24.8 us
    dot_general x7, matrix products, nt(): lax.dot_general(a, b, (((1,), (1,)), ((), ())), preferred_element_type=jn...  13.3 us
    ppermute x12, waiting for transfers between devices, permute(): lax.ppermute(values, ('head', 'blk'), [(place(i), place(j)) for i, j in p...  11.9 us
  transfers between devices with their start and end apart: 13, of which 2 were waited for; matrix products, arithmetic and copies ran while one was open for 11% of the time, Pallas kernels for 49%

commit v1 on v0

v1 whole, which is shorter than its diff:
```python
import functools
import math

import jax
import jax.numpy as jnp
from jax import lax
from jax.experimental import pallas as pl
from jax.experimental.pallas import tpu as pltpu
from jax.sharding import PartitionSpec as P

D = 768
HEADS = 12
HEAD_DIM = 64
HALF = 32
FF = 2048
DOCS = 4
NS_STEPS = 5
GROUP = 8
SPARE = 2
BLOCK = 256
WIDE = 512

EPSILON = 1e-05
NEGATIVE = -1e30
RATES = (0.5, 0.5, 0.5, 7.0, 1.0, 1.0, 0.5)
COEFF_A = 3.4445
COEFF_B = -4.775
COEFF_C = 2.0315
OWNERS = (18, 19, 22, 21, 16, 17, 20)
MESH = pl.DeviceIdType.MESH
ANY = pl.BlockSpec(memory_space=pl.ANY)
VMEM = pl.BlockSpec(memory_space=pltpu.VMEM)
SMEM = pl.BlockSpec(memory_space=pltpu.SMEM)
SCALE = HEAD_DIM ** (-0.5)


def nt(a, b):
    return lax.dot_general(a, b, (((1,), (1,)), ((), ())), preferred_element_type=jnp.float32)


def nn(a, b):
    return jnp.dot(a, b, preferred_element_type=jnp.float32)


def attends(device):
    plane = device // GROUP
    return jnp.logical_and(plane < 4, plane != SPARE)


def combo_of(device):
    plane = device // GROUP
    place = device % GROUP
    return (place // 4) * HEADS + 4 * (plane - plane // 3) + place % 4


def device_of(combo):
    group = (combo % HEADS) // 4
    return GROUP * (group + group // 2) + 4 * (combo // HEADS) + combo % 4


class Net:
    def __init__(self, mesh):
        self.inner = mesh.shape["head"]
        self.count = mesh.shape["head"] * mesh.shape["blk"]
        self.planes = self.count // GROUP

    def permute(self, values, pairs):
        outer = self.count // self.inner

        def place(device):
            return (device % self.inner) * outer + device // self.inner

        return lax.ppermute(values, ("head", "blk"), [(place(i), place(j)) for i, j in pairs])

    def me(self):
        return lax.axis_index("blk") * self.inner + lax.axis_index("head")

    def at(self, device):
        return {"blk": device // self.inner, "head": device % self.inner}

    def meet(self, me, size):
        self.greet(me, size)
        pl.semaphore_wait(pltpu.get_barrier_semaphore(), size - 1)

    def greet(self, me, size):
        barrier = pltpu.get_barrier_semaphore()

        def greet(k, carry):
            pl.semaphore_signal(barrier, inc=1, device_id=self.at(peer(me, k, size)), device_id_type=MESH)
            return carry

        lax.fori_loop(1, size, greet, 0)

    def meet_attending(self, me):
        barrier = pltpu.get_barrier_semaphore()

        @pl.when(attends(me))
        def _():
            def greet(combo, carry):
                other = device_of(combo)

                @pl.when(other != me)
                def _():
                    pl.semaphore_signal(barrier, inc=1, device_id=self.at(other), device_id_type=MESH)

                return carry

            lax.fori_loop(0, 2 * HEADS, greet, 0)
            pl.semaphore_wait(barrier, 2 * HEADS - 1)

    def meet_heads(self, me):
        barrier = pltpu.get_barrier_semaphore()

        @pl.when(attends(me))
        def _():
            for owner in OWNERS[:3]:
                pl.semaphore_signal(barrier, inc=1, device_id=self.at(owner), device_id_type=MESH)
            pl.semaphore_wait(barrier, 3)

        for owner in OWNERS[:3]:

            @pl.when(me == owner)
            def _():
                def greet(combo, carry):
                    pl.semaphore_signal(barrier, inc=1, device_id=self.at(device_of(combo)), device_id_type=MESH)
                    return carry

                lax.fori_loop(0, 2 * HEADS, greet, 0)
                pl.semaphore_wait(barrier, 2 * HEADS)

    def shift(self, values, steps):
        far = GROUP * steps
        return self.permute(values, [(i, (i + far) % self.count) for i in range(self.count)])

    def flip(self, values, distance):
        return self.permute(values, [(i, i ^ distance) for i in range(self.count)])


def peer(me, k, size):
    return (me // size) * size + (me % size + k) % size


def flip_x(device):
    return device + 4 - 8 * ((device % GROUP) // 4)


def flip_y(device):
    return device + 1 - 2 * (device % 2)


def flip_core(device):
    return device + 2 - 4 * ((device % 4) // 2)


class Flow:
    def __init__(self, source, target, take, put, goes=None, size=None):
        self.source, self.target, self.take, self.put = source, target, take, put
        self.goes = goes or (lambda i, j: i >= 0)
        self.size = size

    def scratch(self):
        return []

    def semaphores(self):
        return self.size

    def bind(self, net, inputs, outputs, scratch, send, receive, local):
        self.net = net
        self.input, self.output = inputs[self.source], outputs[self.target]
        self.held = scratch
        self.send, self.receive, self.local = send, receive, local

    def copy(self, source, target, index, device):
        return pltpu.make_async_remote_copy(
            source,
            target,
            self.send.at[index],
            self.receive.at[index],
            device_id=self.net.at(device),
            device_id_type=MESH,
        )

    def remote(self, i, j, k):
        return self.copy(self.input.at[self.take(i, j)], self.output.at[self.put(i, j)], k, j)

    def near(self, i):
        return pltpu.make_async_copy(self.input.at[self.take(i, i)], self.output.at[self.put(i, i)], self.local)

    def start(self, me):
        def one(k, carry):
            other = peer(me, k, self.size)

            @pl.when(self.goes(me, other))
            def _():
                self.remote(me, other, k).start()

            return carry

        lax.fori_loop(1, self.size, one, 0)

        @pl.when(self.goes(me, me))
        def _():
            self.near(me).start()

    def middle(self, me):
        pass

    def finish(self, me):
        def one(k, carry):
            other = peer(me, k, self.size)

            @pl.when(self.goes(me, other))
            def _():
                self.remote(me, other, k).wait_send()

            before = peer(me, self.size - k, self.size)

            @pl.when(self.goes(before, me))
            def _():
                self.remote(before, me, k).wait_recv()

            return carry

        lax.fori_loop(1, self.size, one, 0)

        @pl.when(self.goes(me, me))
        def _():
            self.near(me).wait()


class Across(Flow):
    def __init__(self, net, source, target, take, put, goes=None):
        super().__init__(source, target, take, put, goes, net.count)
        self.planes = net.planes

    def semaphores(self):
        return self.planes

    def other(self, me, k):
        return (me + k * GROUP) % self.size

    def start(self, me):
        for k in range(1, self.planes):
            far = self.other(me, k)

            @pl.when(self.goes(me, far))
            def _(k=k, far=far):
                self.remote(me, far, k).start()

        @pl.when(self.goes(me, me))
        def _():
            self.near(me).start()

    def finish(self, me):
        for k in range(1, self.planes):
            far, before = self.other(me, k), self.other(me, self.planes - k)

            @pl.when(self.goes(me, far))
            def _(k=k, far=far):
                self.remote(me, far, k).wait_send()

            @pl.when(self.goes(before, me))
            def _(k=k, before=before):
                self.remote(before, me, k).wait_recv()

        @pl.when(self.goes(me, me))
        def _():
            self.near(me).wait()


class FanIn(Flow):
    def __init__(self, source, target, owner, take, put, goes=None, size=None):
        super().__init__(source, target, take, put, goes, size)
        self.place = owner

    def owner(self, me):
        return (me // self.size) * self.size + self.place

    def sends(self, me):
        return jnp.logical_and(me % self.size != self.place, self.goes(me, self.owner(me)))

    def step(self, me):
        return (self.place - me % self.size + self.size) % self.size

    def start(self, me):
        @pl.when(self.sends(me))
        def _():
            self.remote(me, self.owner(me), self.step(me)).start()

        @pl.when(jnp.logical_and(me % self.size == self.place, self.goes(me, me)))
        def _():
            self.near(me).start()

    def finish(self, me):
        @pl.when(self.sends(me))
        def _():
            self.remote(me, self.owner(me), self.step(me)).wait_send()

        @pl.when(me % self.size == self.place)
        def _():
            def one(k, carry):
                before = peer(me, self.size - k, self.size)

                @pl.when(self.goes(before, me))
                def _():
                    self.remote(before, me, k).wait_recv()

                return carry

            lax.fori_loop(1, self.size, one, 0)

        @pl.when(jnp.logical_and(me % self.size == self.place, self.goes(me, me)))
        def _():
            self.near(me).wait()


class FanOut(Flow):
    def __init__(self, source, target, owner, take, put):
        super().__init__(source, target, take, put)
        self.owner = owner

    def start(self, me):
        @pl.when(me == self.owner)
        def _():
            def one(k, carry):
                self.remote(me, peer(me, k, self.size), k).start()
                return carry

            lax.fori_loop(1, self.size, one, 0)
            self.near(me).start()

    def finish(self, me):
        @pl.when(me == self.owner)
        def _():
            def one(k, carry):
                self.remote(me, peer(me, k, self.size), k).wait_send()
                return carry

            lax.fori_loop(1, self.size, one, 0)
            self.near(me).wait()

        @pl.when(me != self.owner)
        def _():
            self.remote(self.owner, me, (me - self.owner + self.net.count) % self.size).wait_recv()


class PlaneGather(Flow):
    def __init__(self, source, target, put=lambda i: i % GROUP):
        super().__init__(source, target, None, put)

    def semaphores(self):
        return GROUP

    def partners(self, me):
        return [flip_x(me), flip_y(me), flip_x(flip_y(me))]

    def place(self, device):
        return self.output.at[self.put(device)]

    def own(self, me, index, device):
        return self.copy(self.input, self.place(me), index, device)

    def passed(self, me, index, partner):
        return self.copy(self.place(partner), self.place(partner), 4 + index, flip_core(me))

    def start(self, me):
        for index, partner in enumerate(self.partners(me)):
            self.own(me, 1 + index, partner).start()
        self.own(me, 0, flip_core(me)).start()
        pltpu.make_async_copy(self.input, self.place(me), self.local).start()

    def middle(self, me):
        for index, partner in enumerate(self.partners(me)):
            self.own(me, 1 + index, partner).wait_recv()
            self.passed(me, index, partner).start()

    def finish(self, me):
        for index, partner in enumerate(self.partners(me)):
            self.own(me, 1 + index, partner).wait_send()
            self.passed(me, index, partner).wait()
        self.own(me, 0, flip_core(me)).wait()
        pltpu.make_async_copy(self.input, self.place(me), self.local).wait()


class PlaneScatter(Flow):
    def __init__(self, source, target, block, lead=(), runs=None, gathers=False):
        super().__init__(source, target, None, None)
        self.block, self.lead, self.gathers = block, lead, gathers
        self.runs = runs or (lambda i: i >= 0)
        self.every = (slice(None),) * len(lead)

    def scratch(self):
        pair = pltpu.VMEM(self.lead + (2, 2) + self.block, jnp.bfloat16)
        shapes = [pair, pair, pltpu.VMEM((3,) + self.lead + self.block, jnp.bfloat16)]
        if self.gathers:
            shapes += [
                pltpu.VMEM(self.lead + self.block, jnp.bfloat16),
                pltpu.VMEM(self.lead + self.lead + self.block, jnp.bfloat16),
            ]
        return shapes

    def semaphores(self):
        return 5 + (self.lead[0] if self.gathers else 0)

    def onward(self, me, source):
        spare = GROUP * SPARE + me % GROUP
        return self.copy(self.held[3], self.held[4].at[source], 5 + source, spare)

    def partners(self, me):
        return [flip_x(me), flip_y(me), flip_x(flip_y(me))]

    def half(self, core):
        return self.input.at[self.every + (slice(None), core)]

    def first(self, me):
        return self.copy(self.half(1 - (me % 4) // 2), self.held[1], 0, flip_core(me))

    def mine(self, me):
        return pltpu.make_async_copy(self.half((me % 4) // 2), self.held[0], self.local)

    def spot(self, device):
        return self.every + ((device % GROUP) // 4, device % 2)

    def second(self, me, index, partner):
        return self.copy(self.held[0].at[self.spot(partner)], self.held[2].at[index], 1 + index, partner)

    def start(self, me):
        @pl.when(self.runs(me))
        def _():
            self.first(me).start()
            self.mine(me).start()

    def pair(self, device):
        spot = self.spot(device)
        return self.held[0][spot].astype(jnp.float32) + self.held[1][spot].astype(jnp.float32)

    def middle(self, me):
        @pl.when(self.runs(me))
        def _():
            self.mine(me).wait()
            self.first(me).wait_recv()
            for index, partner in enumerate(self.partners(me)):
                self.held[0][self.spot(partner)] = self.pair(partner).astype(jnp.bfloat16)
                self.second(me, index, partner).start()

    def finish(self, me):
        @pl.when(self.runs(me))
        def _():
            total = self.pair(me)
            for index, partner in enumerate(self.partners(me)):
                self.second(me, index, partner).wait_recv()
                total = total + self.held[2][index].astype(jnp.float32)
            if self.gathers:
                plane = me // GROUP
                self.held[3][...] = total.astype(jnp.bfloat16)

                @pl.when(plane != SPARE)
                def _():
                    self.onward(me, plane).start()

            self.output[...] = total
            self.first(me).wait_send()
            for index, partner in enumerate(self.partners(me)):
                self.second(me, index, partner).wait_send()
            if self.gathers:

                @pl.when(plane != SPARE)
                def _():
                    self.onward(me, plane).wait_send()

                @pl.when(plane == SPARE)
                def _():
                    for source in range(self.lead[0]):
                        if source != SPARE:
                            self.onward(me, source).wait_recv()
                            self.output[...] += self.held[4][source].astype(jnp.float32)


def bind_all(net, flows, inputs, outputs, scratch, send, receive, local):
    used = 0
    for number, flow in enumerate(flows):
        need = len(flow.scratch())
        flow.bind(
            net, inputs, outputs, scratch[used : used + need], send.at[number], receive.at[number], local.at[number]
        )
        used += need


def exchange_kernel(net, meet, flows, sources, targets, *refs):
    inputs = refs[:sources]
    outputs = refs[sources : sources + targets]
    me = net.me()
    meet(me)
    bind_all(net, flows, inputs, outputs, refs[sources + targets : -3], *refs[-3:])
    for flow in flows:
        flow.start(me)
    for flow in flows:
        flow.middle(me)
    for flow in flows:
        flow.finish(me)


def flow_scratch(flows):
    most = max(flow.semaphores() for flow in flows)
    return [shape for flow in flows for shape in flow.scratch()] + [
        pltpu.SemaphoreType.DMA((len(flows), most)),
        pltpu.SemaphoreType.DMA((len(flows), most)),
        pltpu.SemaphoreType.DMA((len(flows),)),
    ]


def exchange(net, name, number, flows, sources, shapes, size=None, meet=None):
    size = size or net.count
    for flow in flows:
        flow.size = flow.size or size
    summed = {flow.target for flow in flows if isinstance(flow, PlaneScatter)}
    moved = sum(math.prod(s.shape) * s.dtype.itemsize for s in shapes)
    return pl.pallas_call(
        functools.partial(
            exchange_kernel, net, meet or (lambda me: net.meet(me, size)), flows, len(sources), len(shapes)
        ),
        out_shape=shapes,
        in_specs=[ANY] * len(sources),
        out_specs=[VMEM if k in summed else ANY for k in range(len(shapes))],
        scratch_shapes=flow_scratch(flows),
        compiler_params=pltpu.CompilerParams(collective_id=number, has_side_effects=True),
        cost_estimate=pl.CostEstimate(flops=0, bytes_accessed=8 * moved, transcendentals=0),
        name=name,
    )(*sources)


def gather_kernel(net, flows, extras, x_ref, w_ref, *refs):
    extra_refs, (all_ref, wall_ref), refs = refs[:extras], refs[extras : extras + 2], refs[extras + 2 :]
    extra_all, (send, receive, wsend, wreceive, local), refs = refs[:extras], refs[extras : extras + 5], refs[extras + 5 :]
    count = net.count
    planes = net.planes
    me = net.me()
    plane = me // GROUP
    place = me % GROUP
    half = place // 4
    spot = place % 4
    across = flip_x(me)
    beside = flip_y(me)
    sibling = flip_core(me)
    net.meet(me, count)
    bind_all(net, flows, extra_refs, extra_all, (), *refs)

    def remote(source, target, index, device):
        return pltpu.make_async_remote_copy(
            source, target, send.at[index], receive.at[index], device_id=net.at(device), device_id_type=MESH
        )

    swap = remote(x_ref.at[1 - half], all_ref.at[plane, half, spot], 0, across)
    swap.start()

    def second(step, which):
        target = (me + step * GROUP) % count
        block = all_ref.at[plane, which, spot]
        return remote(block, block, 1 + (step - 1) * 2 + (which + half) % 2, target)

    def direct(step):
        target = (me + step * GROUP) % count
        return remote(x_ref.at[half], all_ref.at[plane, half, spot], 1 + (step - 1) * 2, target)

    third_base = 1 + 2 * (planes - 1)

    def third(step, which):
        source_plane = (plane + planes - step) % planes
        block = all_ref.at[source_plane, which, spot]
        return remote(block, block, third_base + step * 2 + which, beside)

    fourth_base = third_base + 2 * planes

    def fourth(step, which):
        source_plane = (plane + planes - step) % planes
        block = all_ref.at[source_plane, which, pl.ds((spot // 2) * 2, 2)]
        return remote(block, block, fourth_base + step * 2 + which, sibling)

    for step in range(1, planes):
        direct(step).start()
    mine = pltpu.make_async_copy(x_ref.at[half], all_ref.at[plane, half, spot], local.at[0])
    mine.start()

    def weights(combo):
        target = device_of(combo)
        return pltpu.make_async_remote_copy(
            w_ref.at[combo % HEADS],
            wall_ref.at[me],
            wsend.at[combo],
            wreceive.at[me],
            device_id=net.at(target),
            device_id_type=MESH,
        )

    def send_weights(combo, carry):
        @pl.when(device_of(combo) != me)
        def _():
            weights(combo).start()

        return carry

    mine.wait()
    swap.wait_recv()
    for step in range(1, planes):
        second(step, 1 - half).start()
    for which in range(2):
        third(0, which).start()
    lax.fori_loop(0, 2 * HEADS, send_weights, 0)
    for flow in flows:
        flow.start(me)
    for step in range(planes):
        if step > 0:
            second(step, half).wait_recv()
            second(step, 1 - half).wait_recv()
            for which in range(2):
                third(step, which).start()
            for which in range(2):
                third(step - 1, which).wait_recv()
            for which in range(2):
                fourth(step - 1, which).start()
    for which in range(2):
        third(planes - 1, which).wait_recv()
    for which in range(2):
        fourth(planes - 1, which).start()
    for step in range(planes):
        for which in range(2):
            fourth(step, which).wait_recv()

    @pl.when(attends(me))
    def _():
        own = pltpu.make_async_copy(w_ref.at[combo_of(me) % HEADS], wall_ref.at[me], local.at[1])
        own.start()
        own.wait()

        def took(k, carry):
            before = (me + k) % count
            pltpu.make_async_remote_copy(
                w_ref.at[0],
                wall_ref.at[before],
                wsend.at[0],
                wreceive.at[before],
                device_id=net.at(before),
                device_id_type=MESH,
            ).wait_recv()
            return carry

        lax.fori_loop(1, count, took, 0)

    def sent(combo, carry):
        @pl.when(device_of(combo) != me)
        def _():
            weights(combo).wait_send()

        return carry

    lax.fori_loop(0, 2 * HEADS, sent, 0)
    swap.wait_send()
    for step in range(1, planes):
        direct(step).wait_send()
        second(step, 1 - half).wait_send()
    for step in range(planes):
        for which in range(2):
            third(step, which).wait_send()
            fourth(step, which).wait_send()
    for flow in flows:
        flow.finish(me)


def gather_tokens(net, number, normed, columns, flows, extras, shapes):
    planes = net.planes
    copies = 1 + 2 * (planes - 1) + 4 * planes
    for flow in flows:
        flow.size = flow.size or net.count
    shapes = [
        jax.ShapeDtypeStruct((planes, 2, 4) + normed.shape[1:], normed.dtype),
        jax.ShapeDtypeStruct((net.count,) + columns.shape[1:], columns.dtype),
    ] + shapes
    return pl.pallas_call(
        functools.partial(gather_kernel, net, flows, len(extras)),
        out_shape=shapes,
        in_specs=[ANY] * (2 + len(extras)),
        out_specs=[ANY] * len(shapes),
        scratch_shapes=[
            pltpu.SemaphoreType.DMA((copies,)),
            pltpu.SemaphoreType.DMA((copies,)),
            pltpu.SemaphoreType.DMA((2 * HEADS,)),
            pltpu.SemaphoreType.DMA((net.count,)),
            pltpu.SemaphoreType.DMA((2,)),
        ]
        + flow_scratch(flows),
        compiler_params=pltpu.CompilerParams(collective_id=number, has_side_effects=True),
        cost_estimate=pl.CostEstimate(flops=0, bytes_accessed=100 * 2**20, transcendentals=0),
        name="gather_tokens",
    )(normed, columns, *extras)


def rope_rows(values, cosine, sine):
    first, second = values[:HALF], values[HALF:]
    return jnp.concatenate([first * cosine - second * sine, second * cosine + first * sine], axis=0)


def rope_rows_back(values, cosine, sine):
    first, second = values[:HALF], values[HALF:]
    return jnp.concatenate([first * cosine + second * sine, second * cosine - first * sine], axis=0)


def columns_of(index):
    return pl.ds(pl.multiple_of(index * BLOCK, BLOCK), BLOCK)


def wide_columns(index):
    return pl.ds(pl.multiple_of(index * WIDE, WIDE), WIDE)


def permitted(query_block, key_block, start):
    shape = (BLOCK, WIDE)
    key = key_block * BLOCK + lax.broadcasted_iota(jnp.int32, shape, 0)
    query = query_block * WIDE + lax.broadcasted_iota(jnp.int32, shape, 1)
    return (key <= query) & (key >= start)


def sweep(bounds_ref, query_block, step, carried):
    diagonal = query_block * (WIDE // BLOCK)
    first, whole = bounds_ref[0, query_block], bounds_ref[1, query_block]
    carried = lax.fori_loop(first, whole, functools.partial(step, True), carried)
    carried = lax.fori_loop(whole, diagonal, functools.partial(step, False), carried)
    return lax.fori_loop(diagonal, diagonal + WIDE // BLOCK, functools.partial(step, True), carried)


def fold(rows):
    return jnp.concatenate([rows[:HALF], rows[HALF:]], axis=1)


def unfold(rows):
    return jnp.concatenate([rows[:, :HEAD_DIM], rows[:, HEAD_DIM:]], axis=0)


def attend_kernel(net, *refs):
    @pl.when(attends(net.me()))
    def _():
        attend_body(*refs)


def attend_body(first_ref, x_ref, w_ref, cos_ref, sin_ref, start_ref, qkv_ref, mixed_ref, total_ref, packed_ref, key_rows):
    blocks = qkv_ref.shape[1] // BLOCK
    weights = w_ref[...]

    def project(chunk, carry):
        tokens = x_ref[chunk // 2, chunk % 2].reshape(BLOCK, D)
        here = columns_of(chunk)
        made = nt(weights, tokens)
        cosine, sine = cos_ref[:, here], sin_ref[:, here]
        query = rope_rows(made[:HEAD_DIM], cosine, sine)
        key = rope_rows(made[HEAD_DIM : 2 * HEAD_DIM], cosine, sine)
        qkv_ref[:HEAD_DIM, here] = query.astype(jnp.bfloat16) * SCALE
        qkv_ref[HEAD_DIM : 2 * HEAD_DIM, here] = key.astype(jnp.bfloat16)
        qkv_ref[2 * HEAD_DIM :, here] = made[2 * HEAD_DIM :].astype(jnp.bfloat16)
        key_rows[here, :] = key.T.astype(jnp.bfloat16)
        return carry

    lax.fori_loop(0, blocks, project, 0)

    def query_step(query_block, carry):
        here = wide_columns(query_block)
        query = qkv_ref[:HEAD_DIM, here]
        start = start_ref[:, here]

        def key_step(masked, key_block, held):
            top, total, mixed = held
            there = columns_of(key_block)
            scores = nn(key_rows[there, :], query)
            if masked:
                allowed = permitted(query_block, key_block, start)
                scores = jnp.where(allowed, scores, NEGATIVE)
            new_top = jnp.maximum(top, jnp.max(scores, axis=0, keepdims=True))
            weights = jnp.exp(scores - new_top)
            if masked:
                weights = jnp.where(allowed, weights, 0.0)
            factor = jnp.exp(top - new_top)
            total = total * factor + jnp.sum(weights, axis=0, keepdims=True)
            mixed = mixed * factor + nn(qkv_ref[2 * HEAD_DIM :, there], weights.astype(jnp.bfloat16))
            return new_top, total, mixed

        top, total, mixed = sweep(
            first_ref,
            query_block,
            key_step,
            (
                jnp.full((1, WIDE), NEGATIVE, jnp.float32),
                jnp.zeros((1, WIDE), jnp.float32),
                jnp.zeros((HEAD_DIM, WIDE), jnp.float32),
            ),
        )
        mixed = mixed / total
        mixed_ref[:, here] = mixed
        total_ref[:, here] = top + jnp.log(total)
        rows = mixed.T
        for part in range(WIDE // 64):
            packed_ref[query_block * (WIDE // 64) + part] = fold(rows[part * 64 : part * 64 + 64]).astype(
                jnp.bfloat16
            )
        return carry

    lax.fori_loop(0, qkv_ref.shape[1] // WIDE, query_step, 0)


def attend(net, first, tokens, weights, cosine, sine, start):
    length = start.shape[1]
    return pl.pallas_call(
        functools.partial(attend_kernel, net),
        out_shape=[
            jax.ShapeDtypeStruct((3 * HEAD_DIM, length), jnp.bfloat16),
            jax.ShapeDtypeStruct((HEAD_DIM, length), jnp.float32),
            jax.ShapeDtypeStruct((1, length), jnp.float32),
            jax.ShapeDtypeStruct((net.count, HALF, 128), jnp.bfloat16),
        ],
        in_specs=[SMEM] + [VMEM] * 5,
        out_specs=[VMEM] * 4,
        scratch_shapes=[pltpu.VMEM((length, HEAD_DIM), jnp.bfloat16)],
        cost_estimate=pl.CostEstimate(flops=2 * 10**9, bytes_accessed=8 * 2**20, transcendentals=2 * 10**6),
        name="attend",
    )(first, tokens, weights, cosine, sine, start)


def attend_back_kernel(net, *refs):
    @pl.when(attends(net.me()))
    def _():
        attend_back_body(*refs)


def attend_back_body(
    first_ref,
    x_ref,
    qkv_ref,
    mixed_ref,
    total_ref,
    cos_ref,
    sin_ref,
    start_ref,
    grad_ref,
    packed_ref,
    weight_ref,
    query_rows,
    key_rows,
    value_rows,
    grad_rows,
    grad_columns,
    correction,
    key_grad,
    value_grad,
    all_grad,
):
    blocks = qkv_ref.shape[1] // BLOCK
    parts = BLOCK // 64

    def prepare(chunk, carry):
        here = columns_of(chunk)
        turned = qkv_ref[:, here].astype(jnp.float32)
        query_rows[here, :] = turned[:HEAD_DIM].T.astype(jnp.bfloat16)
        key_rows[here, :] = turned[HEAD_DIM : 2 * HEAD_DIM].T.astype(jnp.bfloat16)
        value_rows[here, :] = turned[2 * HEAD_DIM :].T.astype(jnp.bfloat16)
        pieces = [unfold(grad_ref[chunk * parts + part].astype(jnp.float32)) for part in range(parts)]
        rows = jnp.concatenate(pieces, axis=0)
        grad_rows[here, :] = rows.astype(jnp.bfloat16)
        across = rows.T
        grad_columns[:, here] = across.astype(jnp.bfloat16)
        correction[:, here] = jnp.sum(across * mixed_ref[:, here], axis=0, keepdims=True)
        key_grad[here, :] = jnp.zeros((BLOCK, HEAD_DIM), jnp.float32)
        value_grad[here, :] = jnp.zeros((BLOCK, HEAD_DIM), jnp.float32)
        return carry

    lax.fori_loop(0, blocks, prepare, 0)

    wide_parts = WIDE // 64

    def query_step(query_block, carry):
        here = wide_columns(query_block)
        query = qkv_ref[:HEAD_DIM, here]
        start = start_ref[:, here]
        total = total_ref[:, here]
        fix = correction[:, here]
        grad = grad_columns[:, here]
        query_in_rows = query_rows[here, :]
        grad_in_rows = grad_rows[here, :]

        def key_step(masked, key_block, query_grad):
            there = columns_of(key_block)
            scores = nn(key_rows[there, :], query)
            weights = jnp.exp(scores - total)
            if masked:
                weights = jnp.where(permitted(query_block, key_block, start), weights, 0.0)
            value_grad[there, :] += nn(weights.astype(jnp.bfloat16), grad_in_rows)
            slope = nn(value_rows[there, :], grad)
            change = (weights * (slope - fix)).astype(jnp.bfloat16)
            key_grad[there, :] += nn(change, query_in_rows)
            return query_grad + nn(qkv_ref[HEAD_DIM : 2 * HEAD_DIM, there], change)

        query_grad = sweep(first_ref, query_block, key_step, jnp.zeros((HEAD_DIM, WIDE), jnp.float32))
        query_grad = rope_rows_back(query_grad * SCALE, cos_ref[:, here], sin_ref[:, here])
        all_grad[:HEAD_DIM, here] = query_grad.astype(jnp.bfloat16)
        rows = query_grad.T.astype(jnp.bfloat16)
        for part in range(wide_parts):
            packed_ref[query_block * wide_parts + part, :64, :HEAD_DIM] = rows[part * 64 : part * 64 + 64]
        return carry

    lax.fori_loop(0, qkv_ref.shape[1] // WIDE, query_step, 0)
    weight_ref[...] = jnp.zeros(weight_ref.shape, jnp.float32)

    def close(chunk, carry):
        here = columns_of(chunk)
        key = rope_rows_back(key_grad[here, :].T, cos_ref[:, here], sin_ref[:, here])
        value = value_grad[here, :]
        all_grad[HEAD_DIM : 2 * HEAD_DIM, here] = key.astype(jnp.bfloat16)
        all_grad[2 * HEAD_DIM :, here] = value.T.astype(jnp.bfloat16)
        rows = key.T.astype(jnp.bfloat16)
        for part in range(parts):
            token = chunk * parts + part
            packed_ref[token, :64, HEAD_DIM:] = rows[part * 64 : part * 64 + 64]
            packed_ref[token, 64:, :] = fold(value[part * 64 : part * 64 + 64]).astype(jnp.bfloat16)
        tokens = x_ref[chunk // 2, chunk % 2].reshape(BLOCK, D)
        weight_ref[...] += nn(all_grad[:, here], tokens)
        return carry

    lax.fori_loop(0, blocks, close, 0)


def attend_back(net, first, tokens, qkv, mixed, total, cosine, sine, start, grad):
    length = start.shape[1]
    rows = pltpu.VMEM((length, HEAD_DIM), jnp.bfloat16)
    sums = pltpu.VMEM((length, HEAD_DIM), jnp.float32)
    return pl.pallas_call(
        functools.partial(attend_back_kernel, net),
        out_shape=[
            jax.ShapeDtypeStruct((net.count, 96, 128), jnp.bfloat16),
            jax.ShapeDtypeStruct((3 * HEAD_DIM, D), jnp.float32),
        ],
        in_specs=[SMEM] + [VMEM] * 8,
        out_specs=[VMEM] * 2,
        scratch_shapes=[
            rows,
            rows,
            rows,
            rows,
            pltpu.VMEM((HEAD_DIM, length), jnp.bfloat16),
            pltpu.VMEM((1, length), jnp.float32),
            sums,
            sums,
            pltpu.VMEM((3 * HEAD_DIM, length), jnp.bfloat16),
        ],
        cost_estimate=pl.CostEstimate(flops=4 * 10**9, bytes_accessed=12 * 2**20, transcendentals=2 * 10**6),
        name="attend_back",
    )(first, tokens, qkv, mixed, total, cosine, sine, start, grad)


def tn(a, b):
    return lax.dot_general(a, b, (((0,), (0,)), ((), ())), preferred_element_type=jnp.float32)


def mean_of(values):
    return jnp.mean(values, axis=-1, keepdims=True)


def layer_norm(values):
    center = values - mean_of(values)
    return center * lax.rsqrt(mean_of(center * center) + EPSILON)


def norm_back(values, gradient):
    center = values - mean_of(values)
    inverse = lax.rsqrt(mean_of(center * center) + EPSILON)
    normed = center * inverse
    return inverse * (gradient - mean_of(gradient) - normed * mean_of(gradient * normed))


def after_kernel(parts_ref, tokens_ref, out_ref, mixed_ref, middle_ref, second_ref):
    for micro in range(2):
        here = slice(64 * micro, 64 * micro + 64)
        for pair in range(HEADS // 2):
            two = [unfold(parts_ref[micro * HEADS + 2 * pair + k].astype(jnp.float32)) for k in range(2)]
            mixed_ref[here, 128 * pair : 128 * pair + 128] = jnp.concatenate(two, axis=1).astype(jnp.bfloat16)
    middle = tokens_ref[...].astype(jnp.float32) + nn(mixed_ref[...], out_ref[...])
    middle_ref[...] = middle
    second_ref[...] = layer_norm(middle).astype(jnp.bfloat16)


def after_attention(parts, tokens, out):
    shape = tokens.shape
    return pl.pallas_call(
        after_kernel,
        out_shape=[
            jax.ShapeDtypeStruct(shape, jnp.bfloat16),
            jax.ShapeDtypeStruct(shape, jnp.float32),
            jax.ShapeDtypeStruct(shape, jnp.bfloat16),
        ],
        in_specs=[VMEM] * 3,
        out_specs=[VMEM] * 3,
        cost_estimate=pl.CostEstimate(flops=2 * 10**8, bytes_accessed=3 * 2**20, transcendentals=0),
        name="after_attention",
    )(parts, tokens, out)


def feed_forward_kernel(net, *refs):
    planes = net.planes
    second_ref, cotangent_ref = refs[:2]
    blocks = refs[2 : 2 + planes]
    second_terms, result_terms = refs[2 + planes : 4 + planes]
    terms = refs[4 + planes : 4 + 2 * planes]
    weights, slopes, products, sums = refs[4 + 2 * planes :]
    plane = net.me() // GROUP
    span = D // planes
    part = FF // GROUP
    for step, block in enumerate(blocks):
        source = (plane + planes - step) % planes
        weights[pl.ds(pl.multiple_of(source * span, span), span), :] = block[...]

    def forward(chunk, carry):
        here = columns_of(chunk)
        second, cotangent = second_ref[here, :], cotangent_ref[here, :]
        both = nn(second, weights[:, : 2 * part])
        gate, up = both[:, :part], both[:, part:]
        sigmoid = jax.nn.sigmoid(gate)
        silu = gate * sigmoid
        product = (silu * up).astype(jnp.bfloat16)
        change = nn(cotangent, weights[:, 2 * part :])
        slopes[here, :part] = (change * up * sigmoid * (1.0 + gate * (1.0 - sigmoid))).astype(jnp.bfloat16)
        slopes[here, part:] = (change * silu).astype(jnp.bfloat16)
        products[here, :] = product
        second_terms[here, :] = nt(slopes[here, :], weights[:, : 2 * part]).astype(jnp.bfloat16)
        result_terms[here, :] = nt(product, weights[:, 2 * part :]).astype(jnp.bfloat16)
        return carry

    lax.fori_loop(0, second_ref.shape[0] // BLOCK, forward, 0)
    for begin in range(0, D, BLOCK):
        here = slice(begin, begin + BLOCK)
        sums[here, : 2 * part] = tn(second_ref[:, here], slopes[...]).astype(jnp.bfloat16)
        sums[here, 2 * part :] = tn(cotangent_ref[:, here], products[...]).astype(jnp.bfloat16)
    for step, term in enumerate(terms):
        target = (plane + step) % planes
        term[...] = sums[pl.ds(pl.multiple_of(target * span, span), span), :]


def feed_forward(net, second, cotangent, blocks):
    tokens = second.shape[0]
    part = FF // GROUP
    low = jnp.bfloat16
    return pl.pallas_call(
        functools.partial(feed_forward_kernel, net),
        out_shape=[jax.ShapeDtypeStruct((tokens, D), low)] * 2
        + [jax.ShapeDtypeStruct((D // net.planes, 3 * part), low)] * net.planes,
        in_specs=[VMEM] * (2 + net.planes),
        out_specs=[VMEM] * (2 + net.planes),
        scratch_shapes=[
            pltpu.VMEM((D, 3 * part), low),
            pltpu.VMEM((tokens, 2 * part), low),
            pltpu.VMEM((tokens, part), low),
            pltpu.VMEM((D, 3 * part), low),
        ],
        cost_estimate=pl.CostEstimate(flops=35 * 10**8, bytes_accessed=10 * 2**20, transcendentals=10**6),
        name="feed_forward",
    )(second, cotangent, *blocks)


def before_kernel(second_grad_ref, middle_ref, cotangent_ref, mixed_ref, out_ref, middle_grad_ref, folded_ref, terms_ref):
    middle_grad = cotangent_ref[...].astype(jnp.float32) + norm_back(middle_ref[...], second_grad_ref[...])
    middle_grad_ref[...] = middle_grad
    low = middle_grad.astype(jnp.bfloat16)
    mixed_grad = nt(low, out_ref[...])
    for micro in range(2):
        rows = mixed_grad[64 * micro : 64 * micro + 64]
        for head in range(HEADS):
            folded_ref[micro * HEADS + head] = fold(rows[:, HEAD_DIM * head : HEAD_DIM * head + HEAD_DIM]).astype(
                jnp.bfloat16
            )
    terms_ref[...] = tn(mixed_ref[...], low).astype(jnp.bfloat16)


def before_attention(second_grad, middle, cotangent, mixed, out):
    return pl.pallas_call(
        before_kernel,
        out_shape=[
            jax.ShapeDtypeStruct(middle.shape, jnp.float32),
            jax.ShapeDtypeStruct((2 * HEADS, HALF, 128), jnp.bfloat16),
            jax.ShapeDtypeStruct((D, D), jnp.bfloat16),
        ],
        in_specs=[VMEM] * 5,
        out_specs=[VMEM] * 3,
        cost_estimate=pl.CostEstimate(flops=4 * 10**8, bytes_accessed=5 * 2**20, transcendentals=0),
        name="before_attention",
    )(second_grad, middle, cotangent, mixed, out)


def input_kernel(grads_ref, weights_ref, tokens_ref, middle_grad_ref, input_ref, query, key, value):
    for micro in range(2):
        here = slice(64 * micro, 64 * micro + 64)
        for pair in range(HEADS // 2):
            head = 2 * pair
            two = [grads_ref[HEADS * micro + head + k].astype(jnp.float32) for k in range(2)]
            there = slice(128 * pair, 128 * pair + 128)
            query[here, there] = jnp.concatenate([t[:64, :HEAD_DIM] for t in two], axis=1).astype(jnp.bfloat16)
            key[here, there] = jnp.concatenate([t[:64, HEAD_DIM:] for t in two], axis=1).astype(jnp.bfloat16)
            value[here, there] = jnp.concatenate([unfold(t[64:96]) for t in two], axis=1).astype(jnp.bfloat16)
    gradient = (
        nt(query[...], weights_ref[0]) + nt(key[...], weights_ref[1]) + nt(value[...], weights_ref[2])
    )
    input_ref[...] = middle_grad_ref[...] + norm_back(tokens_ref[...].astype(jnp.float32), gradient)


def input_gradient(grads, weights, tokens, middle_grad):
    rows = pltpu.VMEM(tokens.shape, jnp.bfloat16)
    return pl.pallas_call(
        input_kernel,
        out_shape=jax.ShapeDtypeStruct(tokens.shape, jnp.float32),
        in_specs=[VMEM] * 4,
        out_specs=VMEM,
        scratch_shapes=[rows] * 3,
        cost_estimate=pl.CostEstimate(flops=5 * 10**8, bytes_accessed=6 * 2**20, transcendentals=0),
        name="input_gradient",
    )(grads, weights, tokens, middle_grad)


def solve_heads(me, head_ref, moment_ref, target, scratch):
    wide, semaphore, parts, moment = scratch[0], scratch[3], scratch[4], scratch[5]

    @pl.when(jnp.logical_or(me == OWNERS[0], jnp.logical_or(me == OWNERS[1], me == OWNERS[2])))
    def _():
        move(head_ref, parts, semaphore)
        move(moment_ref, moment, semaphore)

        def join(pair, carry):
            first = parts[2 * pair].astype(jnp.float32) + parts[HEADS + 2 * pair].astype(jnp.float32)
            second = parts[2 * pair + 1].astype(jnp.float32) + parts[HEADS + 2 * pair + 1].astype(jnp.float32)
            here = pl.ds(pl.multiple_of(pair * 128, 128), 128)
            gradient = jnp.concatenate([first, second], axis=0).T
            wide[:, here] = (0.75 * gradient + 0.25 * moment[:, here].astype(jnp.float32)).astype(jnp.bfloat16)
            return carry

        lax.fori_loop(0, HEADS // 2, join, 0)
        solve(D, target, scratch)


def solve_late(me, out_ref, ffn_ref, out_target, ffn_target, scratch):
    wide, semaphore = scratch[0], scratch[3]

    @pl.when(me == OWNERS[3])
    def _():
        move(out_ref, wide.at[:, pl.ds(0, D)], semaphore)
        solve(D, out_target, scratch)

    @pl.when(jnp.logical_or(me == OWNERS[4], jnp.logical_or(me == OWNERS[5], me == OWNERS[6])))
    def _():
        move(ffn_ref, wide, semaphore)
        solve(FF, ffn_target, scratch)


def move(source, target, semaphore):
    copy = pltpu.make_async_copy(source, target, semaphore)
    copy.start()
    copy.wait()


def solve(span, target, scratch):
    wide, gram, polynomial, semaphore = scratch[:4]

    def blocks_of(index):
        return pl.ds(pl.multiple_of(index * BLOCK, BLOCK), BLOCK)

    def mirror(target, i, j, block):
        target[i * BLOCK : (i + 1) * BLOCK, j * BLOCK : (j + 1) * BLOCK] = block.astype(jnp.bfloat16)
        if i != j:
            target[j * BLOCK : (j + 1) * BLOCK, i * BLOCK : (i + 1) * BLOCK] = block.T.astype(jnp.bfloat16)

    chunks = span // BLOCK

    def measure(index, total):
        values = wide[:, blocks_of(index)].astype(jnp.float32)
        return total + jnp.sum(values * values, axis=0, keepdims=True)

    total = lax.fori_loop(0, chunks, measure, jnp.zeros((1, BLOCK), jnp.float32))
    frobenius = jnp.sqrt(jnp.sum(total, axis=1, keepdims=True)) + 1e-07

    def scale(index, carry):
        here = blocks_of(index)
        wide[:, here] = (wide[:, here].astype(jnp.float32) / frobenius).astype(jnp.bfloat16)
        return carry

    lax.fori_loop(0, chunks, scale, 0)

    def step(_, carry):
        for i in range(D // BLOCK):
            for j in range(i + 1):
                mirror(
                    gram,
                    i,
                    j,
                    nt(
                        wide[i * BLOCK : (i + 1) * BLOCK, :span],
                        wide[j * BLOCK : (j + 1) * BLOCK, :span],
                    ),
                )
        for i in range(D // BLOCK):
            for j in range(i + 1):
                square = nn(gram[i * BLOCK : (i + 1) * BLOCK, :], gram[:, j * BLOCK : (j + 1) * BLOCK])
                linear = gram[i * BLOCK : (i + 1) * BLOCK, j * BLOCK : (j + 1) * BLOCK].astype(jnp.float32)
                mirror(polynomial, i, j, COEFF_B * linear + COEFF_C * square)

        def advance(index, inner):
            here = blocks_of(index)
            old = wide[:, here]
            wide[:, here] = (COEFF_A * old.astype(jnp.float32) + nn(polynomial[...], old)).astype(jnp.bfloat16)
            return inner

        lax.fori_loop(0, chunks, advance, 0)
        return carry

    lax.fori_loop(0, NS_STEPS, step, 0)
    move(wide.at[:, pl.ds(0, span)], target, semaphore)


def solve_scratch(span, heads):
    square = pltpu.VMEM((D, D), jnp.bfloat16)
    shapes = [pltpu.VMEM((D, span), jnp.bfloat16), square, square, pltpu.SemaphoreType.DMA]
    if heads:
        shapes += [pltpu.VMEM((2 * HEADS, HEAD_DIM, D), jnp.bfloat16), square]
    return shapes


SQUARE = jax.ShapeDtypeStruct((D, D), jnp.bfloat16)
SOLVE_COST = pl.CostEstimate(flops=25 * 10**9, bytes_accessed=8 * 2**20, transcendentals=0)


def newton_kernel(net, head_ref, moment_ref, out_ref, ffn_ref, attn_target, ffn_target, *scratch):
    me = net.me()
    solve_heads(me, head_ref, moment_ref, attn_target, scratch)
    solve_late(me, out_ref, ffn_ref, attn_target, ffn_target, scratch)


def newton(net, *sources):
    return pl.pallas_call(
        functools.partial(newton_kernel, net),
        out_shape=[SQUARE, jax.ShapeDtypeStruct((D, FF), jnp.bfloat16)],
        in_specs=[ANY] * 4,
        out_specs=[ANY] * 2,
        scratch_shapes=solve_scratch(FF, True),
        cost_estimate=SOLVE_COST,
        name="newton",
    )(*sources)


def on_device(net, tokens, doc_ids, cotangent, attn_weight, ffn_weight, attn_moment, ffn_moment):
    micro_count, token_count, width = tokens.shape
    rows = attn_weight.shape[1]
    count, planes = net.count, net.planes
    length = count * token_count
    me = net.me()
    plane, place = me // GROUP, me % GROUP
    x_bit = place // 4
    both = micro_count * token_count
    part = FF // GROUP
    low = jnp.bfloat16
    everything = (slice(None),)

    attn_low = attn_weight.astype(low)
    ffn_low = ffn_weight.astype(low)

    def cut_up(values):
        return values.reshape(3, rows, GROUP, part).transpose(2, 1, 0, 3).reshape(GROUP, rows, 3 * part)

    cut = cut_up(ffn_low)
    out_grad = cotangent.reshape(both, width)
    hidden = tokens.astype(jnp.float32).reshape(both, width)
    normed = layer_norm(hidden).astype(low)
    counts = jnp.sum((doc_ids[:, :, None] == jnp.arange(DOCS)[None, None, :]).astype(jnp.float32), axis=1)
    tail = jnp.pad(counts.reshape(-1).astype(low), (0, HEAD_DIM - micro_count * DOCS))
    columns = attn_low[:3].reshape(3, rows, HEADS, HEAD_DIM).transpose(2, 1, 0, 3).reshape(HEADS, rows, 3 * HEAD_DIM)
    columns = jnp.concatenate([columns, jnp.broadcast_to(tail, (HEADS, rows, HEAD_DIM))], axis=2)
    moment_low = attn_moment.astype(low)
    all_tokens, all_columns, plane_cut, plane_out, moment_plane, moment_out = gather_tokens(
        net,
        0,
        normed.reshape(micro_count, token_count, width),
        columns,
        [
            Flow(0, 0, lambda i, j: j % GROUP, lambda i, j: i % GROUP, size=GROUP),
            Across(net, 1, 1, lambda i, j: 0, lambda i, j: i // GROUP),
            Across(net, 3, 3, lambda i, j: 0, lambda i, j: i // GROUP, lambda i, j: j // GROUP == SPARE),
        ]
        + [Flow(2, 2, lambda i, j: j % GROUP, lambda i, j: i % GROUP, size=GROUP)],
        [cut, attn_low[3:], cut_up(ffn_moment.astype(low)), moment_low[3:]],
        [
            jax.ShapeDtypeStruct(cut.shape, low),
            jax.ShapeDtypeStruct((planes, rows, D), low),
            jax.ShapeDtypeStruct(cut.shape, low),
            jax.ShapeDtypeStruct((planes, rows, D), low),
        ],
    )
    late_own = plane_cut.reshape(GROUP * rows, 3 * part)
    late_blocks = [late_own] + [net.shift(late_own, step) for step in range(1, planes)]

    head_weights = all_columns[:, :, : 3 * HEAD_DIM].reshape(D, 3 * HEAD_DIM).T
    every_count = jnp.sum(all_columns[:, 0, 3 * HEAD_DIM :].astype(jnp.float32), axis=0)
    own_count = lax.dynamic_slice_in_dim(every_count, x_bit * DOCS, DOCS, 0)
    starts = jnp.cumsum(own_count) - own_count
    index = jnp.arange(length).astype(jnp.float32)
    start = jnp.max(jnp.where(starts[:, None] <= index[None, :], starts[:, None], 0.0), axis=0)
    inverse = 10000.0 ** (-(jnp.arange(HALF, dtype=jnp.float32) * 2.0) / HEAD_DIM)
    angles = inverse[:, None] * (index - start)[None, :]
    cosine, sine = jnp.cos(angles), jnp.sin(angles)
    start = start.astype(jnp.int32)
    diagonal = jnp.arange(length // WIDE, dtype=jnp.int32) * (WIDE // BLOCK)
    first = jnp.clip(start[::WIDE] // BLOCK, 0, diagonal)
    first = jnp.stack([first, jnp.clip((start[WIDE - 1 :: WIDE] + BLOCK - 1) // BLOCK, first, diagonal)])
    start = start[None, :]

    qkv, mixed, total, packed = attend(net, first, all_tokens, head_weights, cosine, sine, start)
    mixed_parts, moment_whole, plane_out_grad, out_full = exchange(
        net,
        "mixed_exchange",
        1,
        [PlaneGather(2, 2), PlaneGather(3, 3, lambda i: everything + (i % GROUP,))]
        + [Flow(0, 0, lambda i, j: j, lambda i, j: combo_of(i), lambda i, j: attends(i))]
        + [FanIn(1, 1, OWNERS[k], lambda i, j, k=k: k, lambda i, j: i) for k in range(3)],
        [packed, moment_low, out_grad, plane_out],
        [
            jax.ShapeDtypeStruct((2 * HEADS, HALF, 128), low),
            jax.ShapeDtypeStruct((count, rows, D), low),
            jax.ShapeDtypeStruct((GROUP, both, width), low),
            jax.ShapeDtypeStruct((planes, GROUP, rows, D), low),
        ],
    )
    plane_out_grad = plane_out_grad.reshape(GROUP * both, width)
    out_full = out_full.reshape(D, D)
    own_tokens = tokens.reshape(both, width)
    mixed_tokens, middle, second = after_attention(mixed_parts, own_tokens, out_full)
    (plane_second,) = exchange(
        net,
        "second_exchange",
        10,
        [PlaneGather(0, 0)],
        [second],
        [jax.ShapeDtypeStruct((GROUP, both, width), low)],
        GROUP,
    )
    plane_second = plane_second.reshape(GROUP * both, width)
    second_terms, result_terms, *ffn_terms = feed_forward(net, plane_second, plane_out_grad, late_blocks)
    sides = (2, 2, 2, both, width)
    (second_grad,) = exchange(
        net,
        "second_grad_exchange",
        8,
        [PlaneScatter(0, 0, (both, width))],
        [second_terms.reshape(sides)],
        [jax.ShapeDtypeStruct((both, width), jnp.float32)],
        GROUP,
    )
    ffn_block = ffn_terms[0].astype(jnp.float32)
    for step in range(1, planes):
        ffn_block = ffn_block + net.shift(ffn_terms[step], step).astype(jnp.float32)
    ffn_update = 0.75 * ffn_block + 0.25 * moment_plane.reshape(GROUP * rows, 3 * part).astype(jnp.float32)
    ffn_update, ffn_block = ffn_update.astype(low), ffn_block.astype(low)
    middle_grad, folded, out_terms = before_attention(second_grad, middle, out_grad, mixed_tokens, out_full)
    grad_parts, out_total, ffn_whole = exchange(
        net,
        "mixed_grad_exchange",
        2,
        [
            PlaneScatter(1, 1, (rows, D), (planes,), gathers=True),
            Flow(0, 0, lambda i, j: combo_of(j), lambda i, j: i, lambda i, j: attends(j)),
        ]
        + [
            FanIn(
                2,
                2,
                OWNERS[4 + k],
                lambda i, j, k=k: (slice(None), pl.ds(part * k, part)),
                lambda i, j: (i // GROUP, slice(None), pl.ds(pl.multiple_of(part * (i % GROUP), part), part)),
            )
            for k in range(3)
        ],
        [folded, out_terms.reshape(planes, 2, 2, 2, rows, D), ffn_update],
        [
            jax.ShapeDtypeStruct((count, HALF, 128), low),
            jax.ShapeDtypeStruct((planes, rows, D), jnp.float32),
            jax.ShapeDtypeStruct((planes, GROUP * rows, FF), low),
        ],
    )
    out_update = (0.75 * out_total + 0.25 * moment_out.astype(jnp.float32)).astype(low)

    early_low, grad_parts = lax.optimization_barrier((attn_low[:3], grad_parts))
    attn_full = lax.all_gather(early_low, ("blk", "head"), axis=1, tiled=True)
    grad_packed, head_grad = attend_back(
        net, first, all_tokens, qkv, mixed, total, cosine, sine, start, grad_parts
    )
    head_low = head_grad.astype(low)
    out_update, grad_packed, head_low = lax.optimization_barrier((out_update, grad_packed, head_low))
    (out_whole,) = exchange(
        net,
        "out_exchange",
        4,
        [
            FanIn(
                0,
                0,
                OWNERS[3] % GROUP,
                lambda i, j: everything,
                lambda i, j: everything + (i % GROUP,),
                lambda i, j: j == OWNERS[3],
            )
        ],
        [out_update],
        [jax.ShapeDtypeStruct((planes, GROUP, rows, D), low)],
        GROUP,
    )
    out_whole, grad_packed, head_low = lax.optimization_barrier((out_whole, grad_packed, head_low))
    (head_whole,) = exchange(
        net,
        "head_exchange",
        9,
        [
            FanIn(0, 0, OWNERS[k], lambda i, j, k=k: k, lambda i, j: combo_of(i), lambda i, j: attends(i))
            for k in range(3)
        ],
        [head_low.reshape(3, HEAD_DIM, D)],
        [jax.ShapeDtypeStruct((2 * HEADS, HEAD_DIM, D), low)],
        meet=net.meet_heads,
    )
    grad_packed, head_low, head_whole = lax.optimization_barrier((grad_packed, head_low, head_whole))
    head_rows = jnp.pad(head_low.T.reshape(count, rows, 3 * HEAD_DIM), ((0, 0), (0, 0), (0, 64)))
    outgoing = jnp.concatenate([grad_packed, head_rows.reshape(count, rows * 2, 128)], axis=1)
    ffn_rows, result_sides = ffn_block.reshape(GROUP, rows, 3 * part), result_terms.reshape(sides)
    last = [
        jax.ShapeDtypeStruct((2 * HEADS, 96 + 2 * rows, 128), low),
        jax.ShapeDtypeStruct((GROUP, rows, 3 * part), low),
        jax.ShapeDtypeStruct((both, width), jnp.float32),
    ]

    def last_flows(base, runs):
        return [
            PlaneScatter(base + 2, base + 2, (both, width), runs=runs),
            Flow(
                base,
                base,
                lambda i, j: j,
                lambda i, j: combo_of(i),
                lambda i, j: jnp.logical_and(attends(i), runs(j)),
            ),
            Flow(
                base + 1,
                base + 1,
                lambda i, j: j % GROUP,
                lambda i, j: i % GROUP,
                lambda i, j: runs(i),
                size=GROUP,
            ),
        ]

    early_last = exchange(
        net,
        "attending_exchange",
        7,
        last_flows(0, attends),
        [outgoing, ffn_rows, result_sides],
        last,
        meet=net.meet_attending,
    )
    attn_done, ffn_done = newton(
        net, head_whole, moment_whole.reshape(D, D), out_whole.reshape(D, D), ffn_whole.reshape(D, FF)
    )
    attn_done, ffn_done, outgoing, *early_last = lax.optimization_barrier(
        (attn_done, ffn_done, outgoing, *early_last)
    )
    attn_step, ffn_step, out_row_grad, *late_last = exchange(
        net,
        "step_exchange",
        5,
        [FanOut(1, 1, OWNERS[4 + k], lambda i, j: j, lambda i, j, k=k: k) for k in range(3)]
        + [FanOut(0, 0, OWNERS[k], lambda i, j: j, lambda i, j, k=k: k) for k in range(4)]
        + [Across(net, 2, 2, lambda i, j: j // GROUP, lambda i, j: 0, lambda i, j: i // GROUP == SPARE)]
        + last_flows(3, lambda i: jnp.logical_not(attends(i))),
        [
            attn_done.reshape(count, rows, D),
            ffn_done.reshape(count, rows, FF),
            out_total.astype(low),
            outgoing,
            ffn_rows,
            result_sides,
        ],
        [
            jax.ShapeDtypeStruct((4, rows, D), low),
            jax.ShapeDtypeStruct((3, rows, FF), low),
            jax.ShapeDtypeStruct((1, rows, D), low),
        ]
        + last,
    )
    grads, ffn_parts, result = (jnp.where(attends(me), a, b) for a, b in zip(early_last, late_last))
    ffn_grad = ffn_parts.reshape(GROUP, rows, 3, part).transpose(2, 1, 0, 3).reshape(3, rows, FF).astype(jnp.float32)
    ffn_moment_new = 0.5 * ffn_moment + 0.5 * ffn_grad

    input_grad = input_gradient(grads, attn_full, own_tokens, middle_grad)
    row_grads = grads[:, 96:].reshape(micro_count, HEADS, rows, 256).astype(jnp.float32)
    summed = jnp.sum(row_grads, axis=0)
    early_grad = summed[:, :, : 3 * HEAD_DIM].reshape(HEADS, rows, 3, HEAD_DIM).transpose(2, 1, 0, 3).reshape(3, rows, D)
    attn_grad = jnp.concatenate([early_grad, out_row_grad.astype(jnp.float32)], axis=0)
    attn_moment_new = 0.5 * attn_moment + 0.5 * attn_grad

    output = (middle + result).astype(low)

    rates = jnp.asarray(RATES, jnp.float32)[:, None, None]
    attn_master = attn_weight - rates[:4] * attn_step.astype(jnp.float32)
    ffn_master = ffn_weight - rates[4:] * ffn_step.astype(jnp.float32)
    shape = (micro_count, token_count, width)
    return (
        output.reshape(shape),
        input_grad.reshape(shape),
        attn_grad,
        ffn_grad,
        attn_master,
        ffn_master,
        attn_moment_new,
        ffn_moment_new,
        attn_master.astype(low),
        ffn_master.astype(low),
    )


def solution(mesh):
    wide = P(None, ("blk", "head"), None)
    return jax.shard_map(
        functools.partial(on_device, Net(mesh)),
        mesh=mesh,
        in_specs=(wide, P(None, ("blk", "head")), wide, wide, wide, wide, wide),
        out_specs=(wide,) * 10,
        check_vma=False,
    )
```

time: 372 us -> 357 us (0.960)
  Pallas kernels: 243 us -> 293 us
  matrix products: 18.1 us -> 0 us
  local copies, waits for them, and re-layouts: 30.1 us -> 14.2 us
  starting transfers between devices: 24.8 us -> 11 us
  waiting for transfers between devices: 12 us -> 4.51 us
  other arithmetic: 26 us -> 19.1 us
    pallas_call x7 -> x8, Pallas kernels: 161 us -> 190 us  [exchange(): pl.pallas_call(functools.partial(exchange_kernel, net, meet or (lambda me...]
    pallas_call x2 -> x6, Pallas kernels: 75.2 us -> 95.9 us  [the longest x1 38 us: gather_tokens(): pl.pallas_call(functools.partial(gather_kernel, net, flows, len(extras)),...]
    dot_general x15 -> x0, matrix products: 18.1 us -> none  [the longest x7 13.3 us: nt(): lax.dot_general(a, b, (((1,), (1,)), ((), ())), preferred_element_type=jn...]
    ppermute x12 -> x6, starting transfers between devices: 24.8 us -> 11 us  [permute(): lax.ppermute(values, ('head', 'blk'), [(place(i), place(j)) for i, j in p...]
    reshape x19 -> x5, local copies, waits for them, and re-layouts: 10.3 us -> 2.75 us  [the longest x4 2.61 us: cut_up(): values.reshape(3, rows, GROUP, part).transpose(2, 1, 0, 3)]
    ppermute x12 -> x6, waiting for transfers between devices: 11.9 us -> 4.49 us  [permute(): lax.ppermute(values, ('head', 'blk'), [(place(i), place(j)) for i, j in p...]
  transfers between devices with their start and end apart: 13 -> 7, of which waited for: 2 -> 1; matrix products, arithmetic and copies ran while one was open for 11% -> 5% of each run, Pallas kernels for 49% -> 58%
where the time goes in v1:
time: 357 us; the launch traced here: 356 us
  Pallas kernels  293 us (82%)
  other arithmetic  19.1 us (5%)
  between operations  14.7 us (4%)
  local copies, waits for them, and re-layouts  14.2 us (4%)
  starting transfers between devices  11 us (3%)
  waiting for transfers between devices  4.51 us (1%)
    pallas_call x8, Pallas kernels, exchange(): pl.pallas_call(functools.partial(exchange_kernel, net, meet or (lambda me...  190 us
    pallas_call x1, Pallas kernels, gather_tokens(): pl.pallas_call(functools.partial(gather_kernel, net, flows, len(extras)),...  38 us
    pallas_call x1, Pallas kernels, newton(): pl.pallas_call(functools.partial(newton_kernel, net), out_shape=[SQUARE,...  37.6 us
    ppermute x6, starting transfers between devices, permute(): lax.ppermute(values, ('head', 'blk'), [(place(i), place(j)) for i, j in p...  11 us
    pallas_call x1, Pallas kernels, feed_forward(): pl.pallas_call(functools.partial(feed_forward_kernel, net), out_shape=[ja...  9.09 us
  transfers between devices with their start and end apart: 7, of which 1 were waited for; matrix products, arithmetic and copies ran while one was open for 5% of the time, Pallas kernels for 58%

profile of v1, /device:TPU:18, one launch (start us, length us, event | category | flops | bytes accessed | tf_op | source)
XLA Modules:
  0.0 356.4 jit_solution(3887317042361422139)
XLA Ops:
  17.1 38.0 %gather_tokens.1 = (bf16[4,2,4,64,768]{4,3,2,1,0:T(8,128)(2,1)}, bf16[32,24,256]{2,1,0:T(8,128)(2,1)}, bf16[8,24,768]{2,1,0:T(8,128)(2,1)}, bf16[4,24,768]{2,1,0...) custom-call(bf16[2,64,768]{2,1,0:T(8,128)(2,1)} %fusion.4.x_ref, ...), custom_call_target="tpu_custom_call" | custom-call | bytes 104857600 | tf_op jit(solution)/shard_map/gather_tokens/pallas_call | solution.py:678
  55.1 6.0 %collective-permute-start = (bf16[192,768]{1,0:T(8,128)(2,1)}, bf16[192,768]{1,0:T(8,128)(2,1)S(1)}, u32[]{:S(2)}, u32[]{:S(2)}) collective-permute-start(bf16[192,768]{1,0:T(8,128)(2,1)} %bitcast.94), channel_id=1, source_target_pairs={{0,4},{16,20},{1,5},{17,21},{2,6},{18,22},{3,7},{19,23},{4,8},{20,... | collective-permute-start | bytes 884744 | tf_op jit(solution)/shard_map/ppermute | solution.py:73
  61.4 2.7 collective-permute-start.2
  65.7 1.9 copy.40
  67.6 1.8 multiply_sine_fusion
  69.9 3.2 attend.1
  73.2 44.5 %mixed_exchange.1 = (bf16[24,32,128]{2,1,0:T(8,128)(2,1)}, bf16[32,24,768]{2,1,0:T(8,128)(2,1)}, bf16[8,128,768]{2,1,0:T(8,128)(2,1)}, bf16[4,8,24,768]{3,2,1,0:T(8,128)(2,1)}) custom-call(bf16[32,32,128]{2,1,0:T(8,128)(2,1)} %get-tuple-element.71.refs_0_, bf16[4,24,768]{2,1,0:T(8,128)(2,1)} %copy-done.13, bf16[128,768]{1,0:T(8,128)(2,1)} %bitcast.82, ...), custom_call_target="tpu_custom_call" | custom-call | bytes 33030144 | tf_op jit(solution)/shard_map/mixed_exchange/pallas_call | solution.py:518
  117.7 2.8 after_attention.1
  120.5 14.5 %second_exchange.1 = bf16[8,128,768]{2,1,0:T(8,128)(2,1)} custom-call(bf16[128,768]{1,0:T(8,128)(2,1)} %get-tuple-element.76.refs_0_), custom_call_target="tpu_custom_call" | custom-call | bytes 12582912 | tf_op jit(solution)/shard_map/second_exchange/pallas_call | solution.py:518
  136.0 9.1 %feed_forward.1 = (bf16[1024,768]{1,0:T(8,128)(2,1)}, bf16[1024,768]{1,0:T(8,128)(2,1)}, bf16[192,768]{1,0:T(8,128)(2,1)}, bf16[192,768]{1,0:T(8,128)(2,1)}, bf1...) custom-call(bf16[1024,768]{1,0:T(8,128)(2,1)} %bitcast.68, bf16[1024,768]{1,0:T(8,128)(2,1)} %bitcast.92, ...), custom_call_target="tpu_custom_call" | custom-call | flops 3500000000 | bytes 10485760 | tf_op jit(solution)/shard_map/feed_forward/pallas_call | solution.py:1046
  145.1 2.0 collective-permute-start.3
  147.1 16.0 %second_grad_exchange.1.second_grad_ref = f32[128,768]{1,0:T(8,128)} custom-call(bf16[2,2,2,128,768]{4,3,2,1,0:T(8,128)(2,1)} %bitcast.69), custom_call_target="tpu_custom_call" | custom-call | bytes 3145728 | tf_op jit(solution)/shard_map/second_grad_exchange/pallas_call | solution.py:518
  163.1 3.8 %before_attention.1 = (f32[128,768]{1,0:T(8,128)}, bf16[24,32,128]{2,1,0:T(8,128)(2,1)}, bf16[768,768]{1,0:T(8,128)(2,1)}) custom-call(f32[128,768]{1,0:T(8,128)} %second_grad_exchange.1.second_grad_ref, f32[128,768]{1,0:T(8,128)} %get-tuple-element.75.middle_ref, bf16[128,768]{1,0:T(8,128)(2,1)} %bitcast.83, bf16[128,768]{1,0:T(8,128)(2,1)} %get-tuple-element.80.mixed_ref, ...), custom_call_target="tpu_custom_call" | custom-call | flops 400000000 | bytes 5242880 | tf_op jit(solution)/shard_map/before_attention/pallas_call | solution.py:1078
  166.9 4.5 %collective-permute-done.4 = bf16[192,768]{1,0:T(8,128)(2,1)S(1)} collective-permute-done((bf16[192,768]{1,0:T(8,128)(2,1)}, bf16[192,768]{1,0:T(8,128)(2,1)S(1)}, u32[]{:S(2)}, u32[]{:S(2)}) %collective-permute-start.4) | collective-permute-done | bytes 294944 | tf_op jit(solution)/shard_map/ppermute | solution.py:73
  172.4 34.9 %mixed_grad_exchange.1 = (bf16[32,32,128]{2,1,0:T(8,128)(2,1)}, f32[4,24,768]{2,1,0:T(8,128)}, bf16[4,192,2048]{2,1,0:T(8,128)(2,1)}) custom-call(bf16[24,32,128]{2,1,0:T(8,128)(2,1)} %get-tuple-element.81.refs_0_, bf16[4,2,2,2,24,768]{5,4,3,2,1,0:T(8,128)(2,1)} %bitcast.75, bf16[192,768]{1,0:T(8,128)(2,1)} %get-tuple-element.137.refs_2_), custom_call_target="tpu_custom_call" | custom-call | bytes 29622272 | tf_op jit(solution)/shard_map/mixed_grad_exchange/pallas_call | solution.py:518
  207.4 3.6 %attend_back.1 = (bf16[32,96,128]{2,1,0:T(8,128)(2,1)}, f32[192,768]{1,0:T(8,128)}) custom-call(s32[2,4]{1,0:T(2,128)} %pad_add_fusion.refs_0_, bf16[4,2,4,64,768]{4,3,2,1,0:T(8,128)(2,1)} %get-tuple-element.70.refs_1_, bf16[192,2048]{1,0:T(8,128)(2,1)} %get-tuple-element.90.refs_2_, f32[64,2048]{1,0:T(8,128)} %get-tuple-element.91.refs_3_, ...), custom_call_target="tpu_custom_call" | custom-call | flops 4000000000 | bytes 12582912 | tf_op jit(solution)/shard_map/attend_back/pallas_call | solution.py:931
  211.1 1.8 convert_element_type.152
  213.6 12.4 %out_exchange.1 = bf16[4,8,24,768]{3,2,1,0:T(8,128)(2,1)} custom-call(bf16[4,24,768]{2,1,0:T(8,128)(2,1)} %get-tuple-element.97.refs_0_), custom_call_target="tpu_custom_call" | custom-call | bytes 9437184 | tf_op jit(solution)/shard_map/out_exchange/pallas_call | solution.py:518
  226.1 1.9 head_exchange.1.head_ref
  230.7 4.3 %attending_exchange.1 = (bf16[24,144,128]{2,1,0:T(8,128)(2,1)}, bf16[8,24,768]{2,1,0:T(8,128)(2,1)}, f32[128,768]{1,0:T(8,128)}) custom-call(bf16[32,144,128]{2,1,0:T(8,128)(2,1)} %copy-done, bf16[8,24,768]{2,1,0:T(8,128)(2,1)} %bitcast.63, bf16[2,2,2,128,768]{4,3,2,1,0:T(8,128)(2,1)} %bitcast.55), custom_call_target="tpu_custom_call" | custom-call | bytes 12582912 | tf_op jit(solution)/shard_map/attending_exchange/pallas_call | solution.py:518
  235.0 37.6 %newton.1 = (bf16[768,768]{1,0:T(8,128)(2,1)}, bf16[768,2048]{1,0:T(8,128)(2,1)}) custom-call(bf16[24,64,768]{2,1,0:T(8,128)(2,1)} %head_exchange.1.head_ref, bf16[768,768]{1,0:T(8,128)(2,1)} %bitcast.93, bf16[768,768]{1,0:T(8,128)(2,1)} %bitcast.79, bf16[768,2048]{1,0:T(8,128)(2,1)} %bitcast.91), custom_call_target="tpu_custom_call" | custom-call | flops 24999999488 | bytes 8388608 | tf_op jit(solution)/shard_map/newton/pallas_call | solution.py:1238
  272.7 61.5 %step_exchange.1 = (bf16[4,24,768]{2,1,0:T(8,128)(2,1)}, bf16[3,24,2048]{2,1,0:T(8,128)(2,1)}, bf16[1,24,768]{2,1,0:T(8,128)(2,1)}, bf16[24,144,128]{2,1,0:T(8,1...) custom-call(bf16[32,24,768]{2,1,0:T(8,128)(2,1)} %bitcast.73, bf16[32,24,2048]{2,1,0:T(8,128)(2,1)} %bitcast.61, ...), custom_call_target="tpu_custom_call" | custom-call | bytes 16416768 | tf_op jit(solution)/shard_map/step_exchange/pallas_call | solution.py:518
  340.8 1.7 add_convert_fusion
  344.9 4.6 %input_gradient.1 = f32[128,768]{1,0:T(8,128)} custom-call(bf16[24,144,128]{2,1,0:T(8,128)(2,1)} %copy-done.2, bf16[3,768,768]{2,1,0:T(8,128)(2,1)} %all-gather.2.cloned.1.call-done.weights_ref, bf16[128,768]{1,0:T(8,128)(2,1)} %bitcast.58, f32[128,768]{1,0:T(8,128)} %get-tuple-element.122.middle_grad_ref), custom_call_target="tpu_custom_call" | custom-call | flops 500000000 | bytes 6291456 | tf_op jit(solution)/shard_map/input_gradient/pallas_call | solution.py:1110
  (130 shorter events, 26.4 us)
Async XLA Ops:
  7.2 3.9 %copy-start.1 = (bf16[2,64,768]{2,1,0:T(8,128)(2,1)S(1)}, bf16[2,64,768]{2,1,0:T(8,128)(2,1)}, u32[]{:S(2)}) copy-start(bf16[2,64,768]{2,1,0:T(8,128)(2,1)} %param.8) | copy-start | bytes 589828
  7.2 337.7 %all-gather.2.cloned.1.call-start = ((), (), s32[]{:S(2)}) async-start(), calls=%async_computation | async-start | bytes 3649536 | tf_op jit(solution)/shard_map/all_gather | solution.py:1389
  8.3 4.6 %copy-start.10 = (bf16[3,24,768]{2,1,0:T(8,128)(2,1)}, bf16[3,24,768]{2,1,0:T(8,128)(2,1)S(1)}, u32[]{:S(2)}) copy-start(bf16[3,24,768]{2,1,0:T(8,128)(2,1)S(1)} %slice.47) | copy-start | bytes 331780
  8.3 4.3 %copy-start.29 = (s32[2,64]{1,0:T(2,128)S(1)}, s32[2,64]{1,0:T(2,128)}, u32[]{:S(2)}) copy-start(s32[2,64]{1,0:T(2,128)} %param.9) | copy-start | bytes 1540
  8.3 4.5 %copy-start.4 = (f32[3,24,2048]{2,1,0:T(8,128)S(1)}, f32[3,24,2048]{2,1,0:T(8,128)}, u32[]{:S(2)}) copy-start(f32[3,24,2048]{2,1,0:T(8,128)} %param.12) | copy-start | bytes 1769476
  15.7 53.7 %copy-start.13 = (bf16[4,24,768]{2,1,0:T(8,128)(2,1)}, bf16[4,24,768]{2,1,0:T(8,128)(2,1)S(1)}, u32[]{:S(2)}) copy-start(bf16[4,24,768]{2,1,0:T(8,128)(2,1)S(1)} %convert_element_type.139.refs_1_) | copy-start | bytes 442372
  55.1 80.0 %collective-permute-start = (bf16[192,768]{1,0:T(8,128)(2,1)}, bf16[192,768]{1,0:T(8,128)(2,1)S(1)}, u32[]{:S(2)}, u32[]{:S(2)}) collective-permute-start(bf16[192,768]{1,0:T(8,128)(2,1)} %bitcast.94), channel_id=1, source_target_pairs={{0,4},{16,20},{1,5},{17,21},{2,6},{18,22},{3,7},{19,23},{4,8},{20,... | collective-permute-start | bytes 884744 | tf_op jit(solution)/shard_map/ppermute | solution.py:73
  61.0 74.0 %collective-permute-start.1 = (bf16[192,768]{1,0:T(8,128)(2,1)}, bf16[192,768]{1,0:T(8,128)(2,1)S(1)}, u32[]{:S(2)}, u32[]{:S(2)}) collective-permute-start(bf16[192,768]{1,0:T(8,128)(2,1)} %bitcast.95), channel_id=1, source_target_pairs={{0,8},{16,24},{1,9},{17,25},{2,10},{18,26},{3,11},{19,27},{4,12},{... | collective-permute-start | bytes 884744 | tf_op jit(solution)/shard_map/ppermute | solution.py:73
  61.4 73.7 %collective-permute-start.2 = (bf16[192,768]{1,0:T(8,128)(2,1)}, bf16[192,768]{1,0:T(8,128)(2,1)S(1)}, u32[]{:S(2)}, u32[]{:S(2)}) collective-permute-start(bf16[192,768]{1,0:T(8,128)(2,1)} %bitcast.96), channel_id=1, source_target_pairs={{0,12},{16,28},{1,13},{17,29},{2,14},{18,30},{3,15},{19,31},{4,0},... | collective-permute-start | bytes 884744 | tf_op jit(solution)/shard_map/ppermute | solution.py:73
  65.5 4.5 %copy-start.23 = (s32[2048]{0:T(1024)}, s32[2048]{0:T(1024)S(1)}, u32[]{:S(2)}) copy-start(s32[2048]{0:T(1024)S(1)} %get-tuple-element.143) | copy-start | bytes 24580
  136.0 11.1 %copy-start.16 = (bf16[8,24,768]{2,1,0:T(8,128)(2,1)S(1)}, bf16[8,24,768]{2,1,0:T(8,128)(2,1)}, u32[]{:S(2)}) copy-start(bf16[8,24,768]{2,1,0:T(8,128)(2,1)} %get-tuple-element.87) | copy-start | bytes 884740
  145.1 21.9 %collective-permute-start.5 = (bf16[192,768]{1,0:T(8,128)(2,1)}, bf16[192,768]{1,0:T(8,128)(2,1)S(1)}, u32[]{:S(2)}, u32[]{:S(2)}) collective-permute-start(bf16[192,768]{1,0:T(8,128)(2,1)} %get-tuple-element.86), channel_id=1, source_target_pairs={{0,12},{16,28},{1,13},{17,29},{2,14},{18,30},{3,15},{19,31},{4,0},... | collective-permute-start | bytes 884744 | tf_op jit(solution)/shard_map/ppermute | solution.py:73
  145.1 26.4 %collective-permute-start.4 = (bf16[192,768]{1,0:T(8,128)(2,1)}, bf16[192,768]{1,0:T(8,128)(2,1)S(1)}, u32[]{:S(2)}, u32[]{:S(2)}) collective-permute-start(bf16[192,768]{1,0:T(8,128)(2,1)} %get-tuple-element.85), channel_id=1, source_target_pairs={{0,8},{16,24},{1,9},{17,25},{2,10},{18,26},{3,11},{19,27},{4,12},{... | collective-permute-start | bytes 884744 | tf_op jit(solution)/shard_map/ppermute | solution.py:73
  145.1 26.3 %collective-permute-start.3 = (bf16[192,768]{1,0:T(8,128)(2,1)}, bf16[192,768]{1,0:T(8,128)(2,1)S(1)}, u32[]{:S(2)}, u32[]{:S(2)}) collective-permute-start(bf16[192,768]{1,0:T(8,128)(2,1)} %get-tuple-element.84), channel_id=1, source_target_pairs={{0,4},{16,20},{1,5},{17,21},{2,6},{18,22},{3,7},{19,23},{4,8},{20,... | collective-permute-start | bytes 884744 | tf_op jit(solution)/shard_map/ppermute | solution.py:73
  163.1 8.3 %copy-start.14 = (bf16[192,768]{1,0:T(8,128)(2,1)S(1)}, bf16[192,768]{1,0:T(8,128)(2,1)}, u32[]{:S(2)}) copy-start(bf16[192,768]{1,0:T(8,128)(2,1)} %get-tuple-element.83) | copy-start | bytes 884740
  207.4 5.5 %copy-start.17 = (f32[4,24,768]{2,1,0:T(8,128)S(1)}, f32[4,24,768]{2,1,0:T(8,128)}, u32[]{:S(2)}) copy-start(f32[4,24,768]{2,1,0:T(8,128)} %get-tuple-element.88) | copy-start | bytes 884740
  207.4 5.4 %copy-start.22 = (bf16[4,24,768]{2,1,0:T(8,128)(2,1)S(1)}, bf16[4,24,768]{2,1,0:T(8,128)(2,1)}, u32[]{:S(2)}) copy-start(bf16[4,24,768]{2,1,0:T(8,128)(2,1)} %get-tuple-element.89) | copy-start | bytes 442372
  272.6 63.0 %copy-start.12 = (bf16[24,144,128]{2,1,0:T(8,128)(2,1)S(1)}, bf16[24,144,128]{2,1,0:T(8,128)(2,1)}, u32[]{:S(2)}) copy-start(bf16[24,144,128]{2,1,0:T(8,128)(2,1)} %get-tuple-element.119) | copy-start | bytes 2654212
  339.9 2.7 copy-start.8
  339.9 2.7 copy-start.15
  339.9 2.7 copy-start.24
  340.0 3.6 %copy-start.6 = (f32[3,24,2048]{2,1,0:T(8,128)}, f32[3,24,2048]{2,1,0:T(8,128)S(1)}, u32[]{:S(2)}) copy-start(f32[3,24,2048]{2,1,0:T(8,128)S(1)} %reshape.246) | copy-start | bytes 1769476
  340.0 2.6 copy-start.11
  340.0 2.6 copy-start.21
  (13 other events, 14.4 us)
Sparse Core Ops, SparseCore 0:
  207.5 84.2 all-gather.1

commit v2 on v1

--- a/solution.py
+++ b/solution.py
@@ -16,6 +16,7 @@
 DOCS = 4
 NS_STEPS = 5
 GROUP = 8
+HOST = 1
 SPARE = 2
 BLOCK = 256
 WIDE = 512
@@ -108,6 +109,11 @@
             lax.fori_loop(0, 2 * HEADS, greet, 0)
             pl.semaphore_wait(barrier, 2 * HEADS - 1)
 
+    def meet_own_plane(self, me):
+        @pl.when(attends(me))
+        def _():
+            self.meet(me, GROUP)
+
     def meet_heads(self, me):
         barrier = pltpu.get_barrier_semaphore()
 
@@ -268,6 +274,18 @@
             self.near(me).wait()
 
 
+class FanAcross(Across):
+    def __init__(self, net, source, target, plane, take, put, goes):
+        super().__init__(
+            net,
+            source,
+            target,
+            take,
+            put,
+            lambda i, j: jnp.logical_and(goes(i, j), j // GROUP == plane),
+        )
+
+
 class FanIn(Flow):
     def __init__(self, source, target, owner, take, put, goes=None, size=None):
         super().__init__(source, target, take, put, goes, size)
@@ -476,14 +494,11 @@
                             self.output[...] += self.held[4][source].astype(jnp.float32)
 
 
-def bind_all(net, flows, inputs, outputs, scratch, send, receive, local):
-    used = 0
+def bind_all(net, flows, inputs, outputs, refs):
     for number, flow in enumerate(flows):
         need = len(flow.scratch())
-        flow.bind(
-            net, inputs, outputs, scratch[used : used + need], send.at[number], receive.at[number], local.at[number]
-        )
-        used += need
+        held, (send, receive), refs = refs[:need], refs[need : need + 2], refs[need + 2 :]
+        flow.bind(net, inputs, outputs, held, send, receive, refs[-1].at[number])
 
 
 def exchange_kernel(net, meet, flows, sources, targets, *refs):
@@ -491,7 +506,7 @@
     outputs = refs[sources : sources + targets]
     me = net.me()
     meet(me)
-    bind_all(net, flows, inputs, outputs, refs[sources + targets : -3], *refs[-3:])
+    bind_all(net, flows, inputs, outputs, refs[sources + targets :])
     for flow in flows:
         flow.start(me)
     for flow in flows:
@@ -501,12 +516,10 @@
 
 
 def flow_scratch(flows):
-    most = max(flow.semaphores() for flow in flows)
-    return [shape for flow in flows for shape in flow.scratch()] + [
-        pltpu.SemaphoreType.DMA((len(flows), most)),
-        pltpu.SemaphoreType.DMA((len(flows), most)),
-        pltpu.SemaphoreType.DMA((len(flows),)),
-    ]
+    shapes = []
+    for flow in flows:
+        shapes += flow.scratch() + [pltpu.SemaphoreType.DMA((flow.semaphores(),))] * 2
+    return shapes + [pltpu.SemaphoreType.DMA((len(flows),))]
 
 
 def exchange(net, name, number, flows, sources, shapes, size=None, meet=None):
@@ -543,7 +556,7 @@
     beside = flip_y(me)
     sibling = flip_core(me)
     net.meet(me, count)
-    bind_all(net, flows, extra_refs, extra_all, (), *refs)
+    bind_all(net, flows, extra_refs, extra_all, refs)
 
     def remote(source, target, index, device):
         return pltpu.make_async_remote_copy(
@@ -1011,7 +1024,7 @@
     part = FF // GROUP
     for step, block in enumerate(blocks):
         source = (plane + planes - step) % planes
-        weights[pl.ds(pl.multiple_of(source * span, span), span), :] = block[...]
+        weights[pl.ds(pl.multiple_of(source * span, span), span), :] = block[:, :D]
 
     def forward(chunk, carry):
         here = columns_of(chunk)
@@ -1089,33 +1102,45 @@
     )(second_grad, middle, cotangent, mixed, out)
 
 
-def input_kernel(grads_ref, weights_ref, tokens_ref, middle_grad_ref, input_ref, query, key, value):
-    for micro in range(2):
-        here = slice(64 * micro, 64 * micro + 64)
-        for pair in range(HEADS // 2):
-            head = 2 * pair
-            two = [grads_ref[HEADS * micro + head + k].astype(jnp.float32) for k in range(2)]
-            there = slice(128 * pair, 128 * pair + 128)
-            query[here, there] = jnp.concatenate([t[:64, :HEAD_DIM] for t in two], axis=1).astype(jnp.bfloat16)
-            key[here, there] = jnp.concatenate([t[:64, HEAD_DIM:] for t in two], axis=1).astype(jnp.bfloat16)
-            value[here, there] = jnp.concatenate([unfold(t[64:96]) for t in two], axis=1).astype(jnp.bfloat16)
-    gradient = (
-        nt(query[...], weights_ref[0]) + nt(key[...], weights_ref[1]) + nt(value[...], weights_ref[2])
-    )
-    input_ref[...] = middle_grad_ref[...] + norm_back(tokens_ref[...].astype(jnp.float32), gradient)
-
-
-def input_gradient(grads, weights, tokens, middle_grad):
-    rows = pltpu.VMEM(tokens.shape, jnp.bfloat16)
+def input_kernel(net, slots, grads_ref, *refs):
+    blocks, partial_ref, weights = refs[: net.planes], refs[net.planes], refs[net.planes + 1]
+    me = net.me()
+    plane = me // GROUP
+    span = D // net.planes
+
+    @pl.when(attends(me))
+    def _():
+        for step, block in enumerate(blocks):
+            source = (plane + net.planes - step) % net.planes
+            weights[pl.ds(pl.multiple_of(source * span, span), span), :] = block[:, D:]
+
+        def one(slot, carry):
+            total = jnp.zeros((GROUP * 64, D), jnp.float32)
+            for group in range(3):
+                rows = []
+                for token in range(GROUP):
+                    given = grads_ref[slot, group, token]
+                    value = unfold(given[64:].astype(jnp.float32)).astype(jnp.bfloat16)
+                    rows.append(jnp.concatenate([given[:64], value], axis=1))
+                taken = jnp.concatenate(rows, axis=0)
+                total = total + nt(taken, weights[:, 192 * group : 192 * group + 192])
+            partial_ref[slot] = total.reshape(GROUP, 64, D).astype(jnp.bfloat16)
+            return carry
+
+        lax.fori_loop(0, jnp.where(plane == HOST, slots, 1), one, 0)
+
+
+def input_partial(net, grads, blocks):
+    slots = grads.shape[0]
     return pl.pallas_call(
-        input_kernel,
-        out_shape=jax.ShapeDtypeStruct(tokens.shape, jnp.float32),
-        in_specs=[VMEM] * 4,
+        functools.partial(input_kernel, net, slots),
+        out_shape=jax.ShapeDtypeStruct((slots, GROUP, 64, D), jnp.bfloat16),
+        in_specs=[VMEM] * (1 + len(blocks)),
         out_specs=VMEM,
-        scratch_shapes=[rows] * 3,
-        cost_estimate=pl.CostEstimate(flops=5 * 10**8, bytes_accessed=6 * 2**20, transcendentals=0),
-        name="input_gradient",
-    )(grads, weights, tokens, middle_grad)
+        scratch_shapes=[pltpu.VMEM((D, blocks[0].shape[1] - D), jnp.bfloat16)],
+        cost_estimate=pl.CostEstimate(flops=10**9, bytes_accessed=6 * 2**20, transcendentals=0),
+        name="input_partial",
+    )(grads, *blocks)
 
 
 def solve_heads(me, head_ref, moment_ref, target, scratch):
@@ -1272,9 +1297,11 @@
     counts = jnp.sum((doc_ids[:, :, None] == jnp.arange(DOCS)[None, None, :]).astype(jnp.float32), axis=1)
     tail = jnp.pad(counts.reshape(-1).astype(low), (0, HEAD_DIM - micro_count * DOCS))
     columns = attn_low[:3].reshape(3, rows, HEADS, HEAD_DIM).transpose(2, 1, 0, 3).reshape(HEADS, rows, 3 * HEAD_DIM)
+    shares = columns.reshape(3, 4, rows, 3 * HEAD_DIM).transpose(1, 2, 0, 3).reshape(4, rows, 9 * HEAD_DIM)
+    shares = jnp.pad(shares, ((0, 0), (0, 0), (0, HEAD_DIM)))
     columns = jnp.concatenate([columns, jnp.broadcast_to(tail, (HEADS, rows, HEAD_DIM))], axis=2)
     moment_low = attn_moment.astype(low)
-    all_tokens, all_columns, plane_cut, plane_out, moment_plane, moment_out = gather_tokens(
+    all_tokens, all_columns, plane_cut, plane_out, moment_plane, moment_out, plane_shares = gather_tokens(
         net,
         0,
         normed.reshape(micro_count, token_count, width),
@@ -1284,16 +1311,20 @@
             Across(net, 1, 1, lambda i, j: 0, lambda i, j: i // GROUP),
             Across(net, 3, 3, lambda i, j: 0, lambda i, j: i // GROUP, lambda i, j: j // GROUP == SPARE),
         ]
-        + [Flow(2, 2, lambda i, j: j % GROUP, lambda i, j: i % GROUP, size=GROUP)],
-        [cut, attn_low[3:], cut_up(ffn_moment.astype(low)), moment_low[3:]],
+        + [
+            Flow(2, 2, lambda i, j: j % GROUP, lambda i, j: i % GROUP, size=GROUP),
+            Flow(4, 4, lambda i, j: j % 4, lambda i, j: i % GROUP, size=GROUP),
+        ],
+        [cut, attn_low[3:], cut_up(ffn_moment.astype(low)), moment_low[3:], shares],
         [
             jax.ShapeDtypeStruct(cut.shape, low),
             jax.ShapeDtypeStruct((planes, rows, D), low),
             jax.ShapeDtypeStruct(cut.shape, low),
             jax.ShapeDtypeStruct((planes, rows, D), low),
+            jax.ShapeDtypeStruct((GROUP,) + shares.shape[1:], low),
         ],
     )
-    late_own = plane_cut.reshape(GROUP * rows, 3 * part)
+    late_own = jnp.concatenate([plane_cut, plane_shares], axis=2).reshape(GROUP * rows, -1)
     late_blocks = [late_own] + [net.shift(late_own, step) for step in range(1, planes)]
 
     head_weights = all_columns[:, :, : 3 * HEAD_DIM].reshape(D, 3 * HEAD_DIM).T
@@ -1346,7 +1377,7 @@
     (second_grad,) = exchange(
         net,
         "second_grad_exchange",
-        8,
+        11,
         [PlaneScatter(0, 0, (both, width))],
         [second_terms.reshape(sides)],
         [jax.ShapeDtypeStruct((both, width), jnp.float32)],
@@ -1385,8 +1416,6 @@
     )
     out_update = (0.75 * out_total + 0.25 * moment_out.astype(jnp.float32)).astype(low)
 
-    early_low, grad_parts = lax.optimization_barrier((attn_low[:3], grad_parts))
-    attn_full = lax.all_gather(early_low, ("blk", "head"), axis=1, tiled=True)
     grad_packed, head_grad = attend_back(
         net, first, all_tokens, qkv, mixed, total, cosine, sine, start, grad_parts
     )
@@ -1424,80 +1453,103 @@
         meet=net.meet_heads,
     )
     grad_packed, head_low, head_whole = lax.optimization_barrier((grad_packed, head_low, head_whole))
+    guests = [p for p in range(planes) if p >= 4 or p == SPARE]
+    slots = 1 + len(guests)
     head_rows = jnp.pad(head_low.T.reshape(count, rows, 3 * HEAD_DIM), ((0, 0), (0, 0), (0, 64)))
-    outgoing = jnp.concatenate([grad_packed, head_rows.reshape(count, rows * 2, 128)], axis=1)
-    ffn_rows, result_sides = ffn_block.reshape(GROUP, rows, 3 * part), result_terms.reshape(sides)
-    last = [
-        jax.ShapeDtypeStruct((2 * HEADS, 96 + 2 * rows, 128), low),
-        jax.ShapeDtypeStruct((GROUP, rows, 3 * part), low),
-        jax.ShapeDtypeStruct((both, width), jnp.float32),
-    ]
-
-    def last_flows(base, runs):
-        return [
-            PlaneScatter(base + 2, base + 2, (both, width), runs=runs),
-            Flow(
-                base,
-                base,
-                lambda i, j: j,
-                lambda i, j: combo_of(i),
-                lambda i, j: jnp.logical_and(attends(i), runs(j)),
-            ),
-            Flow(
-                base + 1,
-                base + 1,
-                lambda i, j: j % GROUP,
-                lambda i, j: i % GROUP,
-                lambda i, j: runs(i),
-                size=GROUP,
-            ),
-        ]
-
-    early_last = exchange(
+
+    def group_of(device):
+        return device // GROUP - (device // GROUP) // 3
+
+    def waits(device):
+        return jnp.logical_not(attends(device))
+
+    def head_flow(runs):
+        return Flow(
+            0, 0, lambda i, j: j, lambda i, j: combo_of(i), lambda i, j: jnp.logical_and(attends(i), runs(j))
+        )
+
+    row_shape = jax.ShapeDtypeStruct((2 * HEADS, rows, 256), low)
+    early_rows, host_grads = exchange(
         net,
         "attending_exchange",
         7,
-        last_flows(0, attends),
-        [outgoing, ffn_rows, result_sides],
-        last,
+        [
+            Across(
+                net,
+                1,
+                1,
+                lambda i, j: j // GROUP,
+                lambda i, j: (0, group_of(i)),
+                lambda i, j: jnp.logical_and(attends(i), attends(j)),
+            )
+        ]
+        + [
+            FanAcross(
+                net, 1, 1, HOST, lambda i, j, p=p: p, lambda i, j, k=k: (1 + k, group_of(i)), lambda i, j: attends(i)
+            )
+            for k, p in enumerate(guests)
+        ]
+        + [head_flow(attends)],
+        [head_rows, grad_packed.reshape(planes, GROUP, 96, 128)],
+        [row_shape, jax.ShapeDtypeStruct((slots, 3, GROUP, 96, 128), low)],
         meet=net.meet_attending,
     )
+    partial = input_partial(net, host_grads, late_blocks)
     attn_done, ffn_done = newton(
         net, head_whole, moment_whole.reshape(D, D), out_whole.reshape(D, D), ffn_whole.reshape(D, FF)
     )
-    attn_done, ffn_done, outgoing, *early_last = lax.optimization_barrier(
-        (attn_done, ffn_done, outgoing, *early_last)
-    )
-    attn_step, ffn_step, out_row_grad, *late_last = exchange(
+    attn_done, ffn_done, partial, early_rows = lax.optimization_barrier((attn_done, ffn_done, partial, early_rows))
+
+    def guest_index(device):
+        p = device // GROUP
+        return p - SPARE - jnp.minimum(p // 4, 1)
+
+    late_rows, ffn_parts, attn_step, ffn_step, out_row_grad, input_parts, result = exchange(
         net,
         "step_exchange",
         5,
-        [FanOut(1, 1, OWNERS[4 + k], lambda i, j: j, lambda i, j, k=k: k) for k in range(3)]
-        + [FanOut(0, 0, OWNERS[k], lambda i, j: j, lambda i, j, k=k: k) for k in range(4)]
-        + [Across(net, 2, 2, lambda i, j: j // GROUP, lambda i, j: 0, lambda i, j: i // GROUP == SPARE)]
-        + last_flows(3, lambda i: jnp.logical_not(attends(i))),
+        [PlaneScatter(6, 6, (both, width))]
+        + [FanOut(3, 3, OWNERS[4 + k], lambda i, j: j, lambda i, j, k=k: k) for k in range(3)]
+        + [FanOut(2, 2, OWNERS[k], lambda i, j: j, lambda i, j, k=k: k) for k in range(4)]
+        + [
+            Flow(
+                5,
+                5,
+                lambda i, j: (1 + guest_index(j), j % GROUP),
+                lambda i, j: i % GROUP,
+                lambda i, j: jnp.logical_and(i // GROUP == HOST, waits(j)),
+            ),
+            Flow(5, 5, lambda i, j: (0, j % GROUP), lambda i, j: i % GROUP, lambda i, j: attends(i), size=GROUP),
+            Flow(1, 1, lambda i, j: j % GROUP, lambda i, j: i % GROUP, size=GROUP),
+            Across(net, 4, 4, lambda i, j: j // GROUP, lambda i, j: 0, lambda i, j: i // GROUP == SPARE),
+            head_flow(waits),
+        ],
         [
+            head_rows,
+            ffn_block.reshape(GROUP, rows, 3 * part),
             attn_done.reshape(count, rows, D),
             ffn_done.reshape(count, rows, FF),
             out_total.astype(low),
-            outgoing,
-            ffn_rows,
-            result_sides,
+            partial,
+            result_terms.reshape(sides),
         ],
         [
+            row_shape,
+            jax.ShapeDtypeStruct((GROUP, rows, 3 * part), low),
             jax.ShapeDtypeStruct((4, rows, D), low),
             jax.ShapeDtypeStruct((3, rows, FF), low),
             jax.ShapeDtypeStruct((1, rows, D), low),
-        ]
-        + last,
+            jax.ShapeDtypeStruct((GROUP, token_count, width), low),
+            jax.ShapeDtypeStruct((both, width), jnp.float32),
+        ],
     )
-    grads, ffn_parts, result = (jnp.where(attends(me), a, b) for a, b in zip(early_last, late_last))
+    row_parts = jnp.where(attends(me), early_rows, late_rows)
+    normed_grad = jnp.sum(input_parts.reshape(2, 4, token_count, width).astype(jnp.float32), axis=1).reshape(both, width)
+    input_grad = middle_grad + norm_back(hidden, normed_grad)
     ffn_grad = ffn_parts.reshape(GROUP, rows, 3, part).transpose(2, 1, 0, 3).reshape(3, rows, FF).astype(jnp.float32)
     ffn_moment_new = 0.5 * ffn_moment + 0.5 * ffn_grad
 
-    input_grad = input_gradient(grads, attn_full, own_tokens, middle_grad)
-    row_grads = grads[:, 96:].reshape(micro_count, HEADS, rows, 256).astype(jnp.float32)
-    summed = jnp.sum(row_grads, axis=0)
+    summed = jnp.sum(row_parts.reshape(micro_count, HEADS, rows, 256).astype(jnp.float32), axis=0)
     early_grad = summed[:, :, : 3 * HEAD_DIM].reshape(HEADS, rows, 3, HEAD_DIM).transpose(2, 1, 0, 3).reshape(3, rows, D)
     attn_grad = jnp.concatenate([early_grad, out_row_grad.astype(jnp.float32)], axis=0)
     attn_moment_new = 0.5 * attn_moment + 0.5 * attn_grad

time: 357 us -> 336 us (0.941)
  between operations: 14.7 us -> 1.27 us
  Pallas kernels: 293 us -> 285 us
    pallas_call x8, Pallas kernels: 190 us -> 183 us  [exchange(): pl.pallas_call(functools.partial(exchange_kernel, net, meet or (lambda me...]
  transfers between devices with their start and end apart: 7 -> 6, of which waited for: 1 -> 2; matrix products, arithmetic and copies ran while one was open for 5% -> 2% of each run, Pallas kernels for 58% -> 27%
where the time goes in v2:
time: 336 us; the launch traced here: 335 us
  Pallas kernels  285 us (85%)
  other arithmetic  19.3 us (6%)
  local copies, waits for them, and re-layouts  13.2 us (4%)
  starting transfers between devices  13 us (4%)
    pallas_call x8, Pallas kernels, exchange(): pl.pallas_call(functools.partial(exchange_kernel, net, meet or (lambda me...  183 us
    pallas_call x1, Pallas kernels, gather_tokens(): pl.pallas_call(functools.partial(gather_kernel, net, flows, len(extras)),...  38.5 us
    pallas_call x1, Pallas kernels, newton(): pl.pallas_call(functools.partial(newton_kernel, net), out_shape=[SQUARE,...  37.6 us
    ppermute x6, starting transfers between devices, permute(): lax.ppermute(values, ('head', 'blk'), [(place(i), place(j)) for i, j in p...  13 us
    pallas_call x1, Pallas kernels, feed_forward(): pl.pallas_call(functools.partial(feed_forward_kernel, net), out_shape=[ja...  9.4 us
  transfers between devices with their start and end apart: 6, of which 2 were waited for; matrix products, arithmetic and copies ran while one was open for 2% of the time, Pallas kernels for 27%

profile of v2, /device:TPU:18, one launch (start us, length us, event | category | flops | bytes accessed | tf_op | source)
XLA Modules:
  0.0 335.3 jit_solution(7864821576668867083)
XLA Ops:
  9.8 38.5 %gather_tokens.1 = (bf16[4,2,4,64,768]{4,3,2,1,0:T(8,128)(2,1)}, bf16[32,24,256]{2,1,0:T(8,128)(2,1)}, bf16[8,24,768]{2,1,0:T(8,128)(2,1)}, bf16[4,24,768]{2,1,0...) custom-call(bf16[2,64,768]{2,1,0:T(8,128)(2,1)} %multiply_convert_fusion.x_ref, ...), custom_call_target="tpu_custom_call" | custom-call | bytes 104857600 | tf_op jit(solution)/shard_map/gather_tokens/pallas_call | solution.py:691
  49.4 6.6 %collective-permute-start = (bf16[192,1408]{1,0:T(8,128)(2,1)S(1)}, bf16[192,1408]{1,0:T(8,128)(2,1)S(1)}, u32[]{:S(2)}, u32[]{:S(2)}) collective-permute-start(bf16[192,1408]{1,0:T(8,128)(2,1)S(1)} %bitcast.86), channel_id=1, source_target_pairs={{0,4},{16,20},{1,5},{17,21},{2,6},{18,22},{3,7},{19,23},{4,8},{20,... | collective-permute-start | bytes 1622024 | tf_op jit(solution)/shard_map/ppermute | solution.py:74
  56.0 2.0 collective-permute-start.1
  58.0 2.4 collective-permute-start.2
  62.0 1.9 copy.46
  64.5 1.8 multiply_sine_fusion
  66.3 3.2 attend.1
  69.6 45.9 %mixed_exchange.1 = (bf16[24,32,128]{2,1,0:T(8,128)(2,1)}, bf16[32,24,768]{2,1,0:T(8,128)(2,1)}, bf16[8,128,768]{2,1,0:T(8,128)(2,1)}, bf16[4,8,24,768]{3,2,1,0:T(8,128)(2,1)}) custom-call(bf16[32,32,128]{2,1,0:T(8,128)(2,1)} %get-tuple-element.68.refs_0_, bf16[4,24,768]{2,1,0:T(8,128)(2,1)} %copy-done.13, bf16[128,768]{1,0:T(8,128)(2,1)} %bitcast.109, ...), custom_call_target="tpu_custom_call" | custom-call | bytes 33030144 | tf_op jit(solution)/shard_map/mixed_exchange/pallas_call | solution.py:531
  115.5 2.8 after_attention.1
  118.3 17.6 %second_exchange.1 = bf16[8,128,768]{2,1,0:T(8,128)(2,1)} custom-call(bf16[128,768]{1,0:T(8,128)(2,1)} %get-tuple-element.73.refs_0_), custom_call_target="tpu_custom_call" | custom-call | bytes 12582912 | tf_op jit(solution)/shard_map/second_exchange/pallas_call | solution.py:531
  136.9 9.4 %feed_forward.1 = (bf16[1024,768]{1,0:T(8,128)(2,1)}, bf16[1024,768]{1,0:T(8,128)(2,1)}, bf16[192,768]{1,0:T(8,128)(2,1)}, bf16[192,768]{1,0:T(8,128)(2,1)}, bf1...) custom-call(bf16[1024,768]{1,0:T(8,128)(2,1)} %bitcast.91, bf16[1024,768]{1,0:T(8,128)(2,1)} %bitcast.121, ...), custom_call_target="tpu_custom_call" | custom-call | flops 3500000000 | bytes 10485760 | tf_op jit(solution)/shard_map/feed_forward/pallas_call | solution.py:1059
  146.3 2.0 collective-permute-start.5
  148.6 16.0 %second_grad_exchange.1.second_grad_ref = f32[128,768]{1,0:T(8,128)} custom-call(bf16[2,2,2,128,768]{4,3,2,1,0:T(8,128)(2,1)} %bitcast.92), custom_call_target="tpu_custom_call" | custom-call | bytes 3145728 | tf_op jit(solution)/shard_map/second_grad_exchange/pallas_call | solution.py:531
  164.6 3.8 %before_attention.1 = (f32[128,768]{1,0:T(8,128)}, bf16[24,32,128]{2,1,0:T(8,128)(2,1)}, bf16[768,768]{1,0:T(8,128)(2,1)}) custom-call(f32[128,768]{1,0:T(8,128)} %second_grad_exchange.1.second_grad_ref, f32[128,768]{1,0:T(8,128)} %get-tuple-element.72.middle_ref, bf16[128,768]{1,0:T(8,128)(2,1)} %bitcast.110, bf16[128,768]{1,0:T(8,128)(2,1)} %get-tuple-element.78.mixed_ref, ...), custom_call_target="tpu_custom_call" | custom-call | flops 400000000 | bytes 5242880 | tf_op jit(solution)/shard_map/before_attention/pallas_call | solution.py:1091
  169.0 2.5 collective-permute-done.5
  172.6 37.5 %mixed_grad_exchange.1 = (bf16[32,32,128]{2,1,0:T(8,128)(2,1)}, f32[4,24,768]{2,1,0:T(8,128)}, bf16[4,192,2048]{2,1,0:T(8,128)(2,1)}) custom-call(bf16[24,32,128]{2,1,0:T(8,128)(2,1)} %get-tuple-element.79.refs_0_, bf16[4,2,2,2,24,768]{5,4,3,2,1,0:T(8,128)(2,1)} %bitcast.98, bf16[192,768]{1,0:T(8,128)(2,1)} %get-tuple-element.131.refs_2_), custom_call_target="tpu_custom_call" | custom-call | bytes 29622272 | tf_op jit(solution)/shard_map/mixed_grad_exchange/pallas_call | solution.py:531
  210.1 3.6 %attend_back.1 = (bf16[32,96,128]{2,1,0:T(8,128)(2,1)}, f32[192,768]{1,0:T(8,128)}) custom-call(s32[2,4]{1,0:T(2,128)} %pad_add_fusion.refs_0_, bf16[4,2,4,64,768]{4,3,2,1,0:T(8,128)(2,1)} %get-tuple-element.67.refs_1_, bf16[192,2048]{1,0:T(8,128)(2,1)} %get-tuple-element.88.refs_2_, f32[64,2048]{1,0:T(8,128)} %get-tuple-element.89.refs_3_, ...), custom_call_target="tpu_custom_call" | custom-call | flops 4000000000 | bytes 12582912 | tf_op jit(solution)/shard_map/attend_back/pallas_call | solution.py:944
  213.7 1.8 convert_element_type.163
  216.3 11.4 %out_exchange.1 = bf16[4,8,24,768]{3,2,1,0:T(8,128)(2,1)} custom-call(bf16[4,24,768]{2,1,0:T(8,128)(2,1)} %get-tuple-element.94.refs_0_), custom_call_target="tpu_custom_call" | custom-call | bytes 9437184 | tf_op jit(solution)/shard_map/out_exchange/pallas_call | solution.py:531
  227.8 1.9 head_exchange.1.head_ref
  230.6 2.7 attending_exchange.1
  233.3 37.6 %newton.1 = (bf16[768,768]{1,0:T(8,128)(2,1)}, bf16[768,2048]{1,0:T(8,128)(2,1)}) custom-call(bf16[24,64,768]{2,1,0:T(8,128)(2,1)} %head_exchange.1.head_ref, bf16[768,768]{1,0:T(8,128)(2,1)} %bitcast.122, bf16[768,768]{1,0:T(8,128)(2,1)} %bitcast.104, bf16[768,2048]{1,0:T(8,128)(2,1)} %bitcast.120), custom_call_target="tpu_custom_call" | custom-call | flops 24999999488 | bytes 8388608 | tf_op jit(solution)/shard_map/newton/pallas_call | solution.py:1263
  270.9 3.1 input_partial.1.refs_5_
  274.0 50.3 %step_exchange.1 = (bf16[24,24,256]{2,1,0:T(8,128)(2,1)}, bf16[8,24,768]{2,1,0:T(8,128)(2,1)}, bf16[4,24,768]{2,1,0:T(8,128)(2,1)}, bf16[3,24,2048]{2,1,0:T(8,12...) custom-call(bf16[32,24,256]{2,1,0:T(8,128)(2,1)} %pad.14.refs_0_, ...), custom_call_target="tpu_custom_call" | custom-call | bytes 17989632 | tf_op jit(solution)/shard_map/step_exchange/pallas_call | solution.py:531
  (137 shorter events, 27.8 us)
Async XLA Ops:
  0.6 2.5 copy-start
  1.9 2.7 copy-start.29
  1.9 3.0 copy-start.10
  2.1 3.5 %copy-start.4 = (f32[3,24,2048]{2,1,0:T(8,128)S(1)}, f32[3,24,2048]{2,1,0:T(8,128)}, u32[]{:S(2)}) copy-start(f32[3,24,2048]{2,1,0:T(8,128)} %param.12) | copy-start | bytes 1769476
  4.9 2.1 copy-start.13
  4.9 2.1 copy-start.5
  49.4 20.2 %copy-start.7 = (bf16[8,24,1408]{2,1,0:T(8,128)(2,1)}, bf16[8,24,1408]{2,1,0:T(8,128)(2,1)S(1)}, u32[]{:S(2)}) copy-start(bf16[8,24,1408]{2,1,0:T(8,128)(2,1)S(1)} %pad_maximum_fusion) | copy-start | bytes 1622020
  49.4 86.5 %collective-permute-start = (bf16[192,1408]{1,0:T(8,128)(2,1)S(1)}, bf16[192,1408]{1,0:T(8,128)(2,1)S(1)}, u32[]{:S(2)}, u32[]{:S(2)}) collective-permute-start(bf16[192,1408]{1,0:T(8,128)(2,1)S(1)} %bitcast.86), channel_id=1, source_target_pairs={{0,4},{16,20},{1,5},{17,21},{2,6},{18,22},{3,7},{19,23},{4,8},{20,... | collective-permute-start | bytes 1622024 | tf_op jit(solution)/shard_map/ppermute | solution.py:74
  56.0 79.9 %collective-permute-start.1 = (bf16[192,1408]{1,0:T(8,128)(2,1)S(1)}, bf16[192,1408]{1,0:T(8,128)(2,1)S(1)}, u32[]{:S(2)}, u32[]{:S(2)}) collective-permute-start(bf16[192,1408]{1,0:T(8,128)(2,1)S(1)} %bitcast.87), channel_id=1, source_target_pairs={{0,8},{16,24},{1,9},{17,25},{2,10},{18,26},{3,11},{19,27},{4,12},{... | collective-permute-start | bytes 1622024 | tf_op jit(solution)/shard_map/ppermute | solution.py:74
  58.0 78.0 %collective-permute-start.2 = (bf16[192,1408]{1,0:T(8,128)(2,1)S(1)}, bf16[192,1408]{1,0:T(8,128)(2,1)}, u32[]{:S(2)}, u32[]{:S(2)}) collective-permute-start(bf16[192,1408]{1,0:T(8,128)(2,1)S(1)} %bitcast.88), channel_id=1, source_target_pairs={{0,12},{16,28},{1,13},{17,29},{2,14},{18,30},{3,15},{19,31},{4,0},... | collective-permute-start | bytes 1622024 | tf_op jit(solution)/shard_map/ppermute | solution.py:74
  61.8 4.5 %copy-start.26 = (s32[2048]{0:T(1024)}, s32[2048]{0:T(1024)S(1)}, u32[]{:S(2)}) copy-start(s32[2048]{0:T(1024)S(1)} %get-tuple-element.137) | copy-start | bytes 24580
  136.9 11.6 %copy-start.18 = (bf16[8,24,768]{2,1,0:T(8,128)(2,1)S(1)}, bf16[8,24,768]{2,1,0:T(8,128)(2,1)}, u32[]{:S(2)}) copy-start(bf16[8,24,768]{2,1,0:T(8,128)(2,1)} %get-tuple-element.85) | copy-start | bytes 884740
  146.3 22.7 %collective-permute-start.3 = (bf16[192,768]{1,0:T(8,128)(2,1)}, bf16[192,768]{1,0:T(8,128)(2,1)S(1)}, u32[]{:S(2)}, u32[]{:S(2)}) collective-permute-start(bf16[192,768]{1,0:T(8,128)(2,1)} %get-tuple-element.82), channel_id=1, source_target_pairs={{0,4},{16,20},{1,5},{17,21},{2,6},{18,22},{3,7},{19,23},{4,8},{20,... | collective-permute-start | bytes 884744 | tf_op jit(solution)/shard_map/ppermute | solution.py:74
  146.3 22.7 %collective-permute-start.4 = (bf16[192,768]{1,0:T(8,128)(2,1)}, bf16[192,768]{1,0:T(8,128)(2,1)S(1)}, u32[]{:S(2)}, u32[]{:S(2)}) collective-permute-start(bf16[192,768]{1,0:T(8,128)(2,1)} %get-tuple-element.83), channel_id=1, source_target_pairs={{0,8},{16,24},{1,9},{17,25},{2,10},{18,26},{3,11},{19,27},{4,12},{... | collective-permute-start | bytes 884744 | tf_op jit(solution)/shard_map/ppermute | solution.py:74
  146.3 25.2 %collective-permute-start.5 = (bf16[192,768]{1,0:T(8,128)(2,1)}, bf16[192,768]{1,0:T(8,128)(2,1)S(1)}, u32[]{:S(2)}, u32[]{:S(2)}) collective-permute-start(bf16[192,768]{1,0:T(8,128)(2,1)} %get-tuple-element.84), channel_id=1, source_target_pairs={{0,12},{16,28},{1,13},{17,29},{2,14},{18,30},{3,15},{19,31},{4,0},... | collective-permute-start | bytes 884744 | tf_op jit(solution)/shard_map/ppermute | solution.py:74
  164.5 7.0 %copy-start.17 = (bf16[192,768]{1,0:T(8,128)(2,1)S(1)}, bf16[192,768]{1,0:T(8,128)(2,1)}, u32[]{:S(2)}) copy-start(bf16[192,768]{1,0:T(8,128)(2,1)} %get-tuple-element.81) | copy-start | bytes 884740
  210.1 5.5 %copy-start.21 = (f32[4,24,768]{2,1,0:T(8,128)S(1)}, f32[4,24,768]{2,1,0:T(8,128)}, u32[]{:S(2)}) copy-start(f32[4,24,768]{2,1,0:T(8,128)} %get-tuple-element.86) | copy-start | bytes 884740
  210.1 5.4 %copy-start.24 = (bf16[4,24,768]{2,1,0:T(8,128)(2,1)S(1)}, bf16[4,24,768]{2,1,0:T(8,128)(2,1)}, u32[]{:S(2)}) copy-start(bf16[4,24,768]{2,1,0:T(8,128)(2,1)} %get-tuple-element.87) | copy-start | bytes 442372
  227.7 1.9 copy-start.3
  325.8 1.6 copy-start.19
  328.7 1.6 copy-start.8
  328.7 3.3 copy-start.28
  329.0 3.0 copy-start.6
  329.8 2.2 copy-start.20
  (12 other events, 15.1 us)

commit v3 on v2

--- a/solution.py
+++ b/solution.py
@@ -18,6 +18,7 @@
 GROUP = 8
 HOST = 1
 SPARE = 2
+KEYS = 512
 BLOCK = 256
 WIDE = 512
 
@@ -109,11 +110,6 @@
             lax.fori_loop(0, 2 * HEADS, greet, 0)
             pl.semaphore_wait(barrier, 2 * HEADS - 1)
 
-    def meet_own_plane(self, me):
-        @pl.when(attends(me))
-        def _():
-            self.meet(me, GROUP)
-
     def meet_heads(self, me):
         barrier = pltpu.get_barrier_semaphore()
 
@@ -401,9 +397,10 @@
 
 
 class PlaneScatter(Flow):
-    def __init__(self, source, target, block, lead=(), runs=None, gathers=False):
+    def __init__(self, source, target, block, lead=(), runs=None, moment=None, whole=None):
         super().__init__(source, target, None, None)
-        self.block, self.lead, self.gathers = block, lead, gathers
+        self.block, self.lead = block, lead
+        self.gathers, self.moment_source, self.whole_target = moment is not None, moment, whole
         self.runs = runs or (lambda i: i >= 0)
         self.every = (slice(None),) * len(lead)
 
@@ -414,11 +411,49 @@
             shapes += [
                 pltpu.VMEM(self.lead + self.block, jnp.bfloat16),
                 pltpu.VMEM(self.lead + self.lead + self.block, jnp.bfloat16),
+                pltpu.VMEM(self.lead + self.block, jnp.bfloat16),
+                pltpu.VMEM(self.lead + self.block, jnp.bfloat16),
             ]
         return shapes
 
+    def bind(self, net, inputs, outputs, scratch, send, receive, local):
+        super().bind(net, inputs, outputs, scratch, send, receive, local)
+        if self.gathers:
+            self.moment, self.whole = inputs[self.moment_source], outputs[self.whole_target]
+
+    def momentum(self):
+        return pltpu.make_async_copy(self.moment, self.held[5], self.receive.at[5 + SPARE])
+
+    def direction(self, place):
+        index = 5 + self.lead[0] + place
+        return self.copy(self.held[6], self.whole.at[:, place], index, OWNERS[3])
+
+    def close(self, me):
+        place = me % GROUP
+        for source in range(self.lead[0]):
+            if source != SPARE:
+                self.onward(me, source).wait_recv()
+                self.output[...] += self.held[4][source].astype(jnp.float32)
+        self.momentum().start()
+        self.momentum().wait()
+        self.held[6][...] = (0.75 * self.output[...] + 0.25 * self.held[5][...].astype(jnp.float32)).astype(jnp.bfloat16)
+
+        @pl.when(me != OWNERS[3])
+        def _():
+            self.direction(place).start()
+            self.direction(place).wait_send()
+
+        @pl.when(me == OWNERS[3])
+        def _():
+            own = pltpu.make_async_copy(self.held[6], self.whole.at[:, place], self.local)
+            own.start()
+            own.wait()
+            for other in range(GROUP):
+                if other != OWNERS[3] % GROUP:
+                    self.direction(other).wait_recv()
+
     def semaphores(self):
-        return 5 + (self.lead[0] if self.gathers else 0)
+        return 5 + (self.lead[0] + GROUP if self.gathers else 0)
 
     def onward(self, me, source):
         spare = GROUP * SPARE + me % GROUP
@@ -488,10 +523,7 @@
 
                 @pl.when(plane == SPARE)
                 def _():
-                    for source in range(self.lead[0]):
-                        if source != SPARE:
-                            self.onward(me, source).wait_recv()
-                            self.output[...] += self.held[4][source].astype(jnp.float32)
+                    self.close(me)
 
 
 def bind_all(net, flows, inputs, outputs, refs):
@@ -726,18 +758,18 @@
 
 
 def permitted(query_block, key_block, start):
-    shape = (BLOCK, WIDE)
-    key = key_block * BLOCK + lax.broadcasted_iota(jnp.int32, shape, 0)
+    shape = (KEYS, WIDE)
+    key = key_block * KEYS + lax.broadcasted_iota(jnp.int32, shape, 0)
     query = query_block * WIDE + lax.broadcasted_iota(jnp.int32, shape, 1)
     return (key <= query) & (key >= start)
 
 
 def sweep(bounds_ref, query_block, step, carried):
-    diagonal = query_block * (WIDE // BLOCK)
+    diagonal = query_block * (WIDE // KEYS)
     first, whole = bounds_ref[0, query_block], bounds_ref[1, query_block]
     carried = lax.fori_loop(first, whole, functools.partial(step, True), carried)
     carried = lax.fori_loop(whole, diagonal, functools.partial(step, False), carried)
-    return lax.fori_loop(diagonal, diagonal + WIDE // BLOCK, functools.partial(step, True), carried)
+    return lax.fori_loop(diagonal, diagonal + WIDE // KEYS, functools.partial(step, True), carried)
 
 
 def fold(rows):
@@ -780,7 +812,7 @@
 
         def key_step(masked, key_block, held):
             top, total, mixed = held
-            there = columns_of(key_block)
+            there = pl.ds(pl.multiple_of(key_block * KEYS, KEYS), KEYS)
             scores = nn(key_rows[there, :], query)
             if masked:
                 allowed = permitted(query_block, key_block, start)
@@ -897,7 +929,7 @@
         grad_in_rows = grad_rows[here, :]
 
         def key_step(masked, key_block, query_grad):
-            there = columns_of(key_block)
+            there = pl.ds(pl.multiple_of(key_block * KEYS, KEYS), KEYS)
             scores = nn(key_rows[there, :], query)
             weights = jnp.exp(scores - total)
             if masked:
@@ -1024,7 +1056,7 @@
     part = FF // GROUP
     for step, block in enumerate(blocks):
         source = (plane + planes - step) % planes
-        weights[pl.ds(pl.multiple_of(source * span, span), span), :] = block[:, :D]
+        weights[pl.ds(pl.multiple_of(source * span, span), span), :] = block[...]
 
     def forward(chunk, carry):
         here = columns_of(chunk)
@@ -1112,7 +1144,7 @@
     def _():
         for step, block in enumerate(blocks):
             source = (plane + net.planes - step) % net.planes
-            weights[pl.ds(pl.multiple_of(source * span, span), span), :] = block[:, D:]
+            weights[pl.ds(pl.multiple_of(source * span, span), span), :] = block[...]
 
         def one(slot, carry):
             total = jnp.zeros((GROUP * 64, D), jnp.float32)
@@ -1137,7 +1169,7 @@
         out_shape=jax.ShapeDtypeStruct((slots, GROUP, 64, D), jnp.bfloat16),
         in_specs=[VMEM] * (1 + len(blocks)),
         out_specs=VMEM,
-        scratch_shapes=[pltpu.VMEM((D, blocks[0].shape[1] - D), jnp.bfloat16)],
+        scratch_shapes=[pltpu.VMEM((D, blocks[0].shape[1]), jnp.bfloat16)],
         cost_estimate=pl.CostEstimate(flops=10**9, bytes_accessed=6 * 2**20, transcendentals=0),
         name="input_partial",
     )(grads, *blocks)
@@ -1324,7 +1356,7 @@
             jax.ShapeDtypeStruct((GROUP,) + shares.shape[1:], low),
         ],
     )
-    late_own = jnp.concatenate([plane_cut, plane_shares], axis=2).reshape(GROUP * rows, -1)
+    late_own = plane_cut.reshape(GROUP * rows, 3 * part)
     late_blocks = [late_own] + [net.shift(late_own, step) for step in range(1, planes)]
 
     head_weights = all_columns[:, :, : 3 * HEAD_DIM].reshape(D, 3 * HEAD_DIM).T
@@ -1337,9 +1369,9 @@
     angles = inverse[:, None] * (index - start)[None, :]
     cosine, sine = jnp.cos(angles), jnp.sin(angles)
     start = start.astype(jnp.int32)
-    diagonal = jnp.arange(length // WIDE, dtype=jnp.int32) * (WIDE // BLOCK)
-    first = jnp.clip(start[::WIDE] // BLOCK, 0, diagonal)
-    first = jnp.stack([first, jnp.clip((start[WIDE - 1 :: WIDE] + BLOCK - 1) // BLOCK, first, diagonal)])
+    diagonal = jnp.arange(length // WIDE, dtype=jnp.int32) * (WIDE // KEYS)
+    first = jnp.clip(start[::WIDE] // KEYS, 0, diagonal)
+    first = jnp.stack([first, jnp.clip((start[WIDE - 1 :: WIDE] + KEYS - 1) // KEYS, first, diagonal)])
     start = start[None, :]
 
     qkv, mixed, total, packed = attend(net, first, all_tokens, head_weights, cosine, sine, start)
@@ -1389,12 +1421,12 @@
     ffn_update = 0.75 * ffn_block + 0.25 * moment_plane.reshape(GROUP * rows, 3 * part).astype(jnp.float32)
     ffn_update, ffn_block = ffn_update.astype(low), ffn_block.astype(low)
     middle_grad, folded, out_terms = before_attention(second_grad, middle, out_grad, mixed_tokens, out_full)
-    grad_parts, out_total, ffn_whole = exchange(
+    grad_parts, out_total, ffn_whole, out_whole = exchange(
         net,
         "mixed_grad_exchange",
         2,
         [
-            PlaneScatter(1, 1, (rows, D), (planes,), gathers=True),
+            PlaneScatter(1, 1, (rows, D), (planes,), moment=3, whole=3),
             Flow(0, 0, lambda i, j: combo_of(j), lambda i, j: i, lambda i, j: attends(j)),
         ]
         + [
@@ -1407,39 +1439,24 @@
             )
             for k in range(3)
         ],
-        [folded, out_terms.reshape(planes, 2, 2, 2, rows, D), ffn_update],
+        [folded, out_terms.reshape(planes, 2, 2, 2, rows, D), ffn_update, moment_out],
         [
             jax.ShapeDtypeStruct((count, HALF, 128), low),
             jax.ShapeDtypeStruct((planes, rows, D), jnp.float32),
             jax.ShapeDtypeStruct((planes, GROUP * rows, FF), low),
+            jax.ShapeDtypeStruct((planes, GROUP, rows, D), low),
         ],
     )
-    out_update = (0.75 * out_total + 0.25 * moment_out.astype(jnp.float32)).astype(low)
-
+    grad_parts, plane_shares = lax.optimization_barrier((grad_parts, plane_shares))
+    share_own = plane_shares.reshape(GROUP * rows, 10 * HEAD_DIM)
+    share_blocks = [share_own]
+    for step in range(1, planes):
+        hop = [(i, (i + GROUP * step) % count) for i in range(count)]
+        share_blocks.append(net.permute(share_own, [(i, j) for i, j in hop if j // GROUP < 4 and j // GROUP != SPARE]))
     grad_packed, head_grad = attend_back(
         net, first, all_tokens, qkv, mixed, total, cosine, sine, start, grad_parts
     )
     head_low = head_grad.astype(low)
-    out_update, grad_packed, head_low = lax.optimization_barrier((out_update, grad_packed, head_low))
-    (out_whole,) = exchange(
-        net,
-        "out_exchange",
-        4,
-        [
-            FanIn(
-                0,
-                0,
-                OWNERS[3] % GROUP,
-                lambda i, j: everything,
-                lambda i, j: everything + (i % GROUP,),
-                lambda i, j: j == OWNERS[3],
-            )
-        ],
-        [out_update],
-        [jax.ShapeDtypeStruct((planes, GROUP, rows, D), low)],
-        GROUP,
-    )
-    out_whole, grad_packed, head_low = lax.optimization_barrier((out_whole, grad_packed, head_low))
     (head_whole,) = exchange(
         net,
         "head_exchange",
@@ -1494,7 +1511,7 @@
         [row_shape, jax.ShapeDtypeStruct((slots, 3, GROUP, 96, 128), low)],
         meet=net.meet_attending,
     )
-    partial = input_partial(net, host_grads, late_blocks)
+    partial = input_partial(net, host_grads, share_blocks)
     attn_done, ffn_done = newton(
         net, head_whole, moment_whole.reshape(D, D), out_whole.reshape(D, D), ffn_whole.reshape(D, FF)
     )

time: 336 us -> 331 us (0.985)
  Pallas kernels: 285 us -> 275 us
  starting transfers between devices: 13 us -> 17 us
    pallas_call x8 -> x7, Pallas kernels: 183 us -> 173 us  [exchange(): pl.pallas_call(functools.partial(exchange_kernel, net, meet or (lambda me...]
    ppermute x6 -> x9, starting transfers between devices: 13 us -> 17 us  [permute(): lax.ppermute(values, ('head', 'blk'), [(place(i), place(j)) for i, j in p...]
  transfers between devices with their start and end apart: 6 -> 9, of which waited for: 2 -> 1; matrix products, arithmetic and copies ran while one was open for 2% -> 3% of each run, Pallas kernels for 27% -> 39%
where the time goes in v3:
time: 331 us; the launch traced here: 329 us
  Pallas kernels  275 us (83%)
  other arithmetic  17.4 us (5%)
  starting transfers between devices  17 us (5%)
  local copies, waits for them, and re-layouts  14.1 us (4%)
  waiting for transfers between devices  4.48 us (1%)
    pallas_call x7, Pallas kernels, exchange(): pl.pallas_call(functools.partial(exchange_kernel, net, meet or (lambda me...  173 us
    pallas_call x1, Pallas kernels, gather_tokens(): pl.pallas_call(functools.partial(gather_kernel, net, flows, len(extras)),...  38.5 us
    pallas_call x1, Pallas kernels, newton(): pl.pallas_call(functools.partial(newton_kernel, net), out_shape=[SQUARE,...  37.6 us
    ppermute x9, starting transfers between devices, permute(): lax.ppermute(values, ('head', 'blk'), [(place(i), place(j)) for i, j in p...  17 us
    pallas_call x1, Pallas kernels, feed_forward(): pl.pallas_call(functools.partial(feed_forward_kernel, net), out_shape=[ja...  9.1 us
  transfers between devices with their start and end apart: 9, of which 1 were waited for; matrix products, arithmetic and copies ran while one was open for 3% of the time, Pallas kernels for 39%

profile of v3, /device:TPU:18, one launch (start us, length us, event | category | flops | bytes accessed | tf_op | source)
XLA Modules:
  0.0 329.3 jit_solution(9106738131211461287)
XLA Ops:
  9.8 38.5 %gather_tokens.1 = (bf16[4,2,4,64,768]{4,3,2,1,0:T(8,128)(2,1)}, bf16[32,24,256]{2,1,0:T(8,128)(2,1)}, bf16[8,24,768]{2,1,0:T(8,128)(2,1)}, bf16[4,24,768]{2,1,0...) custom-call(bf16[2,64,768]{2,1,0:T(8,128)(2,1)} %multiply_convert_fusion.x_ref, ...), custom_call_target="tpu_custom_call" | custom-call | bytes 104857600 | tf_op jit(solution)/shard_map/gather_tokens/pallas_call | solution.py:723
  48.2 6.6 %collective-permute-start = (bf16[192,768]{1,0:T(8,128)(2,1)}, bf16[192,768]{1,0:T(8,128)(2,1)S(1)}, u32[]{:S(2)}, u32[]{:S(2)}) collective-permute-start(bf16[192,768]{1,0:T(8,128)(2,1)} %bitcast.123), channel_id=1, source_target_pairs={{0,4},{16,20},{1,5},{17,21},{2,6},{18,22},{3,7},{19,23},{4,8},{20,... | collective-permute-start | bytes 884744 | tf_op jit(solution)/shard_map/ppermute | solution.py:75
  54.9 2.0 collective-permute-start.1
  56.8 2.4 collective-permute-start.2
  60.9 1.9 copy.46
  62.8 1.8 multiply_sine_fusion
  65.1 3.2 attend.1
  68.4 43.9 %mixed_exchange.1 = (bf16[24,32,128]{2,1,0:T(8,128)(2,1)}, bf16[32,24,768]{2,1,0:T(8,128)(2,1)}, bf16[8,128,768]{2,1,0:T(8,128)(2,1)}, bf16[4,8,24,768]{3,2,1,0:T(8,128)(2,1)}) custom-call(bf16[32,32,128]{2,1,0:T(8,128)(2,1)} %get-tuple-element.65.refs_0_, bf16[4,24,768]{2,1,0:T(8,128)(2,1)} %copy-done.11, bf16[128,768]{1,0:T(8,128)(2,1)} %bitcast.104, ...), custom_call_target="tpu_custom_call" | custom-call | bytes 33030144 | tf_op jit(solution)/shard_map/mixed_exchange/pallas_call | solution.py:563
  112.3 2.8 after_attention.1
  115.1 14.5 %second_exchange.1 = bf16[8,128,768]{2,1,0:T(8,128)(2,1)} custom-call(bf16[128,768]{1,0:T(8,128)(2,1)} %get-tuple-element.73.refs_0_), custom_call_target="tpu_custom_call" | custom-call | bytes 12582912 | tf_op jit(solution)/shard_map/second_exchange/pallas_call | solution.py:563
  130.5 9.1 %feed_forward.1 = (bf16[1024,768]{1,0:T(8,128)(2,1)}, bf16[1024,768]{1,0:T(8,128)(2,1)}, bf16[192,768]{1,0:T(8,128)(2,1)}, bf16[192,768]{1,0:T(8,128)(2,1)}, bf1...) custom-call(bf16[1024,768]{1,0:T(8,128)(2,1)} %bitcast.87, bf16[1024,768]{1,0:T(8,128)(2,1)} %bitcast.120, ...), custom_call_target="tpu_custom_call" | custom-call | flops 3500000000 | bytes 10485760 | tf_op jit(solution)/shard_map/feed_forward/pallas_call | solution.py:1091
  139.6 2.0 collective-permute-start.3
  141.9 15.8 %second_grad_exchange.1.second_grad_ref = f32[128,768]{1,0:T(8,128)} custom-call(bf16[2,2,2,128,768]{4,3,2,1,0:T(8,128)(2,1)} %bitcast.88), custom_call_target="tpu_custom_call" | custom-call | bytes 3145728 | tf_op jit(solution)/shard_map/second_grad_exchange/pallas_call | solution.py:563
  157.7 3.8 %before_attention.1 = (f32[128,768]{1,0:T(8,128)}, bf16[24,32,128]{2,1,0:T(8,128)(2,1)}, bf16[768,768]{1,0:T(8,128)(2,1)}) custom-call(f32[128,768]{1,0:T(8,128)} %second_grad_exchange.1.second_grad_ref, f32[128,768]{1,0:T(8,128)} %get-tuple-element.69.middle_ref, bf16[128,768]{1,0:T(8,128)(2,1)} %bitcast.105, bf16[128,768]{1,0:T(8,128)(2,1)} %get-tuple-element.77.mixed_ref, ...), custom_call_target="tpu_custom_call" | custom-call | flops 400000000 | bytes 5242880 | tf_op jit(solution)/shard_map/before_attention/pallas_call | solution.py:1123
  161.5 4.5 %collective-permute-done.4 = bf16[192,768]{1,0:T(8,128)(2,1)S(1)} collective-permute-done((bf16[192,768]{1,0:T(8,128)(2,1)}, bf16[192,768]{1,0:T(8,128)(2,1)S(1)}, u32[]{:S(2)}, u32[]{:S(2)}) %collective-permute-start.4) | collective-permute-done | bytes 294944 | tf_op jit(solution)/shard_map/ppermute | solution.py:75
  167.0 39.1 %mixed_grad_exchange.1 = (bf16[32,32,128]{2,1,0:T(8,128)(2,1)}, f32[4,24,768]{2,1,0:T(8,128)}, bf16[4,192,2048]{2,1,0:T(8,128)(2,1)}, bf16[4,8,24,768]{3,2,1,0:T(8,128)(2,1)}) custom-call(bf16[24,32,128]{2,1,0:T(8,128)(2,1)} %get-tuple-element.78.refs_0_, bf16[4,2,2,2,24,768]{5,4,3,2,1,0:T(8,128)(2,1)} %bitcast.98, ...), custom_call_target="tpu_custom_call" | custom-call | bytes 39059456 | tf_op jit(solution)/shard_map/mixed_grad_exchange/pallas_call | solution.py:563
  210.1 3.6 %attend_back.1 = (bf16[32,96,128]{2,1,0:T(8,128)(2,1)}, f32[192,768]{1,0:T(8,128)}) custom-call(s32[2,4]{1,0:T(2,128)} %pad_add_fusion.refs_0_, bf16[4,2,4,64,768]{4,3,2,1,0:T(8,128)(2,1)} %get-tuple-element.64.refs_1_, bf16[192,2048]{1,0:T(8,128)(2,1)} %get-tuple-element.70.refs_2_, f32[64,2048]{1,0:T(8,128)} %get-tuple-element.71.refs_3_, ...), custom_call_target="tpu_custom_call" | custom-call | flops 4000000000 | bytes 12582912 | tf_op jit(solution)/shard_map/attend_back/pallas_call | solution.py:976
  213.7 1.8 convert_element_type.155
  215.5 1.7 head_exchange.1.head_ref
  217.2 37.6 %newton.1 = (bf16[768,768]{1,0:T(8,128)(2,1)}, bf16[768,2048]{1,0:T(8,128)(2,1)}) custom-call(bf16[24,64,768]{2,1,0:T(8,128)(2,1)} %head_exchange.1.head_ref, bf16[768,768]{1,0:T(8,128)(2,1)} %bitcast.121, bf16[768,768]{1,0:T(8,128)(2,1)} %bitcast.122, bf16[768,2048]{1,0:T(8,128)(2,1)} %bitcast.119), custom_call_target="tpu_custom_call" | custom-call | flops 24999999488 | bytes 8388608 | tf_op jit(solution)/shard_map/newton/pallas_call | solution.py:1295
  256.6 2.7 attending_exchange.1
  260.2 2.9 input_partial.1.refs_5_
  263.0 55.7 %step_exchange.1 = (bf16[24,24,256]{2,1,0:T(8,128)(2,1)}, bf16[8,24,768]{2,1,0:T(8,128)(2,1)}, bf16[4,24,768]{2,1,0:T(8,128)(2,1)}, bf16[3,24,2048]{2,1,0:T(8,12...) custom-call(bf16[32,24,256]{2,1,0:T(8,128)(2,1)} %pad.14.refs_0_, ...), custom_call_target="tpu_custom_call" | custom-call | bytes 17989632 | tf_op jit(solution)/shard_map/step_exchange/pallas_call | solution.py:563
  324.8 2.5 fusion.8
  (145 shorter events, 27.5 us)
Async XLA Ops:
  1.7 2.7 copy-start.31
  1.7 2.9 copy-start.4
  3.5 2.5 copy-start.5
  7.5 55.3 %copy-start.11 = (bf16[4,24,768]{2,1,0:T(8,128)(2,1)}, bf16[4,24,768]{2,1,0:T(8,128)(2,1)S(1)}, u32[]{:S(2)}) copy-start(bf16[4,24,768]{2,1,0:T(8,128)(2,1)S(1)} %convert_element_type.144.refs_1_) | copy-start | bytes 442372
  48.2 81.4 %collective-permute-start = (bf16[192,768]{1,0:T(8,128)(2,1)}, bf16[192,768]{1,0:T(8,128)(2,1)S(1)}, u32[]{:S(2)}, u32[]{:S(2)}) collective-permute-start(bf16[192,768]{1,0:T(8,128)(2,1)} %bitcast.123), channel_id=1, source_target_pairs={{0,4},{16,20},{1,5},{17,21},{2,6},{18,22},{3,7},{19,23},{4,8},{20,... | collective-permute-start | bytes 884744 | tf_op jit(solution)/shard_map/ppermute | solution.py:75
  54.9 74.8 %collective-permute-start.1 = (bf16[192,768]{1,0:T(8,128)(2,1)}, bf16[192,768]{1,0:T(8,128)(2,1)S(1)}, u32[]{:S(2)}, u32[]{:S(2)}) collective-permute-start(bf16[192,768]{1,0:T(8,128)(2,1)} %bitcast.124), channel_id=1, source_target_pairs={{0,8},{16,24},{1,9},{17,25},{2,10},{18,26},{3,11},{19,27},{4,12},{... | collective-permute-start | bytes 884744 | tf_op jit(solution)/shard_map/ppermute | solution.py:75
  56.8 72.8 %collective-permute-start.2 = (bf16[192,768]{1,0:T(8,128)(2,1)}, bf16[192,768]{1,0:T(8,128)(2,1)S(1)}, u32[]{:S(2)}, u32[]{:S(2)}) collective-permute-start(bf16[192,768]{1,0:T(8,128)(2,1)} %bitcast.125), channel_id=1, source_target_pairs={{0,12},{16,28},{1,13},{17,29},{2,14},{18,30},{3,15},{19,31},{4,0},... | collective-permute-start | bytes 884744 | tf_op jit(solution)/shard_map/ppermute | solution.py:75
  60.7 4.4 %copy-start.25 = (s32[2048]{0:T(1024)}, s32[2048]{0:T(1024)S(1)}, u32[]{:S(2)}) copy-start(s32[2048]{0:T(1024)S(1)} %get-tuple-element.129) | copy-start | bytes 24580
  130.5 11.3 %copy-start.15 = (bf16[8,24,768]{2,1,0:T(8,128)(2,1)S(1)}, bf16[8,24,768]{2,1,0:T(8,128)(2,1)}, u32[]{:S(2)}) copy-start(bf16[8,24,768]{2,1,0:T(8,128)(2,1)} %get-tuple-element.84) | copy-start | bytes 884740
  139.6 21.9 %collective-permute-start.5 = (bf16[192,768]{1,0:T(8,128)(2,1)}, bf16[192,768]{1,0:T(8,128)(2,1)S(1)}, u32[]{:S(2)}, u32[]{:S(2)}) collective-permute-start(bf16[192,768]{1,0:T(8,128)(2,1)} %get-tuple-element.83), channel_id=1, source_target_pairs={{0,12},{16,28},{1,13},{17,29},{2,14},{18,30},{3,15},{19,31},{4,0},... | collective-permute-start | bytes 884744 | tf_op jit(solution)/shard_map/ppermute | solution.py:75
  139.6 26.3 %collective-permute-start.4 = (bf16[192,768]{1,0:T(8,128)(2,1)}, bf16[192,768]{1,0:T(8,128)(2,1)S(1)}, u32[]{:S(2)}, u32[]{:S(2)}) collective-permute-start(bf16[192,768]{1,0:T(8,128)(2,1)} %get-tuple-element.82), channel_id=1, source_target_pairs={{0,8},{16,24},{1,9},{17,25},{2,10},{18,26},{3,11},{19,27},{4,12},{... | collective-permute-start | bytes 884744 | tf_op jit(solution)/shard_map/ppermute | solution.py:75
  139.6 26.3 %collective-permute-start.3 = (bf16[192,768]{1,0:T(8,128)(2,1)}, bf16[192,768]{1,0:T(8,128)(2,1)S(1)}, u32[]{:S(2)}, u32[]{:S(2)}) collective-permute-start(bf16[192,768]{1,0:T(8,128)(2,1)} %get-tuple-element.81), channel_id=1, source_target_pairs={{0,4},{16,20},{1,5},{17,21},{2,6},{18,22},{3,7},{19,23},{4,8},{20,... | collective-permute-start | bytes 884744 | tf_op jit(solution)/shard_map/ppermute | solution.py:75
  157.7 8.3 %copy-start.14 = (bf16[192,768]{1,0:T(8,128)(2,1)S(1)}, bf16[192,768]{1,0:T(8,128)(2,1)}, u32[]{:S(2)}) copy-start(bf16[192,768]{1,0:T(8,128)(2,1)} %get-tuple-element.80) | copy-start | bytes 884740
  166.0 40.2 %copy-start.19 = (bf16[8,24,640]{2,1,0:T(8,128)(2,1)S(1)}, bf16[8,24,640]{2,1,0:T(8,128)(2,1)}, u32[]{:S(2)}) copy-start(bf16[8,24,640]{2,1,0:T(8,128)(2,1)} %get-tuple-element.100) | copy-start | bytes 737284
  206.1 53.2 %collective-permute-start.6 = (bf16[192,640]{1,0:T(8,128)(2,1)S(1)}, bf16[192,640]{1,0:T(8,128)(2,1)S(1)}, u32[]{:S(2)}, u32[]{:S(2)}) collective-permute-start(bf16[192,640]{1,0:T(8,128)(2,1)S(1)} %bitcast.111), channel_id=1, source_target_pairs={{0,4},{16,20},{1,5},{17,21},{2,6},{18,22},{3,7},{19,23},{8,12},{24... | collective-permute-start | bytes 737288 | tf_op jit(solution)/shard_map/ppermute | solution.py:75
  207.5 51.9 %collective-permute-start.7 = (bf16[192,640]{1,0:T(8,128)(2,1)S(1)}, bf16[192,640]{1,0:T(8,128)(2,1)S(1)}, u32[]{:S(2)}, u32[]{:S(2)}) collective-permute-start(bf16[192,640]{1,0:T(8,128)(2,1)S(1)} %bitcast.112), channel_id=1, source_target_pairs={{4,12},{20,28},{5,13},{21,29},{6,14},{22,30},{7,15},{23,31},{8,0},... | collective-permute-start | bytes 737288 | tf_op jit(solution)/shard_map/ppermute | solution.py:75
  208.8 50.6 %collective-permute-start.8 = (bf16[192,640]{1,0:T(8,128)(2,1)S(1)}, bf16[192,640]{1,0:T(8,128)(2,1)S(1)}, u32[]{:S(2)}, u32[]{:S(2)}) collective-permute-start(bf16[192,640]{1,0:T(8,128)(2,1)S(1)} %bitcast.113), channel_id=1, source_target_pairs={{0,12},{16,28},{1,13},{17,29},{2,14},{18,30},{3,15},{19,31},{4,0},... | collective-permute-start | bytes 737288 | tf_op jit(solution)/shard_map/ppermute | solution.py:75
  217.2 37.7 %copy-start.3 = (bf16[192,768]{1,0:T(8,128)(2,1)S(1)}, bf16[192,768]{1,0:T(8,128)(2,1)}, u32[]{:S(2)}) copy-start(bf16[192,768]{1,0:T(8,128)(2,1)} %convert_element_type.155) | copy-start | bytes 884740
  318.8 2.8 copy-start.24
  318.8 2.8 copy-start.16
  318.8 2.8 copy-start.17
  324.8 2.5 copy-start.6
  324.8 2.5 copy-start.8
  324.8 2.5 copy-start.10
  (17 other events, 24.7 us)

commit v4 on v3

--- a/solution.py
+++ b/solution.py
@@ -788,7 +788,7 @@
 
 def attend_body(first_ref, x_ref, w_ref, cos_ref, sin_ref, start_ref, qkv_ref, mixed_ref, total_ref, packed_ref, key_rows):
     blocks = qkv_ref.shape[1] // BLOCK
-    weights = w_ref[...]
+    weights = w_ref[...].astype(jnp.float32).T[: 3 * HEAD_DIM].astype(jnp.bfloat16)
 
     def project(chunk, carry):
         tokens = x_ref[chunk // 2, chunk % 2].reshape(BLOCK, D)
@@ -1017,6 +1017,79 @@
     return inverse * (gradient - mean_of(gradient) - normed * mean_of(gradient * normed))
 
 
+def prepare_kernel(
+    tokens_ref,
+    documents_ref,
+    attn_ref,
+    ffn_ref,
+    attn_moment_ref,
+    ffn_moment_ref,
+    normed_ref,
+    columns_ref,
+    shares_ref,
+    cut_ref,
+    moment_cut_ref,
+    out_ref,
+    moment_ref,
+    out_moment_ref,
+):
+    low = jnp.bfloat16
+    normed_ref[...] = layer_norm(tokens_ref[...].astype(jnp.float32)).astype(low)
+    documents = documents_ref[...]
+    lane = lax.broadcasted_iota(jnp.int32, (1, HEAD_DIM), 1)
+    tail = jnp.zeros((1, HEAD_DIM), jnp.float32)
+    for document in range(DOCS):
+        counts = jnp.sum((documents == document).astype(jnp.float32), axis=1, keepdims=True)
+        for micro in range(documents.shape[0]):
+            tail = jnp.where(lane == micro * DOCS + document, counts[micro : micro + 1], tail)
+    rows = attn_ref.shape[1]
+    tail = jnp.broadcast_to(tail, (rows, HEAD_DIM))
+    empty = jnp.zeros((rows, HEAD_DIM), jnp.float32)
+    for head in range(HEADS):
+        here = slice(HEAD_DIM * head, HEAD_DIM * head + HEAD_DIM)
+        three = [attn_ref[matrix, :, here] for matrix in range(3)]
+        columns_ref[head] = jnp.concatenate(three + [tail], axis=1).astype(low)
+    for share in range(4):
+        pieces = []
+        for head in range(share, HEADS, 4):
+            here = slice(HEAD_DIM * head, HEAD_DIM * head + HEAD_DIM)
+            pieces += [attn_ref[matrix, :, here] for matrix in range(3)]
+        shares_ref[share] = jnp.concatenate(pieces + [empty], axis=1).astype(low)
+    part = FF // GROUP
+    for place in range(GROUP):
+        here = slice(part * place, part * place + part)
+        for matrix in range(3):
+            there = slice(part * matrix, part * matrix + part)
+            cut_ref[place, :, there] = ffn_ref[matrix, :, here].astype(low)
+            moment_cut_ref[place, :, there] = ffn_moment_ref[matrix, :, here].astype(low)
+    out_ref[0] = attn_ref[3].astype(low)
+    moment_ref[...] = attn_moment_ref[...].astype(low)
+    out_moment_ref[0] = attn_moment_ref[3].astype(low)
+
+
+def prepare(tokens, documents, attn, ffn, attn_moment, ffn_moment):
+    rows = attn.shape[1]
+    low = jnp.bfloat16
+    cut = jax.ShapeDtypeStruct((GROUP, rows, 3 * FF // GROUP), low)
+    return pl.pallas_call(
+        prepare_kernel,
+        out_shape=[
+            jax.ShapeDtypeStruct(tokens.shape, low),
+            jax.ShapeDtypeStruct((HEADS, rows, 4 * HEAD_DIM), low),
+            jax.ShapeDtypeStruct((4, rows, 10 * HEAD_DIM), low),
+            cut,
+            cut,
+            jax.ShapeDtypeStruct((1, rows, D), low),
+            jax.ShapeDtypeStruct((4, rows, D), low),
+            jax.ShapeDtypeStruct((1, rows, D), low),
+        ],
+        in_specs=[VMEM] * 6,
+        out_specs=[VMEM] * 8,
+        cost_estimate=pl.CostEstimate(flops=10**7, bytes_accessed=4 * 2**20, transcendentals=0),
+        name="prepare",
+    )(tokens, documents, attn, ffn, attn_moment, ffn_moment)
+
+
 def after_kernel(parts_ref, tokens_ref, out_ref, mixed_ref, middle_ref, second_ref):
     for micro in range(2):
         here = slice(64 * micro, 64 * micro + 64)
@@ -1316,23 +1389,12 @@
     low = jnp.bfloat16
     everything = (slice(None),)
 
-    attn_low = attn_weight.astype(low)
-    ffn_low = ffn_weight.astype(low)
-
-    def cut_up(values):
-        return values.reshape(3, rows, GROUP, part).transpose(2, 1, 0, 3).reshape(GROUP, rows, 3 * part)
-
-    cut = cut_up(ffn_low)
+    own_tokens = tokens.reshape(both, width)
     out_grad = cotangent.reshape(both, width)
-    hidden = tokens.astype(jnp.float32).reshape(both, width)
-    normed = layer_norm(hidden).astype(low)
-    counts = jnp.sum((doc_ids[:, :, None] == jnp.arange(DOCS)[None, None, :]).astype(jnp.float32), axis=1)
-    tail = jnp.pad(counts.reshape(-1).astype(low), (0, HEAD_DIM - micro_count * DOCS))
-    columns = attn_low[:3].reshape(3, rows, HEADS, HEAD_DIM).transpose(2, 1, 0, 3).reshape(HEADS, rows, 3 * HEAD_DIM)
-    shares = columns.reshape(3, 4, rows, 3 * HEAD_DIM).transpose(1, 2, 0, 3).reshape(4, rows, 9 * HEAD_DIM)
-    shares = jnp.pad(shares, ((0, 0), (0, 0), (0, HEAD_DIM)))
-    columns = jnp.concatenate([columns, jnp.broadcast_to(tail, (HEADS, rows, HEAD_DIM))], axis=2)
-    moment_low = attn_moment.astype(low)
+    hidden = own_tokens.astype(jnp.float32)
+    normed, columns, shares, cut, moment_cut, out_low, moment_low, out_moment = prepare(
+        own_tokens, doc_ids, attn_weight, ffn_weight, attn_moment, ffn_moment
+    )
     all_tokens, all_columns, plane_cut, plane_out, moment_plane, moment_out, plane_shares = gather_tokens(
         net,
         0,
@@ -1347,7 +1409,7 @@
             Flow(2, 2, lambda i, j: j % GROUP, lambda i, j: i % GROUP, size=GROUP),
             Flow(4, 4, lambda i, j: j % 4, lambda i, j: i % GROUP, size=GROUP),
         ],
-        [cut, attn_low[3:], cut_up(ffn_moment.astype(low)), moment_low[3:], shares],
+        [cut, out_low, moment_cut, out_moment, shares],
         [
             jax.ShapeDtypeStruct(cut.shape, low),
             jax.ShapeDtypeStruct((planes, rows, D), low),
@@ -1359,7 +1421,7 @@
     late_own = plane_cut.reshape(GROUP * rows, 3 * part)
     late_blocks = [late_own] + [net.shift(late_own, step) for step in range(1, planes)]
 
-    head_weights = all_columns[:, :, : 3 * HEAD_DIM].reshape(D, 3 * HEAD_DIM).T
+    head_weights = all_columns.reshape(D, 4 * HEAD_DIM)
     every_count = jnp.sum(all_columns[:, 0, 3 * HEAD_DIM :].astype(jnp.float32), axis=0)
     own_count = lax.dynamic_slice_in_dim(every_count, x_bit * DOCS, DOCS, 0)
     starts = jnp.cumsum(own_count) - own_count
@@ -1392,7 +1454,6 @@
     )
     plane_out_grad = plane_out_grad.reshape(GROUP * both, width)
     out_full = out_full.reshape(D, D)
-    own_tokens = tokens.reshape(both, width)
     mixed_tokens, middle, second = after_attention(mixed_parts, own_tokens, out_full)
     (plane_second,) = exchange(
         net,

time: 331 us -> 318 us (0.961)
  local copies, waits for them, and re-layouts: 14.1 us -> 5.48 us
    reshape x8 -> x0, local copies, waits for them, and re-layouts: 5.04 us -> none  [the longest x4 2.61 us: cut_up(): values.reshape(3, rows, GROUP, part).transpose(2, 1, 0, 3)]
    pallas_call x7, Pallas kernels: 173 us -> 170 us  [exchange(): pl.pallas_call(functools.partial(exchange_kernel, net, meet or (lambda me...]
  transfers between devices with their start and end apart: 9 -> 9, of which waited for: 1 -> 1; matrix products, arithmetic and copies ran while one was open for 3% -> 2% of each run, Pallas kernels for 39% -> 40%
where the time goes in v4:
time: 318 us; the launch traced here: 317 us
  Pallas kernels  275 us (86%)
  starting transfers between devices  16.7 us (5%)
  other arithmetic  14.4 us (5%)
  local copies, waits for them, and re-layouts  5.48 us (2%)
  waiting for transfers between devices  4.49 us (1%)
    pallas_call x7, Pallas kernels, exchange(): pl.pallas_call(functools.partial(exchange_kernel, net, meet or (lambda me...  170 us
    pallas_call x1, Pallas kernels, gather_tokens(): pl.pallas_call(functools.partial(gather_kernel, net, flows, len(extras)),...  38.8 us
    pallas_call x1, Pallas kernels, newton(): pl.pallas_call(functools.partial(newton_kernel, net), out_shape=[SQUARE,...  37.5 us
    ppermute x9, starting transfers between devices, permute(): lax.ppermute(values, ('head', 'blk'), [(place(i), place(j)) for i, j in p...  16.7 us
    pallas_call x1, Pallas kernels, feed_forward(): pl.pallas_call(functools.partial(feed_forward_kernel, net), out_shape=[ja...  9.1 us
  transfers between devices with their start and end apart: 9, of which 1 were waited for; matrix products, arithmetic and copies ran while one was open for 2% of the time, Pallas kernels for 40%

profile of v4, /device:TPU:18, one launch (start us, length us, event | category | flops | bytes accessed | tf_op | source)
XLA Modules:
  0.0 316.8 jit_solution(5740511459096315188)
XLA Ops:
  0.7 2.8 prepare.1
  3.4 38.8 %gather_tokens.1 = (bf16[4,2,4,64,768]{4,3,2,1,0:T(8,128)(2,1)}, bf16[32,24,256]{2,1,0:T(8,128)(2,1)}, bf16[8,24,768]{2,1,0:T(8,128)(2,1)}, bf16[4,24,768]{2,1,0...) custom-call(bf16[2,64,768]{2,1,0:T(8,128)(2,1)} %bitcast.82, ...), custom_call_target="tpu_custom_call" | custom-call | bytes 104857600 | tf_op jit(solution)/shard_map/gather_tokens/pallas_call | solution.py:723
  42.3 6.6 %collective-permute-start = (bf16[192,768]{1,0:T(8,128)(2,1)}, bf16[192,768]{1,0:T(8,128)(2,1)S(1)}, u32[]{:S(2)}, u32[]{:S(2)}) collective-permute-start(bf16[192,768]{1,0:T(8,128)(2,1)} %bitcast.92), channel_id=1, source_target_pairs={{0,4},{16,20},{1,5},{17,21},{2,6},{18,22},{3,7},{19,23},{4,8},{20,... | collective-permute-start | bytes 884744 | tf_op jit(solution)/shard_map/ppermute | solution.py:75
  48.9 1.9 collective-permute-start.1
  50.8 2.2 collective-permute-start.2
  55.3 1.8 multiply_sine_fusion
  57.1 3.3 %attend.1 = (bf16[192,2048]{1,0:T(8,128)(2,1)}, f32[64,2048]{1,0:T(8,128)}, f32[1,2048]{1,0:T(1,128)}, bf16[32,32,128]{2,1,0:T(8,128)(2,1)}) custom-call(s32[2,4]{1,0:T(2,128)} %pad_add_fusion.refs_0_, bf16[4,2,4,64,768]{4,3,2,1,0:T(8,128)(2,1)} %get-tuple-element.79.refs_1_, bf16[768,256]{1,0:T(8,128)(2,1)} %bitcast.87, ...), custom_call_target="tpu_custom_call" | custom-call | flops 2000000000 | bytes 8388608 | tf_op jit(solution)/shard_map/attend/pallas_call | solution.py:854
  60.4 41.9 %mixed_exchange.1 = (bf16[24,32,128]{2,1,0:T(8,128)(2,1)}, bf16[32,24,768]{2,1,0:T(8,128)(2,1)}, bf16[8,128,768]{2,1,0:T(8,128)(2,1)}, bf16[4,8,24,768]{3,2,1,0:T(8,128)(2,1)}) custom-call(bf16[32,32,128]{2,1,0:T(8,128)(2,1)} %get-tuple-element.80.refs_0_, bf16[4,24,768]{2,1,0:T(8,128)(2,1)} %get-tuple-element.81.refs_1_, bf16[128,768]{1,0:T(8,128)(2,1)} %bitcast.74, ...), custom_call_target="tpu_custom_call" | custom-call | bytes 33030144 | tf_op jit(solution)/shard_map/mixed_exchange/pallas_call | solution.py:563
  102.4 2.8 after_attention.1
  105.2 14.5 %second_exchange.1 = bf16[8,128,768]{2,1,0:T(8,128)(2,1)} custom-call(bf16[128,768]{1,0:T(8,128)(2,1)} %get-tuple-element.89.refs_0_), custom_call_target="tpu_custom_call" | custom-call | bytes 12582912 | tf_op jit(solution)/shard_map/second_exchange/pallas_call | solution.py:563
  120.9 9.1 %feed_forward.1 = (bf16[1024,768]{1,0:T(8,128)(2,1)}, bf16[1024,768]{1,0:T(8,128)(2,1)}, bf16[192,768]{1,0:T(8,128)(2,1)}, bf16[192,768]{1,0:T(8,128)(2,1)}, bf1...) custom-call(bf16[1024,768]{1,0:T(8,128)(2,1)} %bitcast.64, bf16[1024,768]{1,0:T(8,128)(2,1)} %bitcast.89, ...), custom_call_target="tpu_custom_call" | custom-call | flops 3500000000 | bytes 10485760 | tf_op jit(solution)/shard_map/feed_forward/pallas_call | solution.py:1164
  130.0 2.0 collective-permute-start.3
  132.2 15.8 %second_grad_exchange.1.second_grad_ref = f32[128,768]{1,0:T(8,128)} custom-call(bf16[2,2,2,128,768]{4,3,2,1,0:T(8,128)(2,1)} %bitcast.65), custom_call_target="tpu_custom_call" | custom-call | bytes 3145728 | tf_op jit(solution)/shard_map/second_grad_exchange/pallas_call | solution.py:563
  148.1 3.8 %before_attention.1 = (f32[128,768]{1,0:T(8,128)}, bf16[24,32,128]{2,1,0:T(8,128)(2,1)}, bf16[768,768]{1,0:T(8,128)(2,1)}) custom-call(f32[128,768]{1,0:T(8,128)} %second_grad_exchange.1.second_grad_ref, f32[128,768]{1,0:T(8,128)} %get-tuple-element.85.middle_ref, bf16[128,768]{1,0:T(8,128)(2,1)} %bitcast.75, bf16[128,768]{1,0:T(8,128)(2,1)} %get-tuple-element.93.mixed_ref, ...), custom_call_target="tpu_custom_call" | custom-call | flops 400000000 | bytes 5242880 | tf_op jit(solution)/shard_map/before_attention/pallas_call | solution.py:1196
  151.9 4.5 %collective-permute-done.4 = bf16[192,768]{1,0:T(8,128)(2,1)S(1)} collective-permute-done((bf16[192,768]{1,0:T(8,128)(2,1)}, bf16[192,768]{1,0:T(8,128)(2,1)S(1)}, u32[]{:S(2)}, u32[]{:S(2)}) %collective-permute-start.4) | collective-permute-done | bytes 294944 | tf_op jit(solution)/shard_map/ppermute | solution.py:75
  157.4 39.7 %mixed_grad_exchange.1 = (bf16[32,32,128]{2,1,0:T(8,128)(2,1)}, f32[4,24,768]{2,1,0:T(8,128)}, bf16[4,192,2048]{2,1,0:T(8,128)(2,1)}, bf16[4,8,24,768]{3,2,1,0:T(8,128)(2,1)}) custom-call(bf16[24,32,128]{2,1,0:T(8,128)(2,1)} %get-tuple-element.94.refs_0_, bf16[4,2,2,2,24,768]{5,4,3,2,1,0:T(8,128)(2,1)} %bitcast.71, ...), custom_call_target="tpu_custom_call" | custom-call | bytes 39059456 | tf_op jit(solution)/shard_map/mixed_grad_exchange/pallas_call | solution.py:563
  201.0 3.6 %attend_back.1 = (bf16[32,96,128]{2,1,0:T(8,128)(2,1)}, f32[192,768]{1,0:T(8,128)}) custom-call(s32[2,4]{1,0:T(2,128)} %pad_add_fusion.refs_0_, bf16[4,2,4,64,768]{4,3,2,1,0:T(8,128)(2,1)} %get-tuple-element.79.refs_1_, bf16[192,2048]{1,0:T(8,128)(2,1)} %get-tuple-element.86.refs_2_, f32[64,2048]{1,0:T(8,128)} %get-tuple-element.87.refs_3_, ...), custom_call_target="tpu_custom_call" | custom-call | flops 4000000000 | bytes 12582912 | tf_op jit(solution)/shard_map/attend_back/pallas_call | solution.py:976
  204.6 1.8 convert_element_type.122
  206.4 1.7 head_exchange.1.head_ref
  208.2 37.5 %newton.1 = (bf16[768,768]{1,0:T(8,128)(2,1)}, bf16[768,2048]{1,0:T(8,128)(2,1)}) custom-call(bf16[24,64,768]{2,1,0:T(8,128)(2,1)} %head_exchange.1.head_ref, bf16[768,768]{1,0:T(8,128)(2,1)} %bitcast.90, bf16[768,768]{1,0:T(8,128)(2,1)} %bitcast.91, bf16[768,2048]{1,0:T(8,128)(2,1)} %bitcast.88), custom_call_target="tpu_custom_call" | custom-call | flops 24999999488 | bytes 8388608 | tf_op jit(solution)/shard_map/newton/pallas_call | solution.py:1368
  247.4 2.7 attending_exchange.1
  250.9 2.8 input_partial.1.refs_5_
  253.7 53.6 %step_exchange.1 = (bf16[24,24,256]{2,1,0:T(8,128)(2,1)}, bf16[8,24,768]{2,1,0:T(8,128)(2,1)}, bf16[4,24,768]{2,1,0:T(8,128)(2,1)}, bf16[3,24,2048]{2,1,0:T(8,12...) custom-call(bf16[32,24,256]{2,1,0:T(8,128)(2,1)} %pad.4.refs_0_, ...), custom_call_target="tpu_custom_call" | custom-call | bytes 17989632 | tf_op jit(solution)/shard_map/step_exchange/pallas_call | solution.py:563
  312.5 2.3 fusion.11
  (116 shorter events, 17.9 us)
Async XLA Ops:
  0.6 54.0 %copy-start = (bf16[2,64,768]{2,1,0:T(8,128)(2,1)S(1)}, bf16[2,64,768]{2,1,0:T(8,128)(2,1)}, u32[]{:S(2)}) copy-start(bf16[2,64,768]{2,1,0:T(8,128)(2,1)} %param.8) | copy-start | bytes 589828
  42.3 77.7 %collective-permute-start = (bf16[192,768]{1,0:T(8,128)(2,1)}, bf16[192,768]{1,0:T(8,128)(2,1)S(1)}, u32[]{:S(2)}, u32[]{:S(2)}) collective-permute-start(bf16[192,768]{1,0:T(8,128)(2,1)} %bitcast.92), channel_id=1, source_target_pairs={{0,4},{16,20},{1,5},{17,21},{2,6},{18,22},{3,7},{19,23},{4,8},{20,... | collective-permute-start | bytes 884744 | tf_op jit(solution)/shard_map/ppermute | solution.py:75
  48.9 71.1 %collective-permute-start.1 = (bf16[192,768]{1,0:T(8,128)(2,1)}, bf16[192,768]{1,0:T(8,128)(2,1)S(1)}, u32[]{:S(2)}, u32[]{:S(2)}) collective-permute-start(bf16[192,768]{1,0:T(8,128)(2,1)} %bitcast.93), channel_id=1, source_target_pairs={{0,8},{16,24},{1,9},{17,25},{2,10},{18,26},{3,11},{19,27},{4,12},{... | collective-permute-start | bytes 884744 | tf_op jit(solution)/shard_map/ppermute | solution.py:75
  50.8 69.2 %collective-permute-start.2 = (bf16[192,768]{1,0:T(8,128)(2,1)}, bf16[192,768]{1,0:T(8,128)(2,1)S(1)}, u32[]{:S(2)}, u32[]{:S(2)}) collective-permute-start(bf16[192,768]{1,0:T(8,128)(2,1)} %bitcast.94), channel_id=1, source_target_pairs={{0,12},{16,28},{1,13},{17,29},{2,14},{18,30},{3,15},{19,31},{4,0},... | collective-permute-start | bytes 884744 | tf_op jit(solution)/shard_map/ppermute | solution.py:75
  54.5 2.7 copy-start.24
  102.4 17.4 %copy-start.1 = (bf16[2,64,768]{2,1,0:T(8,128)(2,1)S(1)}, bf16[2,64,768]{2,1,0:T(8,128)(2,1)}, u32[]{:S(2)}) copy-start(bf16[2,64,768]{2,1,0:T(8,128)(2,1)} %param.8) | copy-start | bytes 589828
  120.9 11.3 %copy-start.13 = (bf16[8,24,768]{2,1,0:T(8,128)(2,1)S(1)}, bf16[8,24,768]{2,1,0:T(8,128)(2,1)}, u32[]{:S(2)}) copy-start(bf16[8,24,768]{2,1,0:T(8,128)(2,1)} %get-tuple-element.100) | copy-start | bytes 884740
  130.0 21.9 %collective-permute-start.5 = (bf16[192,768]{1,0:T(8,128)(2,1)}, bf16[192,768]{1,0:T(8,128)(2,1)S(1)}, u32[]{:S(2)}, u32[]{:S(2)}) collective-permute-start(bf16[192,768]{1,0:T(8,128)(2,1)} %get-tuple-element.99), channel_id=1, source_target_pairs={{0,12},{16,28},{1,13},{17,29},{2,14},{18,30},{3,15},{19,31},{4,0},... | collective-permute-start | bytes 884744 | tf_op jit(solution)/shard_map/ppermute | solution.py:75
  130.0 26.4 %collective-permute-start.4 = (bf16[192,768]{1,0:T(8,128)(2,1)}, bf16[192,768]{1,0:T(8,128)(2,1)S(1)}, u32[]{:S(2)}, u32[]{:S(2)}) collective-permute-start(bf16[192,768]{1,0:T(8,128)(2,1)} %get-tuple-element.98), channel_id=1, source_target_pairs={{0,8},{16,24},{1,9},{17,25},{2,10},{18,26},{3,11},{19,27},{4,12},{... | collective-permute-start | bytes 884744 | tf_op jit(solution)/shard_map/ppermute | solution.py:75
  130.0 26.4 %collective-permute-start.3 = (bf16[192,768]{1,0:T(8,128)(2,1)}, bf16[192,768]{1,0:T(8,128)(2,1)S(1)}, u32[]{:S(2)}, u32[]{:S(2)}) collective-permute-start(bf16[192,768]{1,0:T(8,128)(2,1)} %get-tuple-element.97), channel_id=1, source_target_pairs={{0,4},{16,20},{1,5},{17,21},{2,6},{18,22},{3,7},{19,23},{4,8},{20,... | collective-permute-start | bytes 884744 | tf_op jit(solution)/shard_map/ppermute | solution.py:75
  148.1 8.3 %copy-start.12 = (bf16[192,768]{1,0:T(8,128)(2,1)S(1)}, bf16[192,768]{1,0:T(8,128)(2,1)}, u32[]{:S(2)}) copy-start(bf16[192,768]{1,0:T(8,128)(2,1)} %get-tuple-element.96) | copy-start | bytes 884740
  156.4 40.7 %copy-start.18 = (bf16[8,24,640]{2,1,0:T(8,128)(2,1)S(1)}, bf16[8,24,640]{2,1,0:T(8,128)(2,1)}, u32[]{:S(2)}) copy-start(bf16[8,24,640]{2,1,0:T(8,128)(2,1)} %get-tuple-element.116) | copy-start | bytes 737284
  197.1 53.0 %collective-permute-start.6 = (bf16[192,640]{1,0:T(8,128)(2,1)S(1)}, bf16[192,640]{1,0:T(8,128)(2,1)S(1)}, u32[]{:S(2)}, u32[]{:S(2)}) collective-permute-start(bf16[192,640]{1,0:T(8,128)(2,1)S(1)} %bitcast.78), channel_id=1, source_target_pairs={{0,4},{16,20},{1,5},{17,21},{2,6},{18,22},{3,7},{19,23},{8,12},{24... | collective-permute-start | bytes 737288 | tf_op jit(solution)/shard_map/ppermute | solution.py:75
  198.4 51.7 %collective-permute-start.7 = (bf16[192,640]{1,0:T(8,128)(2,1)S(1)}, bf16[192,640]{1,0:T(8,128)(2,1)S(1)}, u32[]{:S(2)}, u32[]{:S(2)}) collective-permute-start(bf16[192,640]{1,0:T(8,128)(2,1)S(1)} %bitcast.79), channel_id=1, source_target_pairs={{4,12},{20,28},{5,13},{21,29},{6,14},{22,30},{7,15},{23,31},{8,0},... | collective-permute-start | bytes 737288 | tf_op jit(solution)/shard_map/ppermute | solution.py:75
  199.7 50.4 %collective-permute-start.8 = (bf16[192,640]{1,0:T(8,128)(2,1)S(1)}, bf16[192,640]{1,0:T(8,128)(2,1)S(1)}, u32[]{:S(2)}, u32[]{:S(2)}) collective-permute-start(bf16[192,640]{1,0:T(8,128)(2,1)S(1)} %bitcast.80), channel_id=1, source_target_pairs={{0,12},{16,28},{1,13},{17,29},{2,14},{18,30},{3,15},{19,31},{4,0},... | collective-permute-start | bytes 737288 | tf_op jit(solution)/shard_map/ppermute | solution.py:75
  208.2 37.5 %copy-start.3 = (bf16[192,768]{1,0:T(8,128)(2,1)S(1)}, bf16[192,768]{1,0:T(8,128)(2,1)}, u32[]{:S(2)}) copy-start(bf16[192,768]{1,0:T(8,128)(2,1)} %convert_element_type.122) | copy-start | bytes 884740
  208.2 37.7 %copy-start.16 = (f32[4,24,768]{2,1,0:T(8,128)S(1)}, f32[4,24,768]{2,1,0:T(8,128)}, u32[]{:S(2)}) copy-start(f32[4,24,768]{2,1,0:T(8,128)} %get-tuple-element.120) | copy-start | bytes 884740
  307.4 2.8 copy-start.23
  307.4 2.8 copy-start.14
  307.4 2.8 copy-start.15
  312.1 2.8 copy-start.6
  312.5 2.3 copy-start.9
  312.5 2.3 copy-start.22
  312.5 2.3 copy-start.25
  (15 other events, 17.3 us)

commit v5 on v4

--- a/solution.py
+++ b/solution.py
@@ -884,7 +884,8 @@
     start_ref,
     grad_ref,
     packed_ref,
-    weight_ref,
+    low_ref,
+    turned_ref,
     query_rows,
     key_rows,
     value_rows,
@@ -894,6 +895,7 @@
     key_grad,
     value_grad,
     all_grad,
+    weight_ref,
 ):
     blocks = qkv_ref.shape[1] // BLOCK
     parts = BLOCK // 64
@@ -967,6 +969,9 @@
         return carry
 
     lax.fori_loop(0, blocks, close, 0)
+    low_ref[...] = weight_ref[...].astype(jnp.bfloat16)
+    turned_ref[:, : 3 * HEAD_DIM] = weight_ref[...].T.astype(jnp.bfloat16)
+    turned_ref[:, 3 * HEAD_DIM :] = jnp.zeros((D, HEAD_DIM), jnp.bfloat16)
 
 
 def attend_back(net, first, tokens, qkv, mixed, total, cosine, sine, start, grad):
@@ -977,10 +982,11 @@
         functools.partial(attend_back_kernel, net),
         out_shape=[
             jax.ShapeDtypeStruct((net.count, 96, 128), jnp.bfloat16),
-            jax.ShapeDtypeStruct((3 * HEAD_DIM, D), jnp.float32),
+            jax.ShapeDtypeStruct((3 * HEAD_DIM, D), jnp.bfloat16),
+            jax.ShapeDtypeStruct((D, 4 * HEAD_DIM), jnp.bfloat16),
         ],
         in_specs=[SMEM] + [VMEM] * 8,
-        out_specs=[VMEM] * 2,
+        out_specs=[VMEM] * 3,
         scratch_shapes=[
             rows,
             rows,
@@ -991,6 +997,7 @@
             sums,
             sums,
             pltpu.VMEM((3 * HEAD_DIM, length), jnp.bfloat16),
+            pltpu.VMEM((3 * HEAD_DIM, D), jnp.float32),
         ],
         cost_estimate=pl.CostEstimate(flops=4 * 10**9, bytes_accessed=12 * 2**20, transcendentals=2 * 10**6),
         name="attend_back",
@@ -1514,10 +1521,9 @@
     for step in range(1, planes):
         hop = [(i, (i + GROUP * step) % count) for i in range(count)]
         share_blocks.append(net.permute(share_own, [(i, j) for i, j in hop if j // GROUP < 4 and j // GROUP != SPARE]))
-    grad_packed, head_grad = attend_back(
+    grad_packed, head_low, head_rows = attend_back(
         net, first, all_tokens, qkv, mixed, total, cosine, sine, start, grad_parts
     )
-    head_low = head_grad.astype(low)
     (head_whole,) = exchange(
         net,
         "head_exchange",
@@ -1533,7 +1539,7 @@
     grad_packed, head_low, head_whole = lax.optimization_barrier((grad_packed, head_low, head_whole))
     guests = [p for p in range(planes) if p >= 4 or p == SPARE]
     slots = 1 + len(guests)
-    head_rows = jnp.pad(head_low.T.reshape(count, rows, 3 * HEAD_DIM), ((0, 0), (0, 0), (0, 64)))
+    head_rows = head_rows.reshape(count, rows, 4 * HEAD_DIM)
 
     def group_of(device):
         return device // GROUP - (device // GROUP) // 3

time: 318 us -> 317 us (level)
  transfers between devices with their start and end apart: 9 -> 9, of which waited for: 1 -> 1; matrix products, arithmetic and copies ran while one was open for 2% -> 2% of each run, Pallas kernels for 40% -> 41%
where the time goes in v5:
time: 317 us; the launch traced here: 314 us
  Pallas kernels  275 us (87%)
  starting transfers between devices  16.7 us (5%)
  other arithmetic  12.6 us (4%)
  local copies, waits for them, and re-layouts  4.5 us (1%)
  waiting for transfers between devices  4.5 us (1%)
    pallas_call x7, Pallas kernels, exchange(): pl.pallas_call(functools.partial(exchange_kernel, net, meet or (lambda me...  170 us
    pallas_call x1, Pallas kernels, gather_tokens(): pl.pallas_call(functools.partial(gather_kernel, net, flows, len(extras)),...  38.8 us
    pallas_call x1, Pallas kernels, newton(): pl.pallas_call(functools.partial(newton_kernel, net), out_shape=[SQUARE,...  37.5 us
    ppermute x9, starting transfers between devices, permute(): lax.ppermute(values, ('head', 'blk'), [(place(i), place(j)) for i, j in p...  16.7 us
    pallas_call x1, Pallas kernels, feed_forward(): pl.pallas_call(functools.partial(feed_forward_kernel, net), out_shape=[ja...  9.09 us
  transfers between devices with their start and end apart: 9, of which 1 were waited for; matrix products, arithmetic and copies ran while one was open for 2% of the time, Pallas kernels for 41%

profile of v5, /device:TPU:18, one launch (start us, length us, event | category | flops | bytes accessed | tf_op | source)
XLA Modules:
  0.0 314.2 jit_solution(2201783126856959414)
XLA Ops:
  0.7 2.8 prepare.1
  3.4 38.8 %gather_tokens.1 = (bf16[4,2,4,64,768]{4,3,2,1,0:T(8,128)(2,1)}, bf16[32,24,256]{2,1,0:T(8,128)(2,1)}, bf16[8,24,768]{2,1,0:T(8,128)(2,1)}, bf16[4,24,768]{2,1,0...) custom-call(bf16[2,64,768]{2,1,0:T(8,128)(2,1)} %bitcast.81, ...), custom_call_target="tpu_custom_call" | custom-call | bytes 104857600 | tf_op jit(solution)/shard_map/gather_tokens/pallas_call | solution.py:723
  42.3 6.6 %collective-permute-start = (bf16[192,768]{1,0:T(8,128)(2,1)}, bf16[192,768]{1,0:T(8,128)(2,1)S(1)}, u32[]{:S(2)}, u32[]{:S(2)}) collective-permute-start(bf16[192,768]{1,0:T(8,128)(2,1)} %bitcast.91), channel_id=1, source_target_pairs={{0,4},{16,20},{1,5},{17,21},{2,6},{18,22},{3,7},{19,23},{4,8},{20,... | collective-permute-start | bytes 884744 | tf_op jit(solution)/shard_map/ppermute | solution.py:75
  48.9 1.9 collective-permute-start.1
  50.8 2.2 collective-permute-start.2
  55.4 1.8 multiply_sine_fusion
  57.2 3.3 %attend.1 = (bf16[192,2048]{1,0:T(8,128)(2,1)}, f32[64,2048]{1,0:T(8,128)}, f32[1,2048]{1,0:T(1,128)}, bf16[32,32,128]{2,1,0:T(8,128)(2,1)}) custom-call(s32[2,4]{1,0:T(2,128)} %pad_add_fusion.refs_0_, bf16[4,2,4,64,768]{4,3,2,1,0:T(8,128)(2,1)} %get-tuple-element.79.refs_1_, bf16[768,256]{1,0:T(8,128)(2,1)} %bitcast.86, ...), custom_call_target="tpu_custom_call" | custom-call | flops 2000000000 | bytes 8388608 | tf_op jit(solution)/shard_map/attend/pallas_call | solution.py:854
  60.4 42.0 %mixed_exchange.1 = (bf16[24,32,128]{2,1,0:T(8,128)(2,1)}, bf16[32,24,768]{2,1,0:T(8,128)(2,1)}, bf16[8,128,768]{2,1,0:T(8,128)(2,1)}, bf16[4,8,24,768]{3,2,1,0:T(8,128)(2,1)}) custom-call(bf16[32,32,128]{2,1,0:T(8,128)(2,1)} %get-tuple-element.80.refs_0_, bf16[4,24,768]{2,1,0:T(8,128)(2,1)} %get-tuple-element.81.refs_1_, bf16[128,768]{1,0:T(8,128)(2,1)} %bitcast.72, ...), custom_call_target="tpu_custom_call" | custom-call | bytes 33030144 | tf_op jit(solution)/shard_map/mixed_exchange/pallas_call | solution.py:563
  102.4 2.8 after_attention.1
  105.2 14.5 %second_exchange.1 = bf16[8,128,768]{2,1,0:T(8,128)(2,1)} custom-call(bf16[128,768]{1,0:T(8,128)(2,1)} %get-tuple-element.89.refs_0_), custom_call_target="tpu_custom_call" | custom-call | bytes 12582912 | tf_op jit(solution)/shard_map/second_exchange/pallas_call | solution.py:563
  120.9 9.1 %feed_forward.1 = (bf16[1024,768]{1,0:T(8,128)(2,1)}, bf16[1024,768]{1,0:T(8,128)(2,1)}, bf16[192,768]{1,0:T(8,128)(2,1)}, bf16[192,768]{1,0:T(8,128)(2,1)}, bf1...) custom-call(bf16[1024,768]{1,0:T(8,128)(2,1)} %bitcast.63, bf16[1024,768]{1,0:T(8,128)(2,1)} %bitcast.88, ...), custom_call_target="tpu_custom_call" | custom-call | flops 3500000000 | bytes 10485760 | tf_op jit(solution)/shard_map/feed_forward/pallas_call | solution.py:1171
  130.0 2.0 collective-permute-start.3
  132.3 15.8 %second_grad_exchange.1.second_grad_ref = f32[128,768]{1,0:T(8,128)} custom-call(bf16[2,2,2,128,768]{4,3,2,1,0:T(8,128)(2,1)} %bitcast.64), custom_call_target="tpu_custom_call" | custom-call | bytes 3145728 | tf_op jit(solution)/shard_map/second_grad_exchange/pallas_call | solution.py:563
  148.1 3.8 %before_attention.1 = (f32[128,768]{1,0:T(8,128)}, bf16[24,32,128]{2,1,0:T(8,128)(2,1)}, bf16[768,768]{1,0:T(8,128)(2,1)}) custom-call(f32[128,768]{1,0:T(8,128)} %second_grad_exchange.1.second_grad_ref, f32[128,768]{1,0:T(8,128)} %get-tuple-element.85.middle_ref, bf16[128,768]{1,0:T(8,128)(2,1)} %bitcast.73, bf16[128,768]{1,0:T(8,128)(2,1)} %get-tuple-element.93.mixed_ref, ...), custom_call_target="tpu_custom_call" | custom-call | flops 400000000 | bytes 5242880 | tf_op jit(solution)/shard_map/before_attention/pallas_call | solution.py:1203
  151.9 4.5 %collective-permute-done.4 = bf16[192,768]{1,0:T(8,128)(2,1)S(1)} collective-permute-done((bf16[192,768]{1,0:T(8,128)(2,1)}, bf16[192,768]{1,0:T(8,128)(2,1)S(1)}, u32[]{:S(2)}, u32[]{:S(2)}) %collective-permute-start.4) | collective-permute-done | bytes 294944 | tf_op jit(solution)/shard_map/ppermute | solution.py:75
  157.4 39.7 %mixed_grad_exchange.1 = (bf16[32,32,128]{2,1,0:T(8,128)(2,1)}, f32[4,24,768]{2,1,0:T(8,128)}, bf16[4,192,2048]{2,1,0:T(8,128)(2,1)}, bf16[4,8,24,768]{3,2,1,0:T(8,128)(2,1)}) custom-call(bf16[24,32,128]{2,1,0:T(8,128)(2,1)} %get-tuple-element.94.refs_0_, bf16[4,2,2,2,24,768]{5,4,3,2,1,0:T(8,128)(2,1)} %bitcast.69, ...), custom_call_target="tpu_custom_call" | custom-call | bytes 39059456 | tf_op jit(solution)/shard_map/mixed_grad_exchange/pallas_call | solution.py:563
  201.0 3.6 %attend_back.1 = (bf16[32,96,128]{2,1,0:T(8,128)(2,1)}, bf16[192,768]{1,0:T(8,128)(2,1)}, bf16[768,256]{1,0:T(8,128)(2,1)}) custom-call(s32[2,4]{1,0:T(2,128)} %pad_add_fusion.refs_0_, bf16[4,2,4,64,768]{4,3,2,1,0:T(8,128)(2,1)} %get-tuple-element.79.refs_1_, bf16[192,2048]{1,0:T(8,128)(2,1)} %get-tuple-element.86.refs_2_, ...), custom_call_target="tpu_custom_call" | custom-call | flops 4000000000 | bytes 12582912 | tf_op jit(solution)/shard_map/attend_back/pallas_call | solution.py:981
  204.6 1.7 head_exchange.1.head_ref
  206.4 37.5 %newton.1 = (bf16[768,768]{1,0:T(8,128)(2,1)}, bf16[768,2048]{1,0:T(8,128)(2,1)}) custom-call(bf16[24,64,768]{2,1,0:T(8,128)(2,1)} %head_exchange.1.head_ref, bf16[768,768]{1,0:T(8,128)(2,1)} %bitcast.89, bf16[768,768]{1,0:T(8,128)(2,1)} %bitcast.90, bf16[768,2048]{1,0:T(8,128)(2,1)} %bitcast.87), custom_call_target="tpu_custom_call" | custom-call | flops 24999999488 | bytes 8388608 | tf_op jit(solution)/shard_map/newton/pallas_call | solution.py:1375
  244.5 2.7 attending_exchange.1
  248.2 2.9 input_partial.1.refs_5_
  251.0 53.7 %step_exchange.1 = (bf16[24,24,256]{2,1,0:T(8,128)(2,1)}, bf16[8,24,768]{2,1,0:T(8,128)(2,1)}, bf16[4,24,768]{2,1,0:T(8,128)(2,1)}, bf16[3,24,2048]{2,1,0:T(8,12...) custom-call(bf16[32,24,256]{2,1,0:T(8,128)(2,1)} %bitcast.62, ...), custom_call_target="tpu_custom_call" | custom-call | bytes 17989632 | tf_op jit(solution)/shard_map/step_exchange/pallas_call | solution.py:563
  304.8 1.4 bitcast_reduce_fusion
  309.9 2.3 fusion.11
  (111 shorter events, 15.5 us)
Async XLA Ops:
  0.6 54.0 %copy-start = (bf16[2,64,768]{2,1,0:T(8,128)(2,1)S(1)}, bf16[2,64,768]{2,1,0:T(8,128)(2,1)}, u32[]{:S(2)}) copy-start(bf16[2,64,768]{2,1,0:T(8,128)(2,1)} %param.8) | copy-start | bytes 589828
  42.3 77.7 %collective-permute-start = (bf16[192,768]{1,0:T(8,128)(2,1)}, bf16[192,768]{1,0:T(8,128)(2,1)S(1)}, u32[]{:S(2)}, u32[]{:S(2)}) collective-permute-start(bf16[192,768]{1,0:T(8,128)(2,1)} %bitcast.91), channel_id=1, source_target_pairs={{0,4},{16,20},{1,5},{17,21},{2,6},{18,22},{3,7},{19,23},{4,8},{20,... | collective-permute-start | bytes 884744 | tf_op jit(solution)/shard_map/ppermute | solution.py:75
  48.9 71.1 %collective-permute-start.1 = (bf16[192,768]{1,0:T(8,128)(2,1)}, bf16[192,768]{1,0:T(8,128)(2,1)S(1)}, u32[]{:S(2)}, u32[]{:S(2)}) collective-permute-start(bf16[192,768]{1,0:T(8,128)(2,1)} %bitcast.92), channel_id=1, source_target_pairs={{0,8},{16,24},{1,9},{17,25},{2,10},{18,26},{3,11},{19,27},{4,12},{... | collective-permute-start | bytes 884744 | tf_op jit(solution)/shard_map/ppermute | solution.py:75
  50.8 69.2 %collective-permute-start.2 = (bf16[192,768]{1,0:T(8,128)(2,1)}, bf16[192,768]{1,0:T(8,128)(2,1)S(1)}, u32[]{:S(2)}, u32[]{:S(2)}) collective-permute-start(bf16[192,768]{1,0:T(8,128)(2,1)} %bitcast.93), channel_id=1, source_target_pairs={{0,12},{16,28},{1,13},{17,29},{2,14},{18,30},{3,15},{19,31},{4,0},... | collective-permute-start | bytes 884744 | tf_op jit(solution)/shard_map/ppermute | solution.py:75
  54.5 2.7 copy-start.23
  102.4 17.4 %copy-start.1 = (bf16[2,64,768]{2,1,0:T(8,128)(2,1)S(1)}, bf16[2,64,768]{2,1,0:T(8,128)(2,1)}, u32[]{:S(2)}) copy-start(bf16[2,64,768]{2,1,0:T(8,128)(2,1)} %param.8) | copy-start | bytes 589828
  120.9 11.3 %copy-start.12 = (bf16[8,24,768]{2,1,0:T(8,128)(2,1)S(1)}, bf16[8,24,768]{2,1,0:T(8,128)(2,1)}, u32[]{:S(2)}) copy-start(bf16[8,24,768]{2,1,0:T(8,128)(2,1)} %get-tuple-element.100) | copy-start | bytes 884740
  130.0 21.9 %collective-permute-start.5 = (bf16[192,768]{1,0:T(8,128)(2,1)}, bf16[192,768]{1,0:T(8,128)(2,1)S(1)}, u32[]{:S(2)}, u32[]{:S(2)}) collective-permute-start(bf16[192,768]{1,0:T(8,128)(2,1)} %get-tuple-element.99), channel_id=1, source_target_pairs={{0,12},{16,28},{1,13},{17,29},{2,14},{18,30},{3,15},{19,31},{4,0},... | collective-permute-start | bytes 884744 | tf_op jit(solution)/shard_map/ppermute | solution.py:75
  130.0 26.4 %collective-permute-start.4 = (bf16[192,768]{1,0:T(8,128)(2,1)}, bf16[192,768]{1,0:T(8,128)(2,1)S(1)}, u32[]{:S(2)}, u32[]{:S(2)}) collective-permute-start(bf16[192,768]{1,0:T(8,128)(2,1)} %get-tuple-element.98), channel_id=1, source_target_pairs={{0,8},{16,24},{1,9},{17,25},{2,10},{18,26},{3,11},{19,27},{4,12},{... | collective-permute-start | bytes 884744 | tf_op jit(solution)/shard_map/ppermute | solution.py:75
  130.0 26.3 %collective-permute-start.3 = (bf16[192,768]{1,0:T(8,128)(2,1)}, bf16[192,768]{1,0:T(8,128)(2,1)S(1)}, u32[]{:S(2)}, u32[]{:S(2)}) collective-permute-start(bf16[192,768]{1,0:T(8,128)(2,1)} %get-tuple-element.97), channel_id=1, source_target_pairs={{0,4},{16,20},{1,5},{17,21},{2,6},{18,22},{3,7},{19,23},{4,8},{20,... | collective-permute-start | bytes 884744 | tf_op jit(solution)/shard_map/ppermute | solution.py:75
  148.1 8.3 %copy-start.11 = (bf16[192,768]{1,0:T(8,128)(2,1)S(1)}, bf16[192,768]{1,0:T(8,128)(2,1)}, u32[]{:S(2)}) copy-start(bf16[192,768]{1,0:T(8,128)(2,1)} %get-tuple-element.96) | copy-start | bytes 884740
  156.4 40.7 %copy-start.17 = (bf16[8,24,640]{2,1,0:T(8,128)(2,1)S(1)}, bf16[8,24,640]{2,1,0:T(8,128)(2,1)}, u32[]{:S(2)}) copy-start(bf16[8,24,640]{2,1,0:T(8,128)(2,1)} %get-tuple-element.116) | copy-start | bytes 737284
  197.1 50.2 %collective-permute-start.6 = (bf16[192,640]{1,0:T(8,128)(2,1)S(1)}, bf16[192,640]{1,0:T(8,128)(2,1)S(1)}, u32[]{:S(2)}, u32[]{:S(2)}) collective-permute-start(bf16[192,640]{1,0:T(8,128)(2,1)S(1)} %bitcast.77), channel_id=1, source_target_pairs={{0,4},{16,20},{1,5},{17,21},{2,6},{18,22},{3,7},{19,23},{8,12},{24... | collective-permute-start | bytes 737288 | tf_op jit(solution)/shard_map/ppermute | solution.py:75
  198.4 48.9 %collective-permute-start.7 = (bf16[192,640]{1,0:T(8,128)(2,1)S(1)}, bf16[192,640]{1,0:T(8,128)(2,1)S(1)}, u32[]{:S(2)}, u32[]{:S(2)}) collective-permute-start(bf16[192,640]{1,0:T(8,128)(2,1)S(1)} %bitcast.78), channel_id=1, source_target_pairs={{4,12},{20,28},{5,13},{21,29},{6,14},{22,30},{7,15},{23,31},{8,0},... | collective-permute-start | bytes 737288 | tf_op jit(solution)/shard_map/ppermute | solution.py:75
  199.7 47.6 %collective-permute-start.8 = (bf16[192,640]{1,0:T(8,128)(2,1)S(1)}, bf16[192,640]{1,0:T(8,128)(2,1)S(1)}, u32[]{:S(2)}, u32[]{:S(2)}) collective-permute-start(bf16[192,640]{1,0:T(8,128)(2,1)S(1)} %bitcast.79), channel_id=1, source_target_pairs={{0,12},{16,28},{1,13},{17,29},{2,14},{18,30},{3,15},{19,31},{4,0},... | collective-permute-start | bytes 737288 | tf_op jit(solution)/shard_map/ppermute | solution.py:75
  206.4 37.5 %copy-start.15 = (f32[4,24,768]{2,1,0:T(8,128)S(1)}, f32[4,24,768]{2,1,0:T(8,128)}, u32[]{:S(2)}) copy-start(f32[4,24,768]{2,1,0:T(8,128)} %get-tuple-element.120) | copy-start | bytes 884740
  304.8 2.8 copy-start.22
  304.8 2.8 copy-start.13
  304.8 2.8 copy-start.14
  309.4 2.8 copy-start.5
  309.9 2.3 copy-start.7
  309.9 2.3 copy-start.8
  309.9 2.3 copy-start.21
  309.9 2.3 copy-start.24
  (14 other events, 15.0 us)
